TPU v7x, 32 devices: a whole 2x2x4 slice. The times are simulated.
32 devices in a mesh: groups: 2 (over y), chan: 4 (over z), tm: 2 (over x), beam: 2 (over core).
Axes of the slice: x: 2, y: 2, z: 4, core: 2. Of those that a mesh axis runs over, the one named last changes fastest.
Arguments:
- voltages: bfloat16 [1024, 32768], P(('groups', 'chan', 'beam'), 'tm'), parts along dimension 0, may hold values from -6 to 6
- filter_taps: float32 [8, 1024], replicated, may hold values from -0.09375 to 0.09375
- beam_weights: bfloat16 [256, 2, 1024], replicated, may hold values from -0.25 to 0.25
- station_index: int32 [512], replicated, may hold values from 0 to 255, as said below
- delay_table: int32 [512, 8], P('chan'), may hold values from 0 to 32, as said below
Outputs:
- dedispersed: float32 [2048, 8, 32], P(('groups', 'chan', 'beam'), None, 'tm'), parts along dimension 0
There are 2 independent parts, one for each index of `groups`. A program takes and returns all parts, laid end to end along the dimension named above; an argument that names none is the same for every part. Nothing has to cross between parts.
Inputs may be any that keep to these rules, and one draw needn't show every extreme that they name: `station_index`: the even inputs name each of the 256 weight rows once, and so do the odd inputs. `delay_table`: some entry equals 32.
All inputs are finite; a program needn't handle non-finite values.
Results may differ from a plain program's by a relative error of at most 0.0029.
Values may be sent and summed in bfloat16 or wider, within the bound.
No kernel may reach another device: no remote copies, remote signals or barrier semaphores. Data moves between devices by JAX's collectives and lax.ppermute only.
A program may use at most 64 MiB of HBM per device.

v0:
```python
import functools
import math

import jax
import jax.numpy as jnp
import numpy as np
from jax import lax
from jax.experimental import pallas as pl
from jax.experimental.pallas import tpu as pltpu
from jax.sharding import PartitionSpec as P

VMEM_BYTES = 48 << 20
LANES = 128
WIDE = 256
ROW_BLOCK = 32


def rotated(value, axis, steps):
    count = lax.axis_size(axis)
    return lax.ppermute(value, axis, [(source, (source + steps) % count) for source in range(count)])


def from_previous(value, axis):
    count = lax.axis_size(axis)
    return lax.ppermute(value, axis, [(source, source + 1) for source in range(count - 1)])


def dft_blocks(length, blocks):
    channels = length // 2
    phase = (np.arange(length)[:, None] * np.arange(channels)[None, :] % length) * (2.0 * math.pi / length)
    table = np.stack([np.cos(phase), -np.sin(phase)], axis=1).reshape(length, 2, blocks, channels // blocks)
    return jnp.asarray(np.transpose(table, (2, 0, 1, 3)).reshape(blocks, length, -1), jnp.bfloat16)


def rolled(value, start, axis):
    count = value.shape[axis]
    return lax.dynamic_slice_in_dim(jnp.concatenate([value, value], axis=axis), start, count, axis)


def vmem_spec():
    return pl.BlockSpec(memory_space=pltpu.VMEM)


def spectra_kernel(first, frames, length, has_rim, *refs):
    me_ref, refs = refs[0], refs[1:]
    rim_ref, refs = (refs[0], refs[1:]) if has_rim else (None, refs)
    volt_ref, taps_ref, dft_ref = refs[:3]
    outs, (filt, spread) = refs[3:-2], refs[-2:]
    taps = taps_ref.shape[0]
    rows = volt_ref.shape[0]
    row_block = spread.shape[1]
    half = row_block // 2

    def columns(n, _):
        lane = pl.multiple_of(n * LANES, LANES)
        weights = [taps_ref[t : t + 1, pl.ds(lane, LANES)] for t in range(taps)]

        def load(row, frame):
            if frame < 0:
                ref, frame = rim_ref, frame + taps - 1
            else:
                ref = volt_ref
            at = pl.multiple_of(frame * length + lane, LANES)
            return ref[pl.ds(row, row_block), pl.ds(at, LANES)].astype(jnp.float32)

        for block in range(rows // row_block):
            row = block * row_block
            window = [load(row, first + t - (taps - 1)) for t in range(taps - 1)]
            for f in range(frames):
                window.append(load(row, first + f))
                total = weights[0] * window[0]
                for t in range(1, taps):
                    total = total + weights[t] * window[t]
                window.pop(0)
                slot = (block * frames + f) % spread.shape[0]
                spread[slot] = total
                for p in range(2):
                    picked = spread[slot, pl.ds(p, half, stride=2), :]
                    filt[pl.ds((f * 2 + p) * (rows // 2) + block * half, half), pl.ds(lane, LANES)] = picked.astype(
                        jnp.bfloat16
                    )
        return 0

    lax.fori_loop(0, length // LANES, columns, 0)
    count = dft_ref.shape[0]
    stations = rows // 2
    channels = outs[0].shape[-1]
    for d, out in enumerate(outs):
        block = lax.rem(me_ref[0] + d, count)
        result = jnp.dot(filt[...], dft_ref[block], preferred_element_type=jnp.float32).astype(jnp.bfloat16)
        for f in range(frames):
            for p in range(2):
                at = (f * 2 + p) * stations
                for r in range(2):
                    out[f, p, r] = result[at : at + stations, r * channels : (r + 1) * channels]


def make_spectra(me, rim, voltages, filter_taps, dft, first, frames):
    rows = voltages.shape[0]
    length = filter_taps.shape[1]
    count = dft.shape[0]
    channels = dft.shape[2] // 2
    has_rim = rim is not None
    operands = ([rim] if has_rim else []) + [voltages, filter_taps, dft]
    shape = (frames, 2, 2, rows // 2, channels)
    return pl.pallas_call(
        functools.partial(spectra_kernel, first, frames, length, has_rim),
        out_shape=[jax.ShapeDtypeStruct(shape, jnp.bfloat16)] * count,
        in_specs=[pl.BlockSpec(memory_space=pltpu.SMEM)] + [vmem_spec()] * len(operands),
        out_specs=[vmem_spec()] * count,
        scratch_shapes=[
            pltpu.VMEM((frames * rows, length), jnp.bfloat16),
            pltpu.VMEM((8, min(rows, ROW_BLOCK), LANES), jnp.float32),
        ],
        compiler_params=pltpu.CompilerParams(vmem_limit_bytes=VMEM_BYTES),
        cost_estimate=pl.CostEstimate(
            flops=2 * frames * rows * length * length, bytes_accessed=8 << 20, transcendentals=0
        ),
        name=f"spectra_{first}",
    )(me, *operands)


def beam_kernel(pieces, has_sum, *refs):
    spectra, refs = refs[:pieces], refs[pieces:]
    mixers_ref, place_ref, refs = refs[0], refs[1], refs[2:]
    sums, refs = (refs[0], refs[1:]) if has_sum else (None, refs)
    out, high, low = refs
    frames, _, _, stations, channels = spectra[0].shape
    beams = mixers_ref.shape[1] // 2
    step = min(frames, max(1, WIDE // channels))

    def group(i, _):
        power = None
        for p in range(2):
            sides = []
            for side in range(step):
                parts = []
                for piece in spectra:
                    for r in range(2):
                        parts.append(piece[i * step + side, p, r])
                sides.append(jnp.concatenate(parts, axis=0))
            stacked = jnp.concatenate(sides, axis=1)
            voltage = jnp.dot(mixers_ref[p], stacked, preferred_element_type=jnp.float32)
            real_part, imag_part = voltage[:beams], voltage[beams:]
            term = real_part * real_part + imag_part * imag_part
            power = term if power is None else power + term
        upper = power.astype(jnp.bfloat16)
        at = pl.multiple_of(i * step * channels, step * channels)
        high[:, pl.ds(at, step * channels)] = upper
        low[:, pl.ds(at, step * channels)] = (power - upper.astype(jnp.float32)).astype(jnp.bfloat16)
        return 0

    lax.fori_loop(0, frames // step, group, 0)
    total = jnp.dot(high[...], place_ref[...], preferred_element_type=jnp.float32)
    total = total + jnp.dot(low[...], place_ref[...], preferred_element_type=jnp.float32)
    if has_sum:
        total = total + sums[...]
    out[...] = total


def beam_sums(spectra, mixers, place, sums):
    frames, _, _, stations, channels = spectra[0].shape
    beams = mixers.shape[1] // 2
    operands = [*spectra, mixers, place] + ([] if sums is None else [sums])
    return pl.pallas_call(
        functools.partial(beam_kernel, len(spectra), sums is not None),
        out_shape=jax.ShapeDtypeStruct((beams, place.shape[1]), jnp.float32),
        in_specs=[vmem_spec()] * len(operands),
        out_specs=vmem_spec(),
        scratch_shapes=[pltpu.VMEM((beams, frames * channels), jnp.bfloat16)] * 2,
        compiler_params=pltpu.CompilerParams(vmem_limit_bytes=VMEM_BYTES),
        cost_estimate=pl.CostEstimate(
            flops=2 * 2 * frames * channels * mixers.shape[1] * mixers.shape[2],
            bytes_accessed=8 << 20,
            transcendentals=0,
        ),
        name="beam_sums_first" if sums is None else "beam_sums_rest",
    )(*operands)


def make_mixers(beam_weights, station_index, in_dev):
    chan_devices = lax.axis_size("chan")
    beam_devices = lax.axis_size("beam")
    here, core = lax.axis_index("chan"), lax.axis_index("beam")
    stations = beam_weights.shape[0]
    arranged = beam_weights.reshape(stations, 2, chan_devices, beam_devices, -1)
    chosen = lax.dynamic_index_in_dim(arranged, core, 3, keepdims=False)
    chosen = rolled(chosen, here, 2).reshape(stations, 2, -1)
    order = station_index.reshape(chan_devices, beam_devices, in_dev // 2, 2)
    order = rolled(order[::-1], chan_devices - 1 - here, 0)
    order = rolled(order, core, 1)
    order = jnp.transpose(order, (3, 0, 1, 2))
    order = jnp.broadcast_to(order[:, :, :, None, :], (*order.shape[:3], 2, in_dev // 2)).reshape(2, -1)
    imag_column = (jnp.arange(order.shape[1], dtype=jnp.int32) // (in_dev // 2) % 2 == 1)[None, None, :]
    select = (order[:, None, :] == jnp.arange(stations, dtype=jnp.int32)[None, :, None]).astype(jnp.bfloat16)
    picked = jnp.einsum("trb,ptj->prbj", chosen, select, preferred_element_type=jnp.float32)
    real_part, imag_part = picked[:, 0], picked[:, 1]
    upper = jnp.where(imag_column, -imag_part, real_part)
    lower = jnp.where(imag_column, real_part, imag_part)
    return jnp.concatenate([upper, lower], axis=1).astype(jnp.bfloat16)


def make_place(delay_table, frames_dev):
    channels, curves = delay_table.shape
    groups = lax.axis_size("tm")
    here = lax.axis_index("tm")
    total = groups * frames_dev
    target = lax.rem(here + jnp.arange(groups, dtype=jnp.int32), groups)
    wanted = target[:, None] * frames_dev + jnp.arange(frames_dev, dtype=jnp.int32)[None, :]
    source = wanted[None, :, None, :] + delay_table[:, None, :, None]
    source = source.reshape(channels, -1)
    own = here * frames_dev + jnp.arange(frames_dev, dtype=jnp.int32)
    hit = (source[None] == own[:, None, None]).astype(jnp.float32)
    base = jnp.where(source < total, 1.0 / total, 0.0)[None]
    return (hit - base).astype(jnp.bfloat16).reshape(frames_dev * channels, -1)


def shards(voltages, filter_taps, beam_weights, station_index, delay_table):
    taps, length = filter_taps.shape
    in_dev = voltages.shape[0]
    frames_dev = voltages.shape[1] // length
    chan_devices = lax.axis_size("chan")
    beam_devices = lax.axis_size("beam")
    time_devices = lax.axis_size("tm")
    channels = delay_table.shape[0]
    curves = delay_table.shape[1]
    me = lax.axis_index("chan").astype(jnp.int32).reshape(1)
    dft = dft_blocks(length, chan_devices)
    rim = from_previous(voltages[:, (frames_dev - taps + 1) * length :], "tm")
    split = frames_dev // 2
    mixers = make_mixers(beam_weights, station_index, in_dev)
    place = make_place(delay_table, frames_dev)
    sums = None
    for first in (split, 0):
        own = make_spectra(me, rim if first < taps - 1 else None, voltages, filter_taps, dft, first, split)
        pieces = []
        for d in range(chan_devices):
            here = own[d] if d == 0 else rotated(own[d], "chan", d)
            pieces.append(here)
            for e in range(1, beam_devices):
                pieces.append(rotated(here, "beam", beam_devices - e))
        sums = beam_sums(pieces, mixers, place[first * channels : (first + split) * channels], sums)
    width = curves * frames_dev
    here = sums[:, :width]
    for e in range(1, time_devices):
        here = here + rotated(sums[:, e * width : (e + 1) * width], "tm", e)
    share = here.shape[0] // chan_devices
    final = here[:share]
    for d in range(1, chan_devices):
        final = final + rotated(here[d * share : (d + 1) * share], "chan", d)
    return (final * (1.0 / math.sqrt(length // 2))).reshape(share, curves, frames_dev)


def solution(mesh):
    in_specs = (P(("groups", "chan", "beam"), "tm"), P(), P(), P(), P("chan", None))
    out_specs = P(("groups", "chan", "beam"), None, "tm")
    return jax.shard_map(shards, mesh=mesh, in_specs=in_specs, out_specs=out_specs, check_vma=False)
```

profile of v0, /device:TPU:0, one launch (start us, length us, event | category | flops | bytes accessed | tf_op | source)
XLA Modules:
  0.0 96.2 jit_solution(12094689790372548712)
XLA Ops:
  0.0 1.6 %copy-done = bf16[64,16384]{1,0:T(8,128)(2,1)S(1)} copy-done((bf16[64,16384]{1,0:T(8,128)(2,1)S(1)}, bf16[64,16384]{1,0:T(8,128)(2,1)}, u32[]{:S(2)}) %copy-start) | copy-done | bytes 2097176
  1.6 1.6 %copy-done.2 = bf16[4,1024,256]{2,1,0:T(8,128)(2,1)S(1)} copy-done((bf16[4,1024,256]{2,1,0:T(8,128)(2,1)S(1)}, bf16[4,1024,256]{2,1,0:T(8,128)(2,1)}, u32[]{:S(2)}) %copy-start.2) | copy-done | bytes 2097176
  3.2 0.8 copy-done.4
  3.9 3.7 %spectra_8.1 = (bf16[8,2,2,32,128]{4,3,2,1,0:T(8,128)(2,1)S(1)}, bf16[8,2,2,32,128]{4,3,2,1,0:T(8,128)(2,1)}, bf16[8,2,2,32,128]{4,3,2,1,0:T(8,128)(2,1)}, bf16[8,2,2,32,128]{4,3,2,1,0:T(8,128)(2,1)}) custom-call(s32[1]{0:T(128)} %bitcast.refs_0_, bf16[64,16384]{1,0:T(8,128)(2,1)S(1)} %copy-done, f32[8,1024]{1,0:T(8,128)S(1)} %copy-done.4, ...), custom_call_target="tpu_custom_call" | custom-call | flops 1073741824 | bytes 8388608 | tf_op jit(solution)/shard_map/spectra_8/pallas_call | solution.py:106
  7.7 3.0 %collective-permute-start.9 = (bf16[8,2,2,32,128]{4,3,2,1,0:T(8,128)(2,1)}, bf16[8,2,2,32,128]{4,3,2,1,0:T(8,128)(2,1)}, u32[]{:S(2)}, u32[]{:S(2)}) collective-permute-start(bf16[8,2,2,32,128]{4,3,2,1,0:T(8,128)(2,1)} %get-tuple-element.18), channel_id=1, source_target_pairs={{0,4},{4,8},{8,12},{12,0},{1,5},{5,9},{9,13},{13,1},{2,6},{6,10},{... | collective-permute-start | bytes 786440 | tf_op jit(solution)/shard_map/ppermute | solution.py:20
  10.7 2.6 %collective-permute-start.11 = (bf16[8,2,2,32,128]{4,3,2,1,0:T(8,128)(2,1)}, bf16[8,2,2,32,128]{4,3,2,1,0:T(8,128)(2,1)}, u32[]{:S(2)}, u32[]{:S(2)}) collective-permute-start(bf16[8,2,2,32,128]{4,3,2,1,0:T(8,128)(2,1)} %get-tuple-element.19), channel_id=1, source_target_pairs={{0,8},{4,12},{8,0},{12,4},{1,9},{5,13},{9,1},{13,5},{2,10},{6,14},... | collective-permute-start | bytes 786440 | tf_op jit(solution)/shard_map/ppermute | solution.py:20
  13.3 1.4 %collective-permute-start.13 = (bf16[8,2,2,32,128]{4,3,2,1,0:T(8,128)(2,1)}, bf16[8,2,2,32,128]{4,3,2,1,0:T(8,128)(2,1)}, u32[]{:S(2)}, u32[]{:S(2)}) collective-permute-start(bf16[8,2,2,32,128]{4,3,2,1,0:T(8,128)(2,1)} %get-tuple-element.20), channel_id=1, source_target_pairs={{0,12},{4,0},{8,4},{12,8},{1,13},{5,1},{9,5},{13,9},{2,14},{6,2},{... | collective-permute-start | bytes 786440 | tf_op jit(solution)/shard_map/ppermute | solution.py:20
  14.6 0.0 collective-permute-start.8
  14.6 1.0 %slice.39 = bf16[64,7168]{1,0:T(8,128)(2,1)} slice(bf16[64,16384]{1,0:T(8,128)(2,1)S(1)} %copy-done), slice={[0:64], [9216:16384]} | slice | bytes 1835008 | tf_op jit(solution)/shard_map/slice | solution.py:229
  15.6 3.4 %collective-permute-start = (bf16[64,7168]{1,0:T(8,128)(2,1)}, bf16[64,7168]{1,0:T(8,128)(2,1)S(1)}, u32[]{:S(2)}, u32[]{:S(2)}) collective-permute-start(bf16[64,7168]{1,0:T(8,128)(2,1)} %slice.39), channel_id=1, source_target_pairs={{0,2},{1,3},{4,6},{5,7},{8,10},{9,11},{12,14},{13,15},{16,18},{17,... | collective-permute-start | bytes 2752520 | tf_op jit(solution)/shard_map/ppermute | solution.py:25
  19.1 0.1 reshape.125
  19.2 0.1 copy.17
  19.5 0.1 eq.41
  19.5 0.7 reshape.126
  20.2 1.1 %constant_dynamic-slice_fusion = bf16[256,2,4,1,128]{4,3,2,1,0:T(2,128)(2,1)S(1)} fusion(bf16[256,2,4,2,128]{4,3,2,1,0:T(2,128)(2,1)S(1)} %reshape.126, s32[]{:T(128)S(6)} %select_n.56), kind=kLoop, calls=%fused_computation.41 | loop fusion | bytes 1048580 | tf_op jit(solution)/shard_map/jit(dynamic_index_in_dim)/dynamic_slice | solution.py:187
  21.3 0.9 copy.22
  22.3 0.2 fusion.2
  22.5 0.8 convolution_bitcast_fusion
  23.3 1.9 %copy-done.6 = f32[2,2,512,512]{3,2,0,1:T(8,128)} copy-done((f32[2,2,512,512]{3,2,0,1:T(8,128)}, f32[2,2,512,512]{3,2,0,1:T(8,128)S(1)}, u32[]{:S(2)}) %copy-start.6) | copy-done | bytes 4194328
  25.2 1.2 %select_convert_fusion = bf16[2,512,512]{2,1,0:T(8,128)(2,1)} fusion(f32[2,2,512,512]{3,2,0,1:T(8,128)S(1)} %convolution_bitcast_fusion, pred[512]{0:T(512)(128)(4,1)S(1)} %fusion.11), kind=kLoop, calls=%fused_computation.5 | loop fusion | flops 524288 | bytes 3146240 | tf_op jit(solution)/shard_map/convert.1
  26.5 3.8 %select_convert_fusion.1 = bf16[2,512,512]{2,1,0:T(8,128)(2,1)} fusion(f32[2,2,512,512]{3,2,0,1:T(8,128)} %copy-done.6, pred[512]{0:T(512)(128)(4,1)S(1)} %fusion.11), kind=kLoop, calls=%fused_computation.6 | loop fusion | flops 1572864 | bytes 5243392 | tf_op jit(solution)/shard_map/convert
  30.2 0.1 iota_add_fusion
  30.3 0.1 add.118
  30.4 0.7 bitcast_add_fusion
  31.1 0.7 compare_select_fusion
  31.9 1.0 %copy.24 = s32[128,256]{1,0:T(8,128)S(1)} copy(s32[128,256]{0,1:T(8,128)} %bitcast_add_fusion) | data formatting | bytes 262144 | tf_op jit(solution)/shard_map/add | solution.py:210
  32.9 1.6 %copy.25 = f32[128,256]{1,0:T(8,128)} copy(f32[128,256]{0,1:T(8,128)} %compare_select_fusion) | data formatting | bytes 262144 | tf_op jit(solution)/shard_map/jit(_where)/select_n | solution.py:214
  34.5 0.0 collective-permute-done.9.refs_2_
  34.5 0.2 collective-permute-start.10
  34.8 1.2 %subtract_convert_fusion = bf16[16,128,256]{2,1,0:T(8,128)(2,1)S(1)} fusion(f32[128,256]{1,0:T(8,128)} %copy.25, s32[128,256]{1,0:T(8,128)S(1)} %copy.24, s32[16]{0:T(128)S(1)} %iota_add_fusion.1), kind=kLoop, calls=%fused_computation.4 | loop fusion | flops 2097152 | bytes 1310784 | tf_op jit(solution)/shard_map/convert_element_type | solution.py:215
  36.0 0.0 collective-permute-done.11.refs_4_
  36.0 0.3 collective-permute-start.12
  36.4 0.0 collective-permute-done.13.refs_6_
  36.4 0.2 collective-permute-start.14
  36.6 3.0 %collective-permute-done.refs_1_ = bf16[64,7168]{1,0:T(8,128)(2,1)S(1)} collective-permute-done((bf16[64,7168]{1,0:T(8,128)(2,1)}, bf16[64,7168]{1,0:T(8,128)(2,1)S(1)}, u32[]{:S(2)}, u32[]{:S(2)}) %collective-permute-start) | collective-permute-done | bytes 917536 | tf_op jit(solution)/shard_map/ppermute | solution.py:25
  39.6 1.6 %copy-done.3 = bf16[4,1024,256]{2,1,0:T(8,128)(2,1)S(1)} copy-done((bf16[4,1024,256]{2,1,0:T(8,128)(2,1)S(1)}, bf16[4,1024,256]{2,1,0:T(8,128)(2,1)}, u32[]{:S(2)}) %copy-start.3) | copy-done | bytes 2097176
  41.2 2.9 %spectra_0.1 = (bf16[8,2,2,32,128]{4,3,2,1,0:T(8,128)(2,1)S(1)}, bf16[8,2,2,32,128]{4,3,2,1,0:T(8,128)(2,1)S(1)}, bf16[8,2,2,32,128]{4,3,2,1,0:T(8,128)(2,1)S(1)}, bf16[8,2,2,32,128]{4,3,2,1,0:T(8,128)(2,1)S(1)}) custom-call(s32[1]{0:T(128)} %bitcast.refs_0_, bf16[64,7168]{1,0:T(8,128)(2,1)S(1)} %collective-permute-done.refs_1_, ...), custom_call_target="tpu_custom_call" | custom-call | flops 1073741824 | bytes 8388608 | tf_op jit(solution)/shard_map/spectra_0/pallas_call | solution.py:106
  44.0 0.7 collective-permute-start.2
  44.8 0.0 collective-permute-done.8.refs_1_
  44.8 0.3 collective-permute-start.4
  45.1 0.0 collective-permute-done.10.refs_3_
  45.1 2.9 %collective-permute-start.6 = (bf16[8,2,2,32,128]{4,3,2,1,0:T(8,128)(2,1)S(1)}, bf16[8,2,2,32,128]{4,3,2,1,0:T(8,128)(2,1)S(1)}, u32[]{:S(2)}, u32[]{:S(2)}) collective-permute-start(bf16[8,2,2,32,128]{4,3,2,1,0:T(8,128)(2,1)S(1)} %get-tuple-element.16), channel_id=1, source_target_pairs={{0,12},{4,0},{8,4},{12,8},{1,13},{5,1},{9,5},{13,9},{2,14},{6,2},{... | collective-permute-start | bytes 786440 | tf_op jit(solution)/shard_map/ppermute | solution.py:20
  48.0 0.1 fusion.17
  48.1 0.0 collective-permute-done.12.refs_5_
  48.1 0.1 collective-permute-start.1
  48.2 7.0 %collective-permute-done.2.refs_2_ = bf16[8,2,2,32,128]{4,3,2,1,0:T(8,128)(2,1)S(1)} collective-permute-done((bf16[8,2,2,32,128]{4,3,2,1,0:T(8,128)(2,1)S(1)}, bf16[8,2,2,32,128]{4,3,2,1,0:T(8,128)(2,1)S(1)}, u32[]{:S(2)}, u32[]{:S(2)}) %collective-permute-start.2) | collective-permute-done | bytes 262176 | tf_op jit(solution)/shard_map/ppermute | solution.py:20
  55.2 0.0 collective-permute-start.3
  55.2 10.1 %collective-permute-done.4.refs_4_ = bf16[8,2,2,32,128]{4,3,2,1,0:T(8,128)(2,1)S(1)} collective-permute-done((bf16[8,2,2,32,128]{4,3,2,1,0:T(8,128)(2,1)S(1)}, bf16[8,2,2,32,128]{4,3,2,1,0:T(8,128)(2,1)S(1)}, u32[]{:S(2)}, u32[]{:S(2)}) %collective-permute-start.4) | collective-permute-done | bytes 262176 | tf_op jit(solution)/shard_map/ppermute | solution.py:20
  65.3 0.0 collective-permute-start.5
  65.3 0.0 collective-permute-done.6.refs_6_
  65.3 0.5 collective-permute-start.7
  65.8 0.1 pad_maximum_fusion.refs_8_
  65.9 4.9 %beam_sums_first.1.refs_10_ = f32[512,256]{1,0:T(8,128)S(1)} custom-call(bf16[8,2,2,32,128]{4,3,2,1,0:T(8,128)(2,1)S(1)} %get-tuple-element.17.refs_0_, bf16[8,2,2,32,128]{4,3,2,1,0:T(8,128)(2,1)} %collective-permute-done.8.refs_1_, bf16[8,2,2,32,128]{4,3,2,1,0:T(8,128)(2,1)} %collective-permute-done.9.refs_2_, ...), custom_call_target="tpu_custom_call" | custom-call | flops 2147483648 | bytes 8388608 | tf_op jit(solution)/shard_map/beam_sums_first/pallas_call | solution.py:165
  70.9 0.0 collective-permute-done.5.refs_5_
  70.9 3.7 %beam_sums_rest.1 = f32[512,256]{1,0:T(8,128)S(1)} custom-call(bf16[8,2,2,32,128]{4,3,2,1,0:T(8,128)(2,1)S(1)} %get-tuple-element.13.refs_0_, bf16[8,2,2,32,128]{4,3,2,1,0:T(8,128)(2,1)S(1)} %collective-permute-done.1.refs_1_, bf16[8,2,2,32,128]{4,3,2,1,0:T(8,128)(2,1)S(1)} %collective-permute-done.2.refs_2_, ...), custom_call_target="tpu_custom_call" | custom-call | flops 2147483648 | bytes 8388608 | tf_op jit(solution)/shard_map/beam_sums_rest/pallas_call | solution.py:165
  74.7 2.4 %collective-permute-start.15 = (f32[512,128]{1,0:T(8,128)S(1)}, f32[512,128]{1,0:T(8,128)S(1)}, u32[]{:S(2)}, u32[]{:S(2)}) collective-permute-start(f32[512,128]{1,0:T(8,128)S(1)} %slice.57), channel_id=1, source_target_pairs={{0,2},{2,0},{1,3},{3,1},{4,6},{6,4},{5,7},{7,5},{8,10},{10,8},{9,1... | collective-permute-start | bytes 786440 | tf_op jit(solution)/shard_map/ppermute | solution.py:20
  77.1 6.5 %collective-permute-done.15 = f32[512,128]{1,0:T(8,128)S(1)} collective-permute-done((f32[512,128]{1,0:T(8,128)S(1)}, f32[512,128]{1,0:T(8,128)S(1)}, u32[]{:S(2)}, u32[]{:S(2)}) %collective-permute-start.15) | collective-permute-done | bytes 262176 | tf_op jit(solution)/shard_map/ppermute | solution.py:20
  83.7 5.6 %collective-permute-start.16 = (f32[128,128]{1,0:T(8,128)S(1)}, f32[128,128]{1,0:T(8,128)S(1)}, u32[]{:S(2)}, u32[]{:S(2)}) collective-permute-start(f32[128,128]{1,0:T(8,128)S(1)} %get-tuple-element.23), channel_id=1, source_target_pairs={{0,4},{4,8},{8,12},{12,0},{1,5},{5,9},{9,13},{13,1},{2,6},{6,10},{... | collective-permute-start | bytes 196616 | tf_op jit(solution)/shard_map/ppermute | solution.py:20
  89.2 0.0 collective-permute-start.17
  89.2 2.4 %collective-permute-start.18 = (f32[128,128]{1,0:T(8,128)S(1)}, f32[128,128]{1,0:T(8,128)S(1)}, u32[]{:S(2)}, u32[]{:S(2)}) collective-permute-start(f32[128,128]{1,0:T(8,128)S(1)} %get-tuple-element.24), channel_id=1, source_target_pairs={{0,12},{4,0},{8,4},{12,8},{1,13},{5,1},{9,5},{13,9},{2,14},{6,2},{... | collective-permute-start | bytes 196616 | tf_op jit(solution)/shard_map/ppermute | solution.py:20
  91.7 0.0 collective-permute-done.16
  91.7 3.8 %collective-permute-done.17 = f32[128,128]{1,0:T(8,128)S(1)} collective-permute-done((f32[128,128]{1,0:T(8,128)S(1)}, f32[128,128]{1,0:T(8,128)S(1)}, u32[]{:S(2)}, u32[]{:S(2)}) %collective-permute-start.17) | collective-permute-done | bytes 65568 | tf_op jit(solution)/shard_map/ppermute | solution.py:20
  95.4 0.0 collective-permute-done.18
  95.5 0.7 copy.26
  (37 shorter events, 0.2 us)
Async XLA Ops:
  0.0 1.6 %copy-start = (bf16[64,16384]{1,0:T(8,128)(2,1)S(1)}, bf16[64,16384]{1,0:T(8,128)(2,1)}, u32[]{:S(2)}) copy-start(bf16[64,16384]{1,0:T(8,128)(2,1)} %refs_1_.1) | copy-start | bytes 6291460
  1.6 1.6 %copy-start.2 = (bf16[4,1024,256]{2,1,0:T(8,128)(2,1)S(1)}, bf16[4,1024,256]{2,1,0:T(8,128)(2,1)}, u32[]{:S(2)}) copy-start(bf16[4,1024,256]{2,1,0:T(8,128)(2,1)} %constant.72.clone.refs_4_.refs_3_) | copy-start | bytes 6291460
  3.2 0.8 copy-start.4
  3.9 15.1 %copy-start.11 = (s32[512]{0:T(512)S(1)}, s32[512]{0:T(512)}, u32[]{:S(2)}) copy-start(s32[512]{0:T(512)} %param.9) | copy-start | bytes 6148
  7.7 11.9 %copy-start.9 = (bf16[256,2,1024]{2,1,0:T(2,128)(2,1)S(1)}, bf16[256,2,1024]{2,1,0:T(2,128)(2,1)}, u32[]{:S(2)}) copy-start(bf16[256,2,1024]{2,1,0:T(2,128)(2,1)} %param.8) | copy-start | bytes 3145732
  7.7 26.9 %collective-permute-start.9 = (bf16[8,2,2,32,128]{4,3,2,1,0:T(8,128)(2,1)}, bf16[8,2,2,32,128]{4,3,2,1,0:T(8,128)(2,1)}, u32[]{:S(2)}, u32[]{:S(2)}) collective-permute-start(bf16[8,2,2,32,128]{4,3,2,1,0:T(8,128)(2,1)} %get-tuple-element.18), channel_id=1, source_target_pairs={{0,4},{4,8},{8,12},{12,0},{1,5},{5,9},{9,13},{13,1},{2,6},{6,10},{... | collective-permute-start | bytes 786440 | tf_op jit(solution)/shard_map/ppermute | solution.py:20
  10.7 25.3 %collective-permute-start.11 = (bf16[8,2,2,32,128]{4,3,2,1,0:T(8,128)(2,1)}, bf16[8,2,2,32,128]{4,3,2,1,0:T(8,128)(2,1)}, u32[]{:S(2)}, u32[]{:S(2)}) collective-permute-start(bf16[8,2,2,32,128]{4,3,2,1,0:T(8,128)(2,1)} %get-tuple-element.19), channel_id=1, source_target_pairs={{0,8},{4,12},{8,0},{12,4},{1,9},{5,13},{9,1},{13,5},{2,10},{6,14},... | collective-permute-start | bytes 786440 | tf_op jit(solution)/shard_map/ppermute | solution.py:20
  13.3 23.1 %collective-permute-start.13 = (bf16[8,2,2,32,128]{4,3,2,1,0:T(8,128)(2,1)}, bf16[8,2,2,32,128]{4,3,2,1,0:T(8,128)(2,1)}, u32[]{:S(2)}, u32[]{:S(2)}) collective-permute-start(bf16[8,2,2,32,128]{4,3,2,1,0:T(8,128)(2,1)} %get-tuple-element.20), channel_id=1, source_target_pairs={{0,12},{4,0},{8,4},{12,8},{1,13},{5,1},{9,5},{13,9},{2,14},{6,2},{... | collective-permute-start | bytes 786440 | tf_op jit(solution)/shard_map/ppermute | solution.py:20
  14.6 30.2 %collective-permute-start.8 = (bf16[8,2,2,32,128]{4,3,2,1,0:T(8,128)(2,1)S(1)}, bf16[8,2,2,32,128]{4,3,2,1,0:T(8,128)(2,1)}, u32[]{:S(2)}, u32[]{:S(2)}) collective-permute-start(bf16[8,2,2,32,128]{4,3,2,1,0:T(8,128)(2,1)S(1)} %get-tuple-element.17.refs_0_), channel_id=1, source_target_pairs={{0,1},{1,0},{2,3},{3,2},{4,5},{5,4},{6,7},{7,6},{8,9},{9,8},{10,11... | collective-permute-start | bytes 786440 | tf_op jit(solution)/shard_map/ppermute | solution.py:20
  15.6 24.0 %collective-permute-start = (bf16[64,7168]{1,0:T(8,128)(2,1)}, bf16[64,7168]{1,0:T(8,128)(2,1)S(1)}, u32[]{:S(2)}, u32[]{:S(2)}) collective-permute-start(bf16[64,7168]{1,0:T(8,128)(2,1)} %slice.39), channel_id=1, source_target_pairs={{0,2},{1,3},{4,6},{5,7},{8,10},{9,11},{12,14},{13,15},{16,18},{17,... | collective-permute-start | bytes 2752520 | tf_op jit(solution)/shard_map/ppermute | solution.py:25
  23.3 2.0 %copy-start.6 = (f32[2,2,512,512]{3,2,0,1:T(8,128)}, f32[2,2,512,512]{3,2,0,1:T(8,128)S(1)}, u32[]{:S(2)}) copy-start(f32[2,2,512,512]{3,2,0,1:T(8,128)S(1)} %convolution_bitcast_fusion) | copy-start | bytes 12582916
  26.5 3.9 %copy-start.10 = (s32[128,8]{0,1:T(8,128)S(1)}, s32[128,8]{0,1:T(8,128)}, u32[]{:S(2)}) copy-start(s32[128,8]{0,1:T(8,128)} %param.10) | copy-start | bytes 12292
  30.2 9.3 %copy-start.1 = (bf16[64,16384]{1,0:T(8,128)(2,1)S(1)}, bf16[64,16384]{1,0:T(8,128)(2,1)}, u32[]{:S(2)}) copy-start(bf16[64,16384]{1,0:T(8,128)(2,1)} %refs_1_.1) | copy-start | bytes 6291460
  30.2 9.3 %copy-start.5 = (f32[8,1024]{1,0:T(8,128)S(1)}, f32[8,1024]{1,0:T(8,128)}, u32[]{:S(2)}) copy-start(f32[8,1024]{1,0:T(8,128)} %refs_2_.3) | copy-start | bytes 98308
  34.5 10.6 %collective-permute-start.10 = (bf16[8,2,2,32,128]{4,3,2,1,0:T(8,128)(2,1)}, bf16[8,2,2,32,128]{4,3,2,1,0:T(8,128)(2,1)S(1)}, u32[]{:S(2)}, u32[]{:S(2)}) collective-permute-start(bf16[8,2,2,32,128]{4,3,2,1,0:T(8,128)(2,1)} %collective-permute-done.9.refs_2_), channel_id=1, source_target_pairs={{0,1},{1,0},{2,3},{3,2},{4,5},{5,4},{6,7},{7,6},{8,9},{9,8},{10,11... | collective-permute-start | bytes 786440 | tf_op jit(solution)/shard_map/ppermute | solution.py:20
  36.0 12.1 %collective-permute-start.12 = (bf16[8,2,2,32,128]{4,3,2,1,0:T(8,128)(2,1)}, bf16[8,2,2,32,128]{4,3,2,1,0:T(8,128)(2,1)S(1)}, u32[]{:S(2)}, u32[]{:S(2)}) collective-permute-start(bf16[8,2,2,32,128]{4,3,2,1,0:T(8,128)(2,1)} %collective-permute-done.11.refs_4_), channel_id=1, source_target_pairs={{0,1},{1,0},{2,3},{3,2},{4,5},{5,4},{6,7},{7,6},{8,9},{9,8},{10,11... | collective-permute-start | bytes 786440 | tf_op jit(solution)/shard_map/ppermute | solution.py:20
  36.4 29.6 %collective-permute-start.14 = (bf16[8,2,2,32,128]{4,3,2,1,0:T(8,128)(2,1)}, bf16[8,2,2,32,128]{4,3,2,1,0:T(8,128)(2,1)S(1)}, u32[]{:S(2)}, u32[]{:S(2)}) collective-permute-start(bf16[8,2,2,32,128]{4,3,2,1,0:T(8,128)(2,1)} %collective-permute-done.13.refs_6_), channel_id=1, source_target_pairs={{0,1},{1,0},{2,3},{3,2},{4,5},{5,4},{6,7},{7,6},{8,9},{9,8},{10,11... | collective-permute-start | bytes 786440 | tf_op jit(solution)/shard_map/ppermute | solution.py:20
  39.6 1.6 %copy-start.3 = (bf16[4,1024,256]{2,1,0:T(8,128)(2,1)S(1)}, bf16[4,1024,256]{2,1,0:T(8,128)(2,1)}, u32[]{:S(2)}) copy-start(bf16[4,1024,256]{2,1,0:T(8,128)(2,1)} %constant.72.clone.refs_4_.refs_3_) | copy-start | bytes 6291460
  44.0 21.8 %copy-start.7 = (bf16[2,512,512]{2,1,0:T(8,128)(2,1)S(1)}, bf16[2,512,512]{2,1,0:T(8,128)(2,1)}, u32[]{:S(2)}) copy-start(bf16[2,512,512]{2,1,0:T(8,128)(2,1)} %select_convert_fusion) | copy-start | bytes 3145732
  44.0 21.8 %copy-start.8 = (bf16[2,512,512]{2,1,0:T(8,128)(2,1)S(1)}, bf16[2,512,512]{2,1,0:T(8,128)(2,1)}, u32[]{:S(2)}) copy-start(bf16[2,512,512]{2,1,0:T(8,128)(2,1)} %select_convert_fusion.1) | copy-start | bytes 3145732
  44.0 11.2 %collective-permute-start.2 = (bf16[8,2,2,32,128]{4,3,2,1,0:T(8,128)(2,1)S(1)}, bf16[8,2,2,32,128]{4,3,2,1,0:T(8,128)(2,1)S(1)}, u32[]{:S(2)}, u32[]{:S(2)}) collective-permute-start(bf16[8,2,2,32,128]{4,3,2,1,0:T(8,128)(2,1)S(1)} %get-tuple-element.14), channel_id=1, source_target_pairs={{0,4},{4,8},{8,12},{12,0},{1,5},{5,9},{9,13},{13,1},{2,6},{6,10},{... | collective-permute-start | bytes 786440 | tf_op jit(solution)/shard_map/ppermute | solution.py:20
  44.8 20.5 %collective-permute-start.4 = (bf16[8,2,2,32,128]{4,3,2,1,0:T(8,128)(2,1)S(1)}, bf16[8,2,2,32,128]{4,3,2,1,0:T(8,128)(2,1)S(1)}, u32[]{:S(2)}, u32[]{:S(2)}) collective-permute-start(bf16[8,2,2,32,128]{4,3,2,1,0:T(8,128)(2,1)S(1)} %get-tuple-element.15), channel_id=1, source_target_pairs={{0,8},{4,12},{8,0},{12,4},{1,9},{5,13},{9,1},{13,5},{2,10},{6,14},... | collective-permute-start | bytes 786440 | tf_op jit(solution)/shard_map/ppermute | solution.py:20
  45.1 20.2 %collective-permute-start.6 = (bf16[8,2,2,32,128]{4,3,2,1,0:T(8,128)(2,1)S(1)}, bf16[8,2,2,32,128]{4,3,2,1,0:T(8,128)(2,1)S(1)}, u32[]{:S(2)}, u32[]{:S(2)}) collective-permute-start(bf16[8,2,2,32,128]{4,3,2,1,0:T(8,128)(2,1)S(1)} %get-tuple-element.16), channel_id=1, source_target_pairs={{0,12},{4,0},{8,4},{12,8},{1,13},{5,1},{9,5},{13,9},{2,14},{6,2},{... | collective-permute-start | bytes 786440 | tf_op jit(solution)/shard_map/ppermute | solution.py:20
  48.1 22.8 %collective-permute-start.1 = (bf16[8,2,2,32,128]{4,3,2,1,0:T(8,128)(2,1)S(1)}, bf16[8,2,2,32,128]{4,3,2,1,0:T(8,128)(2,1)S(1)}, u32[]{:S(2)}, u32[]{:S(2)}) collective-permute-start(bf16[8,2,2,32,128]{4,3,2,1,0:T(8,128)(2,1)S(1)} %get-tuple-element.13.refs_0_), channel_id=1, source_target_pairs={{0,1},{1,0},{2,3},{3,2},{4,5},{5,4},{6,7},{7,6},{8,9},{9,8},{10,11... | collective-permute-start | bytes 786440 | tf_op jit(solution)/shard_map/ppermute | solution.py:20
  55.2 15.7 %collective-permute-start.3 = (bf16[8,2,2,32,128]{4,3,2,1,0:T(8,128)(2,1)S(1)}, bf16[8,2,2,32,128]{4,3,2,1,0:T(8,128)(2,1)S(1)}, u32[]{:S(2)}, u32[]{:S(2)}) collective-permute-start(bf16[8,2,2,32,128]{4,3,2,1,0:T(8,128)(2,1)S(1)} %collective-permute-done.2.refs_2_), channel_id=1, source_target_pairs={{0,1},{1,0},{2,3},{3,2},{4,5},{5,4},{6,7},{7,6},{8,9},{9,8},{10,11... | collective-permute-start | bytes 786440 | tf_op jit(solution)/shard_map/ppermute | solution.py:20
  65.3 5.6 %collective-permute-start.5 = (bf16[8,2,2,32,128]{4,3,2,1,0:T(8,128)(2,1)S(1)}, bf16[8,2,2,32,128]{4,3,2,1,0:T(8,128)(2,1)S(1)}, u32[]{:S(2)}, u32[]{:S(2)}) collective-permute-start(bf16[8,2,2,32,128]{4,3,2,1,0:T(8,128)(2,1)S(1)} %collective-permute-done.4.refs_4_), channel_id=1, source_target_pairs={{0,1},{1,0},{2,3},{3,2},{4,5},{5,4},{6,7},{7,6},{8,9},{9,8},{10,11... | collective-permute-start | bytes 786440 | tf_op jit(solution)/shard_map/ppermute | solution.py:20
  65.3 5.6 %collective-permute-start.7 = (bf16[8,2,2,32,128]{4,3,2,1,0:T(8,128)(2,1)S(1)}, bf16[8,2,2,32,128]{4,3,2,1,0:T(8,128)(2,1)S(1)}, u32[]{:S(2)}, u32[]{:S(2)}) collective-permute-start(bf16[8,2,2,32,128]{4,3,2,1,0:T(8,128)(2,1)S(1)} %collective-permute-done.6.refs_6_), channel_id=1, source_target_pairs={{0,1},{1,0},{2,3},{3,2},{4,5},{5,4},{6,7},{7,6},{8,9},{9,8},{10,11... | collective-permute-start | bytes 786440 | tf_op jit(solution)/shard_map/ppermute | solution.py:20
  74.7 8.9 %collective-permute-start.15 = (f32[512,128]{1,0:T(8,128)S(1)}, f32[512,128]{1,0:T(8,128)S(1)}, u32[]{:S(2)}, u32[]{:S(2)}) collective-permute-start(f32[512,128]{1,0:T(8,128)S(1)} %slice.57), channel_id=1, source_target_pairs={{0,2},{2,0},{1,3},{3,1},{4,6},{6,4},{5,7},{7,5},{8,10},{10,8},{9,1... | collective-permute-start | bytes 786440 | tf_op jit(solution)/shard_map/ppermute | solution.py:20
  83.7 8.0 %collective-permute-start.16 = (f32[128,128]{1,0:T(8,128)S(1)}, f32[128,128]{1,0:T(8,128)S(1)}, u32[]{:S(2)}, u32[]{:S(2)}) collective-permute-start(f32[128,128]{1,0:T(8,128)S(1)} %get-tuple-element.23), channel_id=1, source_target_pairs={{0,4},{4,8},{8,12},{12,0},{1,5},{5,9},{9,13},{13,1},{2,6},{6,10},{... | collective-permute-start | bytes 196616 | tf_op jit(solution)/shard_map/ppermute | solution.py:20
  89.2 6.2 %collective-permute-start.17 = (f32[128,128]{1,0:T(8,128)S(1)}, f32[128,128]{1,0:T(8,128)S(1)}, u32[]{:S(2)}, u32[]{:S(2)}) collective-permute-start(f32[128,128]{1,0:T(8,128)S(1)} %get-tuple-element.25), channel_id=1, source_target_pairs={{0,8},{4,12},{8,0},{12,4},{1,9},{5,13},{9,1},{13,5},{2,10},{6,14},... | collective-permute-start | bytes 196616 | tf_op jit(solution)/shard_map/ppermute | solution.py:20
  89.2 6.2 %collective-permute-start.18 = (f32[128,128]{1,0:T(8,128)S(1)}, f32[128,128]{1,0:T(8,128)S(1)}, u32[]{:S(2)}, u32[]{:S(2)}) collective-permute-start(f32[128,128]{1,0:T(8,128)S(1)} %get-tuple-element.24), channel_id=1, source_target_pairs={{0,12},{4,0},{8,4},{12,8},{1,13},{5,1},{9,5},{13,9},{2,14},{6,2},{... | collective-permute-start | bytes 196616 | tf_op jit(solution)/shard_map/ppermute | solution.py:20
where the time goes:
time: 96.6 us; the launch traced here: 96.2 us
  waiting for transfers between devices  30.3 us (31%)
  starting transfers between devices  26.2 us (27%)
  Pallas kernels  15.2 us (16%)
  local copies, waits for them, and re-layouts  15.1 us (16%)
  other arithmetic  8.25 us (9%)
    ppermute x18, waiting for transfers between devices, rotated(): lax.ppermute(value, axis, [(source, (source + steps) % count) for source...  27.4 us
    ppermute x18, starting transfers between devices, rotated(): lax.ppermute(value, axis, [(source, (source + steps) % count) for source...  22.7 us
    pallas_call x2, Pallas kernels, beam_sums(): pl.pallas_call(functools.partial(beam_kernel, len(spectra), sums is not N...  8.65 us
    unnamed x24, local copies, waits for them, and re-layouts  7.51 us
    pallas_call x2, Pallas kernels, make_spectra(): pl.pallas_call(functools.partial(spectra_kernel, first, frames, length, h...  6.56 us
    another operation x2, other arithmetic  4.99 us
    ppermute x1, starting transfers between devices, from_previous(): lax.ppermute(value, axis, [(source, source + 1) for source in range(count...  3.43 us
    ppermute x1, waiting for transfers between devices, from_previous(): lax.ppermute(value, axis, [(source, source + 1) for source in range(count...  2.98 us
  transfers between devices with their start and end apart: 19, of which 5 were waited for; matrix products, arithmetic and copies ran while one was open for 16% of the time, Pallas kernels for 8%

commit v1 on v0

v1 whole, which is shorter than its diff:
```python
import functools
import math

import jax
import jax.numpy as jnp
import numpy as np
from jax import lax
from jax.experimental import pallas as pl
from jax.experimental.pallas import tpu as pltpu
from jax.sharding import PartitionSpec as P

VMEM_BYTES = 24 << 20
ALL_VMEM_BYTES = 60 << 20
LANES = 128
SMALL_COST = 1024
WIDE = 256
ROW_BLOCK = 32


def partner(index, step, count):
    return index ^ (-step % count) if count & (count - 1) == 0 else (index + step) % count


def source_of(index, step, count):
    return index ^ (-step % count) if count & (count - 1) == 0 else (index - step) % count


def exchanged(value, axis, step):
    count = lax.axis_size(axis)
    return lax.ppermute(value, axis, [(source, partner(source, step, count)) for source in range(count)])


def picked_blocks(value, axis, indices):
    return jnp.concatenate([lax.dynamic_slice_in_dim(value, i, 1, axis) for i in indices], axis=axis)


def from_previous(value, axis):
    count = lax.axis_size(axis)
    return lax.ppermute(value, axis, [(source, source + 1) for source in range(count - 1)])


def dft_blocks(length, blocks):
    channels = length // 2
    phase = (np.arange(length)[:, None] * np.arange(channels)[None, :] % length) * (2.0 * math.pi / length)
    table = np.stack([np.cos(phase), -np.sin(phase)], axis=1).reshape(length, 2, blocks, channels // blocks)
    return jnp.asarray(np.transpose(table, (2, 0, 1, 3)).reshape(blocks, length, -1), jnp.bfloat16)


def vmem_spec():
    return pl.BlockSpec(memory_space=pltpu.VMEM)


def spectra_kernel(first, frames, length, has_rim, *refs):
    me_ref, refs = refs[0], refs[1:]
    rim_hbm, refs = (refs[0], refs[1:]) if has_rim else (None, refs)
    volt_hbm, taps_hbm, dft_hbm = refs[:3]
    outs, (volt, taps_ref, dft_ref, filt, spread, made, sems) = refs[3:-7], refs[-7:]
    taps = taps_ref.shape[0]
    rows = volt.shape[1]
    row_block = spread.shape[1]
    half = row_block // 2
    history = taps - 1

    copies = [pltpu.make_async_copy(taps_hbm, taps_ref, sems.at[0])]
    for slot in range(history + frames):
        frame = first + slot - history
        source, at = (rim_hbm, (frame + history) * length) if frame < 0 else (volt_hbm, frame * length)
        copies.append(pltpu.make_async_copy(source.at[:, pl.ds(at, length)], volt.at[slot], sems.at[2 + slot]))
    table_copy = pltpu.make_async_copy(dft_hbm, dft_ref, sems.at[1])
    for copy in copies:
        copy.start()
    table_copy.start()
    for copy in copies:
        copy.wait()

    def columns(n, _):
        lane = pl.multiple_of(n * LANES, LANES)
        weights = [taps_ref[t : t + 1, pl.ds(lane, LANES)] for t in range(taps)]
        for block in range(rows // row_block):
            row = block * row_block

            def load(slot):
                return volt[slot, row : row + row_block, pl.ds(lane, LANES)].astype(jnp.float32)

            window = [load(t) for t in range(history)]
            for f in range(frames):
                window.append(load(f + history))
                total = weights[0] * window[0]
                for t in range(1, taps):
                    total = total + weights[t] * window[t]
                window.pop(0)
                slot = (block * frames + f) % spread.shape[0]
                spread[slot] = total
                for p in range(2):
                    picked = spread[slot, pl.ds(p, half, stride=2), :]
                    filt[pl.ds((f * 2 + p) * (rows // 2) + block * half, half), pl.ds(lane, LANES)] = picked.astype(
                        jnp.bfloat16
                    )
        return 0

    lax.fori_loop(0, length // LANES, columns, 0)
    table_copy.wait()
    count = dft_ref.shape[0]
    stations = rows // 2
    channels = outs[0].shape[-1]
    writes = []
    for d in (*range(1, count), 0):
        block = partner(me_ref[0], d, count)
        result = jnp.dot(filt[...], dft_ref[block], preferred_element_type=jnp.float32).astype(jnp.bfloat16)
        for f in range(frames):
            for p in range(2):
                at = (f * 2 + p) * stations
                for r in range(2):
                    made[d, f, p, r] = result[at : at + stations, r * channels : (r + 1) * channels]
        writes.append(pltpu.make_async_copy(made.at[d], outs[d], sems.at[sems.shape[0] - 1 - d]))
        writes[-1].start()
    for write in writes:
        write.wait()


def make_spectra(me, rim, voltages, filter_taps, dft, first, frames):
    rows = voltages.shape[0]
    taps, length = filter_taps.shape
    count = dft.shape[0]
    channels = dft.shape[2] // 2
    has_rim = rim is not None
    operands = ([rim] if has_rim else []) + [voltages, filter_taps, dft]
    shape = (frames, 2, 2, rows // 2, channels)
    slots = frames + taps - 1
    return pl.pallas_call(
        functools.partial(spectra_kernel, first, frames, length, has_rim),
        out_shape=[jax.ShapeDtypeStruct(shape, jnp.bfloat16)] * count,
        in_specs=[pl.BlockSpec(memory_space=pltpu.SMEM)] + [pl.BlockSpec(memory_space=pl.ANY)] * len(operands),
        out_specs=[pl.BlockSpec(memory_space=pl.ANY)] * count,
        scratch_shapes=[
            pltpu.VMEM((slots, rows, length), jnp.bfloat16),
            pltpu.VMEM((taps, length), jnp.float32),
            pltpu.VMEM(dft.shape, jnp.bfloat16),
            pltpu.VMEM((frames * rows, length), jnp.bfloat16),
            pltpu.VMEM((8, min(rows, ROW_BLOCK), LANES), jnp.float32),
            pltpu.VMEM((count, *shape), jnp.bfloat16),
            pltpu.SemaphoreType.DMA((slots + 2 + count,)),
        ],
        compiler_params=pltpu.CompilerParams(vmem_limit_bytes=ALL_VMEM_BYTES),
        cost_estimate=pl.CostEstimate(flops=SMALL_COST, bytes_accessed=SMALL_COST, transcendentals=0),
        name=f"spectra_{first}",
    )(me, *operands)


def channel_power(spectra, mixers_ref, high, low):
    frames, _, _, _, channels = spectra[0].shape
    beams = mixers_ref.shape[1] // 2
    step = min(frames, max(1, WIDE // channels))

    def group(i, over_frames):
        power = None
        for p in range(2):
            sides = []
            for side in range(step):
                parts = []
                for piece in spectra:
                    for r in range(2):
                        parts.append(piece[i * step + side, p, r])
                sides.append(jnp.concatenate(parts, axis=0))
            stacked = jnp.concatenate(sides, axis=1)
            voltage = jnp.dot(mixers_ref[p], stacked, preferred_element_type=jnp.float32)
            real_part, imag_part = voltage[:beams], voltage[beams:]
            term = real_part * real_part + imag_part * imag_part
            power = term if power is None else power + term
        upper = power.astype(jnp.bfloat16)
        at = pl.multiple_of(i * step * channels, step * channels)
        high[:, pl.ds(at, step * channels)] = upper
        low[:, pl.ds(at, step * channels)] = (power - upper.astype(jnp.float32)).astype(jnp.bfloat16)
        for side in range(step):
            over_frames = over_frames + power[:, side * channels : (side + 1) * channels]
        return over_frames

    return lax.fori_loop(0, frames // step, group, jnp.zeros((beams, channels), jnp.float32))


def placed(high, low, place_ref):
    total = jnp.dot(high[...], place_ref[...], preferred_element_type=jnp.float32)
    return total + jnp.dot(low[...], place_ref[...], preferred_element_type=jnp.float32)


def first_kernel(pieces, *refs):
    spectra, (mixers_ref, place_ref, sums_ref, level_ref, high, low) = refs[:pieces], refs[pieces:]
    level_ref[...] = channel_power(spectra, mixers_ref, high, low).astype(jnp.bfloat16)
    sums_ref[...] = placed(high, low, place_ref)


def last_kernel(pieces, levels, level_scale, *refs):
    spectra, refs = refs[:pieces], refs[pieces:]
    level_refs, refs = refs[:levels], refs[levels:]
    mixers_ref, place_ref, centre_ref, earlier_ref, out, high, low = refs
    channel_power(spectra, mixers_ref, high, low)
    level = level_refs[0][...].astype(jnp.float32)
    for ref in level_refs[1:]:
        level = level + ref[...].astype(jnp.float32)
    level = (level * level_scale).astype(jnp.bfloat16)
    total = earlier_ref[...] - jnp.dot(level, centre_ref[...], preferred_element_type=jnp.float32)
    total = total + placed(high, low, place_ref)
    blocks, share, width = out.shape
    groups = total.shape[1] // width
    for block in range(blocks):
        row, column = block // groups * share, block % groups * width
        out[block] = total[row : row + share, column : column + width].astype(jnp.bfloat16)


def beam_call(kernel, name, out_shape, spectra, mixers, *rest):
    frames, _, _, _, channels = spectra[0].shape
    beams = mixers.shape[1] // 2
    operands = [*spectra, *rest]
    return pl.pallas_call(
        kernel,
        out_shape=out_shape,
        in_specs=[vmem_spec()] * len(operands),
        out_specs=jax.tree.map(lambda _: vmem_spec(), out_shape),
        scratch_shapes=[pltpu.VMEM((beams, frames * channels), jnp.bfloat16)] * 2,
        compiler_params=pltpu.CompilerParams(vmem_limit_bytes=VMEM_BYTES),
        cost_estimate=pl.CostEstimate(flops=SMALL_COST, bytes_accessed=SMALL_COST, transcendentals=0),
        name=name,
    )(*operands)


def tables_kernel(total, *refs):
    where_ref, order_ref, weights_ref, delay_ref, mixers_ref, place_ref, centre_ref = refs
    time = where_ref[0]
    stations = weights_ref.shape[1]
    beams = mixers_ref.shape[1] // 2
    inputs = mixers_ref.shape[2]
    station = lax.broadcasted_iota(jnp.int32, (stations, inputs), 0)
    imag_column = order_ref[2:3, :] == 1
    for p in range(2):
        select = (station == order_ref[p : p + 1, :]).astype(jnp.bfloat16)
        picked = []
        for r in range(2):
            picked.append(
                lax.dot_general(
                    weights_ref[r], select, (((0,), (0,)), ((), ())), preferred_element_type=jnp.float32
                )
            )
        real_part, imag_part = picked
        mixers_ref[p, :beams, :] = jnp.where(imag_column, -imag_part, real_part).astype(jnp.bfloat16)
        mixers_ref[p, beams:, :] = jnp.where(imag_column, real_part, imag_part).astype(jnp.bfloat16)
    channels, curves = delay_ref.shape
    frames, _, width = place_ref.shape
    lane = lax.broadcasted_iota(jnp.int32, (1, width), 1)
    curve = lane // frames % curves
    wanted = lane // (frames * curves) * frames + lane % frames
    source = jnp.broadcast_to(wanted, (channels, width))
    for d in range(curves):
        source = source + jnp.where(curve == d, delay_ref[:, d : d + 1], 0)
    base = jnp.where(source < total, 1.0 / total, 0.0)
    for f in range(frames):
        hit = jnp.where(source == time * frames + f, 1.0, 0.0)
        place_ref[f] = (hit - base).astype(jnp.bfloat16)
    held = jnp.where((source >= time * frames) & (source < (time + 1) * frames), 1.0, 0.0)
    centre_ref[...] = (held - base * frames).astype(jnp.bfloat16)


def make_tables(beam_weights, station_index, delay_table, in_dev, frames_dev):
    chan_devices = lax.axis_size("chan")
    beam_devices = lax.axis_size("beam")
    time_devices = lax.axis_size("tm")
    here, core = lax.axis_index("chan"), lax.axis_index("beam")
    stations = beam_weights.shape[0]
    arranged = jnp.transpose(beam_weights, (1, 0, 2)).reshape(2, stations, chan_devices, beam_devices, -1)
    chosen = lax.dynamic_index_in_dim(arranged, core, 3, keepdims=False)
    chosen = chosen.reshape(2, stations, -1)
    order = station_index.reshape(chan_devices, beam_devices, in_dev // 2, 2)
    order = picked_blocks(order, 0, [source_of(here, d, chan_devices) for d in range(chan_devices)])
    order = picked_blocks(order, 1, [source_of(core, e, beam_devices) for e in range(beam_devices)])
    order = jnp.transpose(order, (3, 0, 1, 2))
    order = jnp.broadcast_to(order[:, :, :, None, :], (*order.shape[:3], 2, in_dev // 2)).reshape(2, -1)
    imag_column = jnp.arange(order.shape[1], dtype=jnp.int32) // (in_dev // 2) % 2
    order = jnp.concatenate([order, imag_column[None]], axis=0)
    where = lax.axis_index("tm").astype(jnp.int32).reshape(1)
    channels, curves = delay_table.shape
    beams = chosen.shape[2]
    inputs = order.shape[1]
    width = time_devices * curves * frames_dev
    return pl.pallas_call(
        functools.partial(tables_kernel, time_devices * frames_dev),
        out_shape=[
            jax.ShapeDtypeStruct((2, 2 * beams, inputs), jnp.bfloat16),
            jax.ShapeDtypeStruct((frames_dev, channels, width), jnp.bfloat16),
            jax.ShapeDtypeStruct((channels, width), jnp.bfloat16),
        ],
        in_specs=[pl.BlockSpec(memory_space=pltpu.SMEM)] + [vmem_spec()] * 3,
        out_specs=[vmem_spec()] * 3,
        compiler_params=pltpu.CompilerParams(vmem_limit_bytes=VMEM_BYTES),
        cost_estimate=pl.CostEstimate(flops=SMALL_COST, bytes_accessed=SMALL_COST, transcendentals=0),
        name="tables",
    )(where, order, chosen, delay_table)


def shards(voltages, filter_taps, beam_weights, station_index, delay_table):
    taps, length = filter_taps.shape
    in_dev = voltages.shape[0]
    frames_dev = voltages.shape[1] // length
    chan_devices = lax.axis_size("chan")
    beam_devices = lax.axis_size("beam")
    time_devices = lax.axis_size("tm")
    channels = delay_table.shape[0]
    curves = delay_table.shape[1]
    me = lax.axis_index("chan").astype(jnp.int32).reshape(1)
    dft = dft_blocks(length, chan_devices)
    history = taps - 1
    rim = from_previous(voltages[:, (frames_dev - history) * length :], "tm")
    half = frames_dev // 2
    ready = []
    for first, frames in ((half, frames_dev - half), (0, half)):
        if first < history:
            rim, mixers, place, centre = lax.optimization_barrier((rim, mixers, place, centre))
        own = list(make_spectra(me, rim if first < history else None, voltages, filter_taps, dft, first, frames))
        if first >= history:
            late, own[0] = lax.optimization_barrier(((beam_weights, station_index, delay_table), own[0]))
            mixers, place, centre = make_tables(*late, in_dev, frames_dev)
            place = place.reshape(frames_dev * channels, -1)
        arrived = {d: exchanged(own[d], "chan", d) for d in range(chan_devices - 1, 0, -1)}
        ready.append([own[0]] + [arrived[d] for d in range(1, chan_devices)])
    ready[0], ready[1][0] = lax.optimization_barrier((ready[0], ready[1][0]))

    def with_hops(arrived):
        pieces = []
        for here in arrived:
            pieces += [here] + [exchanged(here, "beam", e) for e in range(1, beam_devices)]
        return pieces

    beams = mixers.shape[1] // 2
    spectra = with_hops(ready[0])
    shapes = [
        jax.ShapeDtypeStruct((beams, place.shape[1]), jnp.float32),
        jax.ShapeDtypeStruct((beams, channels), jnp.bfloat16),
    ]
    sums, level = beam_call(
        functools.partial(first_kernel, len(spectra)),
        "beam_first",
        shapes,
        spectra,
        mixers,
        mixers,
        place[half * channels :],
    )
    levels = [level] + [exchanged(level, "tm", e) for e in range(1, time_devices)]
    ready[1], sums, levels = lax.optimization_barrier((ready[1], sums, levels))
    spectra = with_hops(ready[1])
    level_scale = 1.0 / (time_devices * (frames_dev - half))
    share = beams // chan_devices
    blocks = beam_call(
        functools.partial(last_kernel, len(spectra), len(levels), level_scale),
        "beam_last",
        jax.ShapeDtypeStruct((chan_devices * time_devices, share, curves * frames_dev), jnp.bfloat16),
        spectra,
        mixers,
        *levels,
        mixers,
        place[: half * channels],
        centre,
        sums,
    )
    blocks = lax.all_to_all(blocks, ("chan", "tm"), split_axis=0, concat_axis=0, tiled=True)
    final = jnp.sum(blocks.astype(jnp.float32), axis=0)
    return (final * (1.0 / math.sqrt(length // 2))).reshape(share, curves, frames_dev)


def solution(mesh):
    in_specs = (P(("groups", "chan", "beam"), "tm"), P(), P(), P(), P("chan", None))
    out_specs = P(("groups", "chan", "beam"), None, "tm")
    return jax.shard_map(shards, mesh=mesh, in_specs=in_specs, out_specs=out_specs, check_vma=False)
```

time: 96.6 us -> 84.5 us (0.87)
  blocking collectives: 0 us -> 11.9 us
  starting transfers between devices: 26.2 us -> 16.8 us
  other arithmetic: 8.25 us -> 0.09 us
  local copies, waits for them, and re-layouts: 15.1 us -> 7.93 us
  Pallas kernels: 15.2 us -> 20.7 us
  waiting for transfers between devices: 30.3 us -> 26.5 us
    all_to_all x0 -> x1, blocking collectives: none -> 11.9 us  [shards(): lax.all_to_all(blocks, ('chan', 'tm'), split_axis=0, concat_axis=0, tiled...]
    ppermute x18 -> x15, starting transfers between devices: 22.7 us -> 11 us  [exchanged(): lax.ppermute(value, axis, [(source, partner(source, step, count)) for sou...]
    unnamed x24 -> x10, local copies, waits for them, and re-layouts: 7.51 us -> 0.02 us
    another operation x2 -> x0, other arithmetic: 4.99 us -> none
    pallas_call x2, Pallas kernels: 6.56 us -> 11.1 us  [make_spectra(): pl.pallas_call(functools.partial(spectra_kernel, first, frames, length, h...]
    ppermute x18 -> x15, waiting for transfers between devices: 27.4 us -> 23.8 us  [exchanged(): lax.ppermute(value, axis, [(source, partner(source, step, count)) for sou...]
    ppermute x1, starting transfers between devices: 3.43 us -> 5.78 us  [from_previous(): lax.ppermute(value, axis, [(source, source + 1) for source in range(count...]
    select_n x1 -> x0, local copies, waits for them, and re-layouts: 1.65 us -> none  [make_place(): base = jnp.where(source < total, 1.0 / total, 0.0)[None]]
  transfers between devices with their start and end apart: 19 -> 16, of which waited for: 5 -> 8; matrix products, arithmetic and copies ran while one was open for 16% -> 6% of each run, Pallas kernels for 8% -> 20%
where the time goes in v1:
time: 84.5 us; the launch traced here: 84.2 us
  waiting for transfers between devices  26.5 us (31%)
  Pallas kernels  20.7 us (24%)
  starting transfers between devices  16.8 us (20%)
  blocking collectives  11.9 us (14%)
  local copies, waits for them, and re-layouts  7.93 us (9%)
    ppermute x15, waiting for transfers between devices, exchanged(): lax.ppermute(value, axis, [(source, partner(source, step, count)) for sou...  23.8 us
    all_to_all x1, blocking collectives, shards(): lax.all_to_all(blocks, ('chan', 'tm'), split_axis=0, concat_axis=0, tiled...  11.9 us
    pallas_call x2, Pallas kernels, make_spectra(): pl.pallas_call(functools.partial(spectra_kernel, first, frames, length, h...  11.1 us
    ppermute x15, starting transfers between devices, exchanged(): lax.ppermute(value, axis, [(source, partner(source, step, count)) for sou...  11 us
    pallas_call x2, Pallas kernels, beam_call(): pl.pallas_call(kernel, out_shape=out_shape, in_specs=[vmem_spec()] * len(...  8.61 us
    ppermute x1, starting transfers between devices, from_previous(): lax.ppermute(value, axis, [(source, source + 1) for source in range(count...  5.78 us
    dynamic_slice x1, local copies, waits for them, and re-layouts, make_tables(): chosen = lax.dynamic_index_in_dim(arranged, core, 3, keepdims=False)  3.27 us
    ppermute x1, waiting for transfers between devices, from_previous(): lax.ppermute(value, axis, [(source, source + 1) for source in range(count...  2.74 us
  transfers between devices with their start and end apart: 16, of which 8 were waited for; matrix products, arithmetic and copies ran while one was open for 6% of the time, Pallas kernels for 20%

profile of v1, /device:TPU:0, one launch (start us, length us, event | category | flops | bytes accessed | tf_op | source)
XLA Modules:
  0.0 84.2 jit_solution(8117309016024858920)
XLA Ops:
  0.0 2.2 %slice.9 = bf16[64,7168]{1,0:T(8,128)(2,1)} slice(bf16[64,16384]{1,0:T(8,128)(2,1)} %refs_2_.3), slice={[0:64], [9216:16384]} | slice | bytes 1835008 | tf_op jit(solution)/shard_map/slice | solution.py:310
  2.2 5.8 %collective-permute-start.3 = (bf16[64,7168]{1,0:T(8,128)(2,1)}, bf16[64,7168]{1,0:T(8,128)(2,1)}, u32[]{:S(2)}, u32[]{:S(2)}) collective-permute-start(bf16[64,7168]{1,0:T(8,128)(2,1)} %slice.9), channel_id=1, source_target_pairs={{0,2},{1,3},{4,6},{5,7},{8,10},{9,11},{12,14},{13,15},{16,18},{17,... | collective-permute-start | bytes 2752520 | tf_op jit(solution)/shard_map/ppermute | solution.py:39
  8.0 0.0 copy-start.4
  8.0 0.0 copy-start.2
  8.0 5.6 %spectra_8.1 = (bf16[8,2,2,32,128]{4,3,2,1,0:T(8,128)(2,1)}, bf16[8,2,2,32,128]{4,3,2,1,0:T(8,128)(2,1)}, bf16[8,2,2,32,128]{4,3,2,1,0:T(8,128)(2,1)}, bf16[8,2,2,32,128]{4,3,2,1,0:T(8,128)(2,1)}) custom-call(s32[1]{0:T(128)} %bitcast.refs_0_, bf16[64,16384]{1,0:T(8,128)(2,1)} %refs_2_.3, f32[8,1024]{1,0:T(8,128)} %refs_3_.2, ...), custom_call_target="tpu_custom_call" | custom-call | flops 1024 | bytes 1024 | tf_op jit(solution)/shard_map/spectra_8/pallas_call | solution.py:130
  13.5 3.7 %collective-permute-start = (bf16[8,2,2,32,128]{4,3,2,1,0:T(8,128)(2,1)}, bf16[8,2,2,32,128]{4,3,2,1,0:T(8,128)(2,1)S(1)}, u32[]{:S(2)}, u32[]{:S(2)}) collective-permute-start(bf16[8,2,2,32,128]{4,3,2,1,0:T(8,128)(2,1)} %get-tuple-element.40), channel_id=1, source_target_pairs={{0,12},{4,8},{8,4},{12,0},{1,13},{5,9},{9,5},{13,1},{2,14},{6,10},... | collective-permute-start | bytes 786440 | tf_op jit(solution)/shard_map/ppermute | solution.py:30
  17.2 0.0 collective-permute-start.1
  17.2 0.8 collective-permute-start.2
  18.0 0.0 copy-done.4
  18.0 0.1 reshape.96
  18.1 0.0 copy-start.3
  18.2 0.1 copy.20
  18.3 0.1 copy.23
  18.4 0.1 copy.22
  18.5 0.1 copy.21
  18.5 0.0 copy-done.2
  18.5 0.7 reshape.98
  19.3 3.3 %dynamic-slice_reduce_fusion = bf16[2,256,4,128]{3,2,0,1:T(4,128)(2,1)S(1)} fusion(bf16[2,256,4,2,128]{4,3,2,0,1:T(2,128)(2,1)S(1)} %reshape.98, s32[]{:T(128)S(6)} %select_n.50), kind=kLoop, calls=%fused_computation | loop fusion | bytes 1048580 | tf_op jit(solution)/shard_map/jit(dynamic_index_in_dim)/dynamic_slice | solution.py:269
  22.6 0.0 copy-done.3
  22.6 0.1 copy.26.refs_3_
  22.7 0.1 reshape.97
  22.8 0.2 reshape.101
  23.0 0.1 copy.29.refs_2_
  23.1 1.1 %tables.1 = (bf16[2,1024,512]{2,1,0:T(8,128)(2,1)S(1)}, bf16[16,128,256]{2,1,0:T(8,128)(2,1)S(1)}, bf16[128,256]{1,0:T(8,128)(2,1)S(1)}) custom-call(s32[1]{0:T(128)} %bitcast.1.refs_0_, s32[3,512]{1,0:T(4,128)S(1)} %pad_add_fusion.1.refs_1_, bf16[2,256,512]{2,1,0:T(8,128)(2,1)S(1)} %copy.29.refs_2_, s32[128,8]{1,0:T(8,128)S(1)} %copy.26.refs_3_), custom_call_target="tpu_custom_call" | custom-call | flops 1024 | bytes 1024 | tf_op jit(solution)/shard_map/tables/pallas_call | solution.py:283
  24.2 2.7 %collective-permute-done.3.refs_1_ = bf16[64,7168]{1,0:T(8,128)(2,1)} collective-permute-done((bf16[64,7168]{1,0:T(8,128)(2,1)}, bf16[64,7168]{1,0:T(8,128)(2,1)}, u32[]{:S(2)}, u32[]{:S(2)}) %collective-permute-start.3) | collective-permute-done | bytes 917536 | tf_op jit(solution)/shard_map/ppermute | solution.py:39
  26.9 0.0 copy-start
  26.9 5.5 %spectra_0.1 = (bf16[8,2,2,32,128]{4,3,2,1,0:T(8,128)(2,1)}, bf16[8,2,2,32,128]{4,3,2,1,0:T(8,128)(2,1)}, bf16[8,2,2,32,128]{4,3,2,1,0:T(8,128)(2,1)}, bf16[8,2,2,32,128]{4,3,2,1,0:T(8,128)(2,1)}) custom-call(s32[1]{0:T(128)} %bitcast.refs_0_, bf16[64,7168]{1,0:T(8,128)(2,1)} %collective-permute-done.3.refs_1_, bf16[64,16384]{1,0:T(8,128)(2,1)} %refs_2_.3, ...), custom_call_target="tpu_custom_call" | custom-call | flops 1024 | bytes 1024 | tf_op jit(solution)/shard_map/spectra_0/pallas_call | solution.py:130
  32.4 0.0 collective-permute-done.refs_2_
  32.4 7.0 %collective-permute-done.1.refs_4_ = bf16[8,2,2,32,128]{4,3,2,1,0:T(8,128)(2,1)S(1)} collective-permute-done((bf16[8,2,2,32,128]{4,3,2,1,0:T(8,128)(2,1)}, bf16[8,2,2,32,128]{4,3,2,1,0:T(8,128)(2,1)S(1)}, u32[]{:S(2)}, u32[]{:S(2)}) %collective-permute-start.1) | collective-permute-done | bytes 262176 | tf_op jit(solution)/shard_map/ppermute | solution.py:30
  39.5 0.0 collective-permute-done.2.refs_6_
  39.5 0.0 copy-done
  39.5 0.0 collective-permute-start.7
  39.5 0.5 collective-permute-start.8
  40.0 0.1 collective-permute-start.9
  40.0 0.4 collective-permute-start.10
  40.5 2.5 %collective-permute-start.4 = (bf16[8,2,2,32,128]{4,3,2,1,0:T(8,128)(2,1)}, bf16[8,2,2,32,128]{4,3,2,1,0:T(8,128)(2,1)S(1)}, u32[]{:S(2)}, u32[]{:S(2)}) collective-permute-start(bf16[8,2,2,32,128]{4,3,2,1,0:T(8,128)(2,1)} %get-tuple-element.52), channel_id=1, source_target_pairs={{0,12},{4,8},{8,4},{12,0},{1,13},{5,9},{9,5},{13,1},{2,14},{6,10},... | collective-permute-start | bytes 786440 | tf_op jit(solution)/shard_map/ppermute | solution.py:30
  43.0 0.0 collective-permute-done.7.refs_1_
  43.0 0.0 collective-permute-start.5
  43.0 0.0 collective-permute-done.8.refs_3_
  43.0 1.9 %collective-permute-start.6 = (bf16[8,2,2,32,128]{4,3,2,1,0:T(8,128)(2,1)}, bf16[8,2,2,32,128]{4,3,2,1,0:T(8,128)(2,1)S(1)}, u32[]{:S(2)}, u32[]{:S(2)}) collective-permute-start(bf16[8,2,2,32,128]{4,3,2,1,0:T(8,128)(2,1)} %get-tuple-element.54), channel_id=1, source_target_pairs={{0,4},{4,0},{8,12},{12,8},{1,5},{5,1},{9,13},{13,9},{2,6},{6,2},{1... | collective-permute-start | bytes 786440 | tf_op jit(solution)/shard_map/ppermute | solution.py:30
  44.9 0.1 fusion.1
  45.0 0.0 collective-permute-done.9.refs_5_
  45.0 0.0 collective-permute-done.10.refs_7_
  45.0 0.0 copy-start.1
  45.0 4.8 %beam_first.1 = (f32[512,256]{1,0:T(8,128)S(1)}, bf16[512,128]{1,0:T(8,128)(2,1)S(1)}) custom-call(bf16[8,2,2,32,128]{4,3,2,1,0:T(8,128)(2,1)S(1)} %copy-done, bf16[8,2,2,32,128]{4,3,2,1,0:T(8,128)(2,1)S(1)} %collective-permute-done.7.refs_1_, bf16[8,2,2,32,128]{4,3,2,1,0:T(8,128)(2,1)S(1)} %collective-permute-done.refs_2_, ...), custom_call_target="tpu_custom_call" | custom-call | flops 1024 | bytes 1024 | tf_op jit(solution)/shard_map/beam_first/pallas_call | solution.py:214
  49.8 0.1 collective-permute-start.11
  49.9 1.9 %collective-permute-done.4.refs_2_ = bf16[8,2,2,32,128]{4,3,2,1,0:T(8,128)(2,1)S(1)} collective-permute-done((bf16[8,2,2,32,128]{4,3,2,1,0:T(8,128)(2,1)}, bf16[8,2,2,32,128]{4,3,2,1,0:T(8,128)(2,1)S(1)}, u32[]{:S(2)}, u32[]{:S(2)}) %collective-permute-start.4) | collective-permute-done | bytes 262176 | tf_op jit(solution)/shard_map/ppermute | solution.py:30
  51.8 13.2 %collective-permute-done.5.refs_4_ = bf16[8,2,2,32,128]{4,3,2,1,0:T(8,128)(2,1)S(1)} collective-permute-done((bf16[8,2,2,32,128]{4,3,2,1,0:T(8,128)(2,1)}, bf16[8,2,2,32,128]{4,3,2,1,0:T(8,128)(2,1)S(1)}, u32[]{:S(2)}, u32[]{:S(2)}) %collective-permute-start.5) | collective-permute-done | bytes 262176 | tf_op jit(solution)/shard_map/ppermute | solution.py:30
  65.0 0.0 collective-permute-done.6.refs_6_
  65.0 0.0 collective-permute-done.11.refs_9_
  65.0 0.0 copy-done.1
  65.0 0.1 collective-permute-start.12
  65.1 0.5 collective-permute-start.13
  65.6 0.1 collective-permute-start.14
  65.7 0.4 collective-permute-start.15
  66.1 0.5 collective-permute-done.12.refs_1_
  66.6 0.4 collective-permute-done.13.refs_3_
  67.0 0.4 collective-permute-done.14.refs_5_
  67.4 0.4 collective-permute-done.15.refs_7_
  67.8 3.8 %beam_last.1 = bf16[8,128,128]{2,1,0:T(8,128)(2,1)S(1)} custom-call(bf16[8,2,2,32,128]{4,3,2,1,0:T(8,128)(2,1)S(1)} %copy-done.1, bf16[8,2,2,32,128]{4,3,2,1,0:T(8,128)(2,1)S(1)} %collective-permute-done.12.refs_1_, bf16[8,2,2,32,128]{4,3,2,1,0:T(8,128)(2,1)S(1)} %collective-permute-done.4.refs_2_, ...), custom_call_target="tpu_custom_call" | custom-call | flops 1024 | bytes 1024 | tf_op jit(solution)/shard_map/beam_last/pallas_call | solution.py:214
  71.5 11.9 %all_to_all.5 = bf16[8,128,128]{2,1,0:T(8,128)(2,1)S(1)} all-to-all(bf16[8,128,128]{2,1,0:T(8,128)(2,1)S(1)} %beam_last.1), channel_id=1, replica_groups=mesh['groups'=2,'chan'=4,'tm'=2,'beam'=2] {'chan','tm'}, dimensions={0} | all-to-all | bytes 524288 | tf_op jit(solution)/shard_map/all_to_all | solution.py:363
  83.5 0.7 copy.27
  (10 shorter events, 0.1 us)
Async XLA Ops:
  2.2 24.7 %collective-permute-start.3 = (bf16[64,7168]{1,0:T(8,128)(2,1)}, bf16[64,7168]{1,0:T(8,128)(2,1)}, u32[]{:S(2)}, u32[]{:S(2)}) collective-permute-start(bf16[64,7168]{1,0:T(8,128)(2,1)} %slice.9), channel_id=1, source_target_pairs={{0,2},{1,3},{4,6},{5,7},{8,10},{9,11},{12,14},{13,15},{16,18},{17,... | collective-permute-start | bytes 2752520 | tf_op jit(solution)/shard_map/ppermute | solution.py:39
  8.0 10.0 %copy-start.4 = (s32[512]{0:T(512)S(1)}, s32[512]{0:T(512)}, u32[]{:S(2)}) copy-start(s32[512]{0:T(512)} %param.9) | copy-start | bytes 6148
  8.0 10.6 %copy-start.2 = (bf16[256,2,1024]{2,1,0:T(2,128)(2,1)S(1)}, bf16[256,2,1024]{2,1,0:T(2,128)(2,1)}, u32[]{:S(2)}) copy-start(bf16[256,2,1024]{2,1,0:T(2,128)(2,1)} %param.8) | copy-start | bytes 3145732
  13.5 18.9 %collective-permute-start = (bf16[8,2,2,32,128]{4,3,2,1,0:T(8,128)(2,1)}, bf16[8,2,2,32,128]{4,3,2,1,0:T(8,128)(2,1)S(1)}, u32[]{:S(2)}, u32[]{:S(2)}) collective-permute-start(bf16[8,2,2,32,128]{4,3,2,1,0:T(8,128)(2,1)} %get-tuple-element.40), channel_id=1, source_target_pairs={{0,12},{4,8},{8,4},{12,0},{1,13},{5,9},{9,5},{13,1},{2,14},{6,10},... | collective-permute-start | bytes 786440 | tf_op jit(solution)/shard_map/ppermute | solution.py:30
  17.2 22.2 %collective-permute-start.1 = (bf16[8,2,2,32,128]{4,3,2,1,0:T(8,128)(2,1)}, bf16[8,2,2,32,128]{4,3,2,1,0:T(8,128)(2,1)S(1)}, u32[]{:S(2)}, u32[]{:S(2)}) collective-permute-start(bf16[8,2,2,32,128]{4,3,2,1,0:T(8,128)(2,1)} %get-tuple-element.41), channel_id=1, source_target_pairs={{0,8},{4,12},{8,0},{12,4},{1,9},{5,13},{9,1},{13,5},{2,10},{6,14},... | collective-permute-start | bytes 786440 | tf_op jit(solution)/shard_map/ppermute | solution.py:30
  17.2 22.2 %collective-permute-start.2 = (bf16[8,2,2,32,128]{4,3,2,1,0:T(8,128)(2,1)}, bf16[8,2,2,32,128]{4,3,2,1,0:T(8,128)(2,1)}, u32[]{:S(2)}, u32[]{:S(2)}) collective-permute-start(bf16[8,2,2,32,128]{4,3,2,1,0:T(8,128)(2,1)} %get-tuple-element.42), channel_id=1, source_target_pairs={{0,4},{4,0},{8,12},{12,8},{1,5},{5,1},{9,13},{13,9},{2,6},{6,2},{1... | collective-permute-start | bytes 786440 | tf_op jit(solution)/shard_map/ppermute | solution.py:30
  18.1 4.4 %copy-start.3 = (s32[128,8]{0,1:T(8,128)S(1)}, s32[128,8]{0,1:T(8,128)}, u32[]{:S(2)}) copy-start(s32[128,8]{0,1:T(8,128)} %param.10) | copy-start | bytes 12292
  26.9 12.5 %copy-start = (bf16[8,2,2,32,128]{4,3,2,1,0:T(8,128)(2,1)S(1)}, bf16[8,2,2,32,128]{4,3,2,1,0:T(8,128)(2,1)}, u32[]{:S(2)}) copy-start(bf16[8,2,2,32,128]{4,3,2,1,0:T(8,128)(2,1)} %get-tuple-element.55.refs_0_) | copy-start | bytes 786436
  39.5 3.5 %collective-permute-start.7 = (bf16[8,2,2,32,128]{4,3,2,1,0:T(8,128)(2,1)S(1)}, bf16[8,2,2,32,128]{4,3,2,1,0:T(8,128)(2,1)S(1)}, u32[]{:S(2)}, u32[]{:S(2)}) collective-permute-start(bf16[8,2,2,32,128]{4,3,2,1,0:T(8,128)(2,1)S(1)} %copy-done), channel_id=1, source_target_pairs={{0,1},{1,0},{2,3},{3,2},{4,5},{5,4},{6,7},{7,6},{8,9},{9,8},{10,11... | collective-permute-start | bytes 786440 | tf_op jit(solution)/shard_map/ppermute | solution.py:30
  39.5 3.5 %collective-permute-start.8 = (bf16[8,2,2,32,128]{4,3,2,1,0:T(8,128)(2,1)S(1)}, bf16[8,2,2,32,128]{4,3,2,1,0:T(8,128)(2,1)S(1)}, u32[]{:S(2)}, u32[]{:S(2)}) collective-permute-start(bf16[8,2,2,32,128]{4,3,2,1,0:T(8,128)(2,1)S(1)} %collective-permute-done.refs_2_), channel_id=1, source_target_pairs={{0,1},{1,0},{2,3},{3,2},{4,5},{5,4},{6,7},{7,6},{8,9},{9,8},{10,11... | collective-permute-start | bytes 786440 | tf_op jit(solution)/shard_map/ppermute | solution.py:30
  40.0 5.0 %collective-permute-start.9 = (bf16[8,2,2,32,128]{4,3,2,1,0:T(8,128)(2,1)S(1)}, bf16[8,2,2,32,128]{4,3,2,1,0:T(8,128)(2,1)S(1)}, u32[]{:S(2)}, u32[]{:S(2)}) collective-permute-start(bf16[8,2,2,32,128]{4,3,2,1,0:T(8,128)(2,1)S(1)} %collective-permute-done.1.refs_4_), channel_id=1, source_target_pairs={{0,1},{1,0},{2,3},{3,2},{4,5},{5,4},{6,7},{7,6},{8,9},{9,8},{10,11... | collective-permute-start | bytes 786440 | tf_op jit(solution)/shard_map/ppermute | solution.py:30
  40.0 4.9 %collective-permute-start.10 = (bf16[8,2,2,32,128]{4,3,2,1,0:T(8,128)(2,1)}, bf16[8,2,2,32,128]{4,3,2,1,0:T(8,128)(2,1)S(1)}, u32[]{:S(2)}, u32[]{:S(2)}) collective-permute-start(bf16[8,2,2,32,128]{4,3,2,1,0:T(8,128)(2,1)} %collective-permute-done.2.refs_6_), channel_id=1, source_target_pairs={{0,1},{1,0},{2,3},{3,2},{4,5},{5,4},{6,7},{7,6},{8,9},{9,8},{10,11... | collective-permute-start | bytes 786440 | tf_op jit(solution)/shard_map/ppermute | solution.py:30
  40.5 11.3 %collective-permute-start.4 = (bf16[8,2,2,32,128]{4,3,2,1,0:T(8,128)(2,1)}, bf16[8,2,2,32,128]{4,3,2,1,0:T(8,128)(2,1)S(1)}, u32[]{:S(2)}, u32[]{:S(2)}) collective-permute-start(bf16[8,2,2,32,128]{4,3,2,1,0:T(8,128)(2,1)} %get-tuple-element.52), channel_id=1, source_target_pairs={{0,12},{4,8},{8,4},{12,0},{1,13},{5,9},{9,5},{13,1},{2,14},{6,10},... | collective-permute-start | bytes 786440 | tf_op jit(solution)/shard_map/ppermute | solution.py:30
  43.0 22.1 %collective-permute-start.5 = (bf16[8,2,2,32,128]{4,3,2,1,0:T(8,128)(2,1)}, bf16[8,2,2,32,128]{4,3,2,1,0:T(8,128)(2,1)S(1)}, u32[]{:S(2)}, u32[]{:S(2)}) collective-permute-start(bf16[8,2,2,32,128]{4,3,2,1,0:T(8,128)(2,1)} %get-tuple-element.53), channel_id=1, source_target_pairs={{0,8},{4,12},{8,0},{12,4},{1,9},{5,13},{9,1},{13,5},{2,10},{6,14},... | collective-permute-start | bytes 786440 | tf_op jit(solution)/shard_map/ppermute | solution.py:30
  43.0 22.1 %collective-permute-start.6 = (bf16[8,2,2,32,128]{4,3,2,1,0:T(8,128)(2,1)}, bf16[8,2,2,32,128]{4,3,2,1,0:T(8,128)(2,1)S(1)}, u32[]{:S(2)}, u32[]{:S(2)}) collective-permute-start(bf16[8,2,2,32,128]{4,3,2,1,0:T(8,128)(2,1)} %get-tuple-element.54), channel_id=1, source_target_pairs={{0,4},{4,0},{8,12},{12,8},{1,5},{5,1},{9,13},{13,9},{2,6},{6,2},{1... | collective-permute-start | bytes 786440 | tf_op jit(solution)/shard_map/ppermute | solution.py:30
  45.0 20.1 %copy-start.1 = (bf16[8,2,2,32,128]{4,3,2,1,0:T(8,128)(2,1)S(1)}, bf16[8,2,2,32,128]{4,3,2,1,0:T(8,128)(2,1)}, u32[]{:S(2)}) copy-start(bf16[8,2,2,32,128]{4,3,2,1,0:T(8,128)(2,1)} %get-tuple-element.63.refs_0_) | copy-start | bytes 786436
  49.8 15.2 %collective-permute-start.11 = (bf16[512,128]{1,0:T(8,128)(2,1)S(1)}, bf16[512,128]{1,0:T(8,128)(2,1)S(1)}, u32[]{:S(2)}, u32[]{:S(2)}) collective-permute-start(bf16[512,128]{1,0:T(8,128)(2,1)S(1)} %get-tuple-element.67.refs_8_), channel_id=1, source_target_pairs={{0,2},{2,0},{1,3},{3,1},{4,6},{6,4},{5,7},{7,5},{8,10},{10,8},{9,1... | collective-permute-start | bytes 393224 | tf_op jit(solution)/shard_map/ppermute | solution.py:30
  65.0 1.6 %collective-permute-start.12 = (bf16[8,2,2,32,128]{4,3,2,1,0:T(8,128)(2,1)S(1)}, bf16[8,2,2,32,128]{4,3,2,1,0:T(8,128)(2,1)S(1)}, u32[]{:S(2)}, u32[]{:S(2)}) collective-permute-start(bf16[8,2,2,32,128]{4,3,2,1,0:T(8,128)(2,1)S(1)} %copy-done.1), channel_id=1, source_target_pairs={{0,1},{1,0},{2,3},{3,2},{4,5},{5,4},{6,7},{7,6},{8,9},{9,8},{10,11... | collective-permute-start | bytes 786440 | tf_op jit(solution)/shard_map/ppermute | solution.py:30
  65.1 1.9 %collective-permute-start.13 = (bf16[8,2,2,32,128]{4,3,2,1,0:T(8,128)(2,1)S(1)}, bf16[8,2,2,32,128]{4,3,2,1,0:T(8,128)(2,1)S(1)}, u32[]{:S(2)}, u32[]{:S(2)}) collective-permute-start(bf16[8,2,2,32,128]{4,3,2,1,0:T(8,128)(2,1)S(1)} %collective-permute-done.4.refs_2_), channel_id=1, source_target_pairs={{0,1},{1,0},{2,3},{3,2},{4,5},{5,4},{6,7},{7,6},{8,9},{9,8},{10,11... | collective-permute-start | bytes 786440 | tf_op jit(solution)/shard_map/ppermute | solution.py:30
  65.6 1.8 %collective-permute-start.14 = (bf16[8,2,2,32,128]{4,3,2,1,0:T(8,128)(2,1)S(1)}, bf16[8,2,2,32,128]{4,3,2,1,0:T(8,128)(2,1)S(1)}, u32[]{:S(2)}, u32[]{:S(2)}) collective-permute-start(bf16[8,2,2,32,128]{4,3,2,1,0:T(8,128)(2,1)S(1)} %collective-permute-done.5.refs_4_), channel_id=1, source_target_pairs={{0,1},{1,0},{2,3},{3,2},{4,5},{5,4},{6,7},{7,6},{8,9},{9,8},{10,11... | collective-permute-start | bytes 786440 | tf_op jit(solution)/shard_map/ppermute | solution.py:30
  65.7 2.1 %collective-permute-start.15 = (bf16[8,2,2,32,128]{4,3,2,1,0:T(8,128)(2,1)S(1)}, bf16[8,2,2,32,128]{4,3,2,1,0:T(8,128)(2,1)S(1)}, u32[]{:S(2)}, u32[]{:S(2)}) collective-permute-start(bf16[8,2,2,32,128]{4,3,2,1,0:T(8,128)(2,1)S(1)} %collective-permute-done.6.refs_6_), channel_id=1, source_target_pairs={{0,1},{1,0},{2,3},{3,2},{4,5},{5,4},{6,7},{7,6},{8,9},{9,8},{10,11... | collective-permute-start | bytes 786440 | tf_op jit(solution)/shard_map/ppermute | solution.py:30

commit v2 on v1

--- a/solution.py
+++ b/solution.py
@@ -50,37 +50,50 @@
     return pl.BlockSpec(memory_space=pltpu.VMEM)
 
 
-def spectra_kernel(first, frames, length, has_rim, *refs):
+def spectra_kernel(first, frames, length, has_rim, emit, *refs):
     me_ref, refs = refs[0], refs[1:]
     rim_hbm, refs = (refs[0], refs[1:]) if has_rim else (None, refs)
     volt_hbm, taps_hbm, dft_hbm = refs[:3]
     outs, (volt, taps_ref, dft_ref, filt, spread, made, sems) = refs[3:-7], refs[-7:]
     taps = taps_ref.shape[0]
-    rows = volt.shape[1]
+    rows = volt.shape[0]
     row_block = spread.shape[1]
     half = row_block // 2
     history = taps - 1
 
-    copies = [pltpu.make_async_copy(taps_hbm, taps_ref, sems.at[0])]
-    for slot in range(history + frames):
-        frame = first + slot - history
-        source, at = (rim_hbm, (frame + history) * length) if frame < 0 else (volt_hbm, frame * length)
-        copies.append(pltpu.make_async_copy(source.at[:, pl.ds(at, length)], volt.at[slot], sems.at[2 + slot]))
+    taps_copy = pltpu.make_async_copy(taps_hbm, taps_ref, sems.at[0])
+    taps_copy.start()
+    early = max(0, history - first)
+    sources = [(volt_hbm, max(0, first - history) * length, early * length, (history + frames - early) * length)]
+    if has_rim:
+        sources.append((rim_hbm, (history - early) * length, 0, early * length))
+    copies = []
+    for block in range(rows // row_block):
+        span = pl.ds(block * row_block, row_block)
+        for n, (source, start, at, size) in enumerate(sources):
+            copies.append(
+                pltpu.make_async_copy(
+                    source.at[span, pl.ds(start, size)],
+                    volt.at[span, pl.ds(at, size)],
+                    sems.at[2 + block * len(sources) + n],
+                )
+            )
+            copies[-1].start()
     table_copy = pltpu.make_async_copy(dft_hbm, dft_ref, sems.at[1])
-    for copy in copies:
-        copy.start()
-    table_copy.start()
-    for copy in copies:
-        copy.wait()
-
-    def columns(n, _):
-        lane = pl.multiple_of(n * LANES, LANES)
-        weights = [taps_ref[t : t + 1, pl.ds(lane, LANES)] for t in range(taps)]
-        for block in range(rows // row_block):
-            row = block * row_block
+    writes = []
+    if emit:
+        *outs, rim_out = outs
+
+    def filtered_block(block):
+        row = block * row_block
+
+        def columns(n, _):
+            lane = pl.multiple_of(n * LANES, LANES)
+            weights = [taps_ref[t : t + 1, pl.ds(lane, LANES)] for t in range(taps)]
 
             def load(slot):
-                return volt[slot, row : row + row_block, pl.ds(lane, LANES)].astype(jnp.float32)
+                at = pl.multiple_of(slot * length + lane, LANES)
+                return volt[row : row + row_block, pl.ds(at, LANES)].astype(jnp.float32)
 
             window = [load(t) for t in range(history)]
             for f in range(frames):
@@ -89,21 +102,33 @@
                 for t in range(1, taps):
                     total = total + weights[t] * window[t]
                 window.pop(0)
-                slot = (block * frames + f) % spread.shape[0]
+                slot = f % spread.shape[0]
                 spread[slot] = total
                 for p in range(2):
                     picked = spread[slot, pl.ds(p, half, stride=2), :]
-                    filt[pl.ds((f * 2 + p) * (rows // 2) + block * half, half), pl.ds(lane, LANES)] = picked.astype(
+                    filt[pl.ds((f * 2 + p) * (rows // 2) + row // 2, half), pl.ds(lane, LANES)] = picked.astype(
                         jnp.bfloat16
                     )
-        return 0
-
-    lax.fori_loop(0, length // LANES, columns, 0)
+            return 0
+
+        lax.fori_loop(0, length // LANES, columns, 0)
+
+    for block in range(rows // row_block):
+        for copy in copies[block * len(sources) : (block + 1) * len(sources)]:
+            copy.wait()
+        if block == 0:
+            taps_copy.wait()
+            table_copy.start()
+        filtered_block(block)
+    if emit:
+        writes.append(
+            pltpu.make_async_copy(volt.at[:, pl.ds(frames * length, history * length)], rim_out, sems.at[2])
+        )
+        writes[-1].start()
     table_copy.wait()
     count = dft_ref.shape[0]
     stations = rows // 2
     channels = outs[0].shape[-1]
-    writes = []
     for d in (*range(1, count), 0):
         block = partner(me_ref[0], d, count)
         result = jnp.dot(filt[...], dft_ref[block], preferred_element_type=jnp.float32).astype(jnp.bfloat16)
@@ -118,7 +143,7 @@
         write.wait()
 
 
-def make_spectra(me, rim, voltages, filter_taps, dft, first, frames):
+def make_spectra(me, rim, voltages, filter_taps, dft, first, frames, emit):
     rows = voltages.shape[0]
     taps, length = filter_taps.shape
     count = dft.shape[0]
@@ -128,18 +153,19 @@
     shape = (frames, 2, 2, rows // 2, channels)
     slots = frames + taps - 1
     return pl.pallas_call(
-        functools.partial(spectra_kernel, first, frames, length, has_rim),
-        out_shape=[jax.ShapeDtypeStruct(shape, jnp.bfloat16)] * count,
+        functools.partial(spectra_kernel, first, frames, length, has_rim, emit),
+        out_shape=[jax.ShapeDtypeStruct(shape, jnp.bfloat16)] * count
+        + [jax.ShapeDtypeStruct((rows, (taps - 1) * length), jnp.bfloat16)] * emit,
         in_specs=[pl.BlockSpec(memory_space=pltpu.SMEM)] + [pl.BlockSpec(memory_space=pl.ANY)] * len(operands),
-        out_specs=[pl.BlockSpec(memory_space=pl.ANY)] * count,
+        out_specs=[pl.BlockSpec(memory_space=pl.ANY)] * (count + emit),
         scratch_shapes=[
-            pltpu.VMEM((slots, rows, length), jnp.bfloat16),
+            pltpu.VMEM((rows, slots * length), jnp.bfloat16),
             pltpu.VMEM((taps, length), jnp.float32),
             pltpu.VMEM(dft.shape, jnp.bfloat16),
             pltpu.VMEM((frames * rows, length), jnp.bfloat16),
             pltpu.VMEM((8, min(rows, ROW_BLOCK), LANES), jnp.float32),
             pltpu.VMEM((count, *shape), jnp.bfloat16),
-            pltpu.SemaphoreType.DMA((slots + 2 + count,)),
+            pltpu.SemaphoreType.DMA((2 * -(-rows // ROW_BLOCK) + 2 + count,)),
         ],
         compiler_params=pltpu.CompilerParams(vmem_limit_bytes=ALL_VMEM_BYTES),
         cost_estimate=pl.CostEstimate(flops=SMALL_COST, bytes_accessed=SMALL_COST, transcendentals=0),
@@ -152,15 +178,15 @@
     beams = mixers_ref.shape[1] // 2
     step = min(frames, max(1, WIDE // channels))
 
-    def group(i, over_frames):
+    def group(first, count, over_frames):
         power = None
         for p in range(2):
             sides = []
-            for side in range(step):
+            for side in range(count):
                 parts = []
                 for piece in spectra:
                     for r in range(2):
-                        parts.append(piece[i * step + side, p, r])
+                        parts.append(piece[first + side, p, r])
                 sides.append(jnp.concatenate(parts, axis=0))
             stacked = jnp.concatenate(sides, axis=1)
             voltage = jnp.dot(mixers_ref[p], stacked, preferred_element_type=jnp.float32)
@@ -168,14 +194,19 @@
             term = real_part * real_part + imag_part * imag_part
             power = term if power is None else power + term
         upper = power.astype(jnp.bfloat16)
-        at = pl.multiple_of(i * step * channels, step * channels)
-        high[:, pl.ds(at, step * channels)] = upper
-        low[:, pl.ds(at, step * channels)] = (power - upper.astype(jnp.float32)).astype(jnp.bfloat16)
-        for side in range(step):
+        at = first * channels if isinstance(first, int) else pl.multiple_of(first * channels, step * channels)
+        high[:, pl.ds(at, count * channels)] = upper
+        low[:, pl.ds(at, count * channels)] = (power - upper.astype(jnp.float32)).astype(jnp.bfloat16)
+        for side in range(count):
             over_frames = over_frames + power[:, side * channels : (side + 1) * channels]
         return over_frames
 
-    return lax.fori_loop(0, frames // step, group, jnp.zeros((beams, channels), jnp.float32))
+    whole = frames // step
+    over_frames = jnp.zeros((beams, channels), jnp.float32)
+    over_frames = lax.fori_loop(0, whole, lambda i, carry: group(i * step, step, carry), over_frames)
+    if frames > whole * step:
+        over_frames = group(whole * step, frames - whole * step, over_frames)
+    return over_frames
 
 
 def placed(high, low, place_ref):
@@ -307,19 +338,21 @@
     me = lax.axis_index("chan").astype(jnp.int32).reshape(1)
     dft = dft_blocks(length, chan_devices)
     history = taps - 1
-    rim = from_previous(voltages[:, (frames_dev - history) * length :], "tm")
-    half = frames_dev // 2
+    half = min(taps - 1, frames_dev // 2)
+    rim = None
     ready = []
     for first, frames in ((half, frames_dev - half), (0, half)):
-        if first < history:
+        emit = rim is None
+        if not emit:
             rim, mixers, place, centre = lax.optimization_barrier((rim, mixers, place, centre))
-        own = list(make_spectra(me, rim if first < history else None, voltages, filter_taps, dft, first, frames))
-        if first >= history:
+        own = make_spectra(me, rim, voltages, filter_taps, dft, first, frames, emit)
+        if emit:
+            *own, rim = own
+            rim = from_previous(rim, "tm")
             late, own[0] = lax.optimization_barrier(((beam_weights, station_index, delay_table), own[0]))
             mixers, place, centre = make_tables(*late, in_dev, frames_dev)
             place = place.reshape(frames_dev * channels, -1)
-        arrived = {d: exchanged(own[d], "chan", d) for d in range(chan_devices - 1, 0, -1)}
-        ready.append([own[0]] + [arrived[d] for d in range(1, chan_devices)])
+        ready.append([own[0]] + [exchanged(own[d], "chan", d) for d in range(1, chan_devices)])
     ready[0], ready[1][0] = lax.optimization_barrier((ready[0], ready[1][0]))
 
     def with_hops(arrived):

time: 84.5 us -> 82.5 us (0.976)
  local copies, waits for them, and re-layouts: 7.93 us -> 5.74 us
  Pallas kernels: 20.7 us -> 21.9 us
  waiting for transfers between devices: 26.5 us -> 25.6 us
    ppermute x15, waiting for transfers between devices: 23.8 us -> 17.2 us  [exchanged(): lax.ppermute(value, axis, [(source, partner(source, step, count)) for sou...]
    ppermute x1, waiting for transfers between devices: 2.74 us -> 8.38 us  [from_previous(): lax.ppermute(value, axis, [(source, source + 1) for source in range(count...]
    slice x1, local copies, waits for them, and re-layouts: 2.18 us -> 0.04 us  [shards(): place[half * channels:]]
    pallas_call x2, Pallas kernels: 8.61 us -> 10.4 us  [beam_call(): pl.pallas_call(kernel, out_shape=out_shape, in_specs=[vmem_spec()] * len(...]
  transfers between devices with their start and end apart: 16 -> 16, of which waited for: 8 -> 7; matrix products, arithmetic and copies ran while one was open for 6% -> 6% of each run, Pallas kernels for 20% -> 15%
where the time goes in v2:
time: 82.5 us; the launch traced here: 82.3 us
  waiting for transfers between devices  25.6 us (31%)
  Pallas kernels  21.9 us (27%)
  starting transfers between devices  16.8 us (20%)
  blocking collectives  12 us (15%)
  local copies, waits for them, and re-layouts  5.74 us (7%)
    ppermute x15, waiting for transfers between devices, exchanged(): lax.ppermute(value, axis, [(source, partner(source, step, count)) for sou...  17.2 us
    all_to_all x1, blocking collectives, shards(): lax.all_to_all(blocks, ('chan', 'tm'), split_axis=0, concat_axis=0, tiled...  12 us
    ppermute x15, starting transfers between devices, exchanged(): lax.ppermute(value, axis, [(source, partner(source, step, count)) for sou...  10.9 us
    pallas_call x2, Pallas kernels, beam_call(): pl.pallas_call(kernel, out_shape=out_shape, in_specs=[vmem_spec()] * len(...  10.4 us
    pallas_call x2, Pallas kernels, make_spectra(): pl.pallas_call(functools.partial(spectra_kernel, first, frames, length, h...  10.4 us
    ppermute x1, waiting for transfers between devices, from_previous(): lax.ppermute(value, axis, [(source, source + 1) for source in range(count...  8.38 us
    ppermute x1, starting transfers between devices, from_previous(): lax.ppermute(value, axis, [(source, source + 1) for source in range(count...  5.83 us
    dynamic_slice x1, local copies, waits for them, and re-layouts, make_tables(): chosen = lax.dynamic_index_in_dim(arranged, core, 3, keepdims=False)  3.27 us
  transfers between devices with their start and end apart: 16, of which 7 were waited for; matrix products, arithmetic and copies ran while one was open for 6% of the time, Pallas kernels for 15%

profile of v2, /device:TPU:0, one launch (start us, length us, event | category | flops | bytes accessed | tf_op | source)
XLA Modules:
  0.0 82.3 jit_solution(5602207455202022617)
XLA Ops:
  0.0 0.0 copy-start.3
  0.0 0.0 copy-start.4
  0.0 0.0 copy-start.2
  0.0 5.5 %spectra_7.1 = (bf16[9,2,2,32,128]{4,3,2,1,0:T(8,128)(2,1)}, bf16[9,2,2,32,128]{4,3,2,1,0:T(8,128)(2,1)}, bf16[9,2,2,32,128]{4,3,2,1,0:T(8,128)(2,1)}, bf16[9,2,...) custom-call(s32[1]{0:T(128)} %bitcast.refs_0_, bf16[64,16384]{1,0:T(8,128)(2,1)} %refs_2_.3, f32[8,1024]{1,0:T(8,128)} %refs_3_.2, ...), custom_call_target="tpu_custom_call" | custom-call | flops 1024 | bytes 1024 | tf_op jit(solution)/shard_map/spectra_7/pallas_call | solution.py:155
  5.5 5.8 %collective-permute-start.3 = (bf16[64,7168]{1,0:T(8,128)(2,1)}, bf16[64,7168]{1,0:T(8,128)(2,1)}, u32[]{:S(2)}, u32[]{:S(2)}) collective-permute-start(bf16[64,7168]{1,0:T(8,128)(2,1)} %get-tuple-element.44), channel_id=1, source_target_pairs={{0,2},{1,3},{4,6},{5,7},{8,10},{9,11},{12,14},{13,15},{16,18},{17,... | collective-permute-start | bytes 2752520 | tf_op jit(solution)/shard_map/ppermute | solution.py:39
  11.4 3.6 %collective-permute-start = (bf16[9,2,2,32,128]{4,3,2,1,0:T(8,128)(2,1)}, bf16[9,2,2,32,128]{4,3,2,1,0:T(8,128)(2,1)S(1)}, u32[]{:S(2)}, u32[]{:S(2)}) collective-permute-start(bf16[9,2,2,32,128]{4,3,2,1,0:T(8,128)(2,1)} %get-tuple-element.41), channel_id=1, source_target_pairs={{0,12},{4,8},{8,4},{12,0},{1,13},{5,9},{9,5},{13,1},{2,14},{6,10},... | collective-permute-start | bytes 884744 | tf_op jit(solution)/shard_map/ppermute | solution.py:30
  15.0 0.0 collective-permute-start.1
  15.0 0.8 collective-permute-start.2
  15.8 0.0 copy-done.3
  15.8 0.1 copy.26.refs_3_
  15.9 0.0 copy-done.4
  15.9 0.1 reshape.96
  16.1 0.1 copy.20
  16.1 0.1 copy.23
  16.2 0.1 copy.22
  16.3 0.1 copy.21
  16.5 0.1 reshape.97
  16.6 0.0 copy-done.2
  16.6 0.7 reshape.98
  17.3 3.3 %dynamic-slice_reduce_fusion = bf16[2,256,4,128]{3,2,0,1:T(4,128)(2,1)S(1)} fusion(bf16[2,256,4,2,128]{4,3,2,0,1:T(2,128)(2,1)S(1)} %reshape.98, s32[]{:T(128)S(6)} %select_n.50), kind=kLoop, calls=%fused_computation | loop fusion | bytes 1048580 | tf_op jit(solution)/shard_map/jit(dynamic_index_in_dim)/dynamic_slice | solution.py:300
  20.6 0.2 reshape.101
  20.8 0.1 copy.29.refs_2_
  20.9 1.1 %tables.1 = (bf16[2,1024,512]{2,1,0:T(8,128)(2,1)S(1)}, bf16[16,128,256]{2,1,0:T(8,128)(2,1)S(1)}, bf16[128,256]{1,0:T(8,128)(2,1)S(1)}) custom-call(s32[1]{0:T(128)} %bitcast.1.refs_0_, s32[3,512]{1,0:T(4,128)S(1)} %pad_add_fusion.1.refs_1_, bf16[2,256,512]{2,1,0:T(8,128)(2,1)S(1)} %copy.29.refs_2_, s32[128,8]{1,0:T(8,128)S(1)} %copy.26.refs_3_), custom_call_target="tpu_custom_call" | custom-call | flops 1024 | bytes 1024 | tf_op jit(solution)/shard_map/tables/pallas_call | solution.py:314
  21.9 8.4 %collective-permute-done.3.refs_1_ = bf16[64,7168]{1,0:T(8,128)(2,1)} collective-permute-done((bf16[64,7168]{1,0:T(8,128)(2,1)}, bf16[64,7168]{1,0:T(8,128)(2,1)}, u32[]{:S(2)}, u32[]{:S(2)}) %collective-permute-start.3) | collective-permute-done | bytes 917536 | tf_op jit(solution)/shard_map/ppermute | solution.py:39
  30.3 0.0 copy-start
  30.3 4.9 %spectra_0.1 = (bf16[7,2,2,32,128]{4,3,2,1,0:T(8,128)(2,1)}, bf16[7,2,2,32,128]{4,3,2,1,0:T(8,128)(2,1)}, bf16[7,2,2,32,128]{4,3,2,1,0:T(8,128)(2,1)}, bf16[7,2,2,32,128]{4,3,2,1,0:T(8,128)(2,1)}) custom-call(s32[1]{0:T(128)} %bitcast.refs_0_, bf16[64,7168]{1,0:T(8,128)(2,1)} %collective-permute-done.3.refs_1_, bf16[64,16384]{1,0:T(8,128)(2,1)} %refs_2_.3, ...), custom_call_target="tpu_custom_call" | custom-call | flops 1024 | bytes 1024 | tf_op jit(solution)/shard_map/spectra_0/pallas_call | solution.py:155
  35.2 0.0 collective-permute-done.refs_2_
  35.2 4.8 %collective-permute-done.1.refs_4_ = bf16[9,2,2,32,128]{4,3,2,1,0:T(8,128)(2,1)S(1)} collective-permute-done((bf16[9,2,2,32,128]{4,3,2,1,0:T(8,128)(2,1)}, bf16[9,2,2,32,128]{4,3,2,1,0:T(8,128)(2,1)S(1)}, u32[]{:S(2)}, u32[]{:S(2)}) %collective-permute-start.1) | collective-permute-done | bytes 294944 | tf_op jit(solution)/shard_map/ppermute | solution.py:30
  40.0 0.0 collective-permute-done.2.refs_6_
  40.0 0.0 copy-done
  40.0 0.0 collective-permute-start.7
  40.0 0.5 collective-permute-start.8
  40.5 0.1 collective-permute-start.9
  40.6 0.4 collective-permute-start.10
  41.1 2.5 %collective-permute-start.4 = (bf16[7,2,2,32,128]{4,3,2,1,0:T(8,128)(2,1)}, bf16[7,2,2,32,128]{4,3,2,1,0:T(8,128)(2,1)S(1)}, u32[]{:S(2)}, u32[]{:S(2)}) collective-permute-start(bf16[7,2,2,32,128]{4,3,2,1,0:T(8,128)(2,1)} %get-tuple-element.54), channel_id=1, source_target_pairs={{0,12},{4,8},{8,4},{12,0},{1,13},{5,9},{9,5},{13,1},{2,14},{6,10},... | collective-permute-start | bytes 688136 | tf_op jit(solution)/shard_map/ppermute | solution.py:30
  43.5 0.0 collective-permute-done.7.refs_1_
  43.5 0.0 collective-permute-start.5
  43.5 0.0 collective-permute-done.8.refs_3_
  43.5 1.9 %collective-permute-start.6 = (bf16[7,2,2,32,128]{4,3,2,1,0:T(8,128)(2,1)}, bf16[7,2,2,32,128]{4,3,2,1,0:T(8,128)(2,1)S(1)}, u32[]{:S(2)}, u32[]{:S(2)}) collective-permute-start(bf16[7,2,2,32,128]{4,3,2,1,0:T(8,128)(2,1)} %get-tuple-element.56), channel_id=1, source_target_pairs={{0,4},{4,0},{8,12},{12,8},{1,5},{5,1},{9,13},{13,9},{2,6},{6,2},{1... | collective-permute-start | bytes 688136 | tf_op jit(solution)/shard_map/ppermute | solution.py:30
  45.5 0.0 copy-start.1
  45.5 0.0 collective-permute-done.9.refs_5_
  45.5 0.0 collective-permute-done.10.refs_7_
  45.5 6.2 %beam_first.1 = (f32[512,256]{1,0:T(8,128)S(1)}, bf16[512,128]{1,0:T(8,128)(2,1)S(1)}) custom-call(bf16[9,2,2,32,128]{4,3,2,1,0:T(8,128)(2,1)S(1)} %copy-done, bf16[9,2,2,32,128]{4,3,2,1,0:T(8,128)(2,1)S(1)} %collective-permute-done.7.refs_1_, bf16[9,2,2,32,128]{4,3,2,1,0:T(8,128)(2,1)S(1)} %collective-permute-done.refs_2_, ...), custom_call_target="tpu_custom_call" | custom-call | flops 1024 | bytes 1024 | tf_op jit(solution)/shard_map/beam_first/pallas_call | solution.py:245
  51.8 0.1 collective-permute-start.11
  51.8 0.0 collective-permute-done.4.refs_2_
  51.8 11.0 %collective-permute-done.5.refs_4_ = bf16[7,2,2,32,128]{4,3,2,1,0:T(8,128)(2,1)S(1)} collective-permute-done((bf16[7,2,2,32,128]{4,3,2,1,0:T(8,128)(2,1)}, bf16[7,2,2,32,128]{4,3,2,1,0:T(8,128)(2,1)S(1)}, u32[]{:S(2)}, u32[]{:S(2)}) %collective-permute-start.5) | collective-permute-done | bytes 229408 | tf_op jit(solution)/shard_map/ppermute | solution.py:30
  62.8 0.0 collective-permute-done.6.refs_6_
  62.8 0.0 collective-permute-done.11.refs_9_
  62.8 0.0 copy-done.1
  62.8 0.1 collective-permute-start.12
  62.9 0.5 collective-permute-start.13
  63.4 0.1 collective-permute-start.14
  63.5 0.4 collective-permute-start.15
  63.9 0.4 collective-permute-done.12.refs_1_
  64.4 0.3 collective-permute-done.13.refs_3_
  64.7 0.3 collective-permute-done.14.refs_5_
  65.0 0.3 collective-permute-done.15.refs_7_
  65.3 4.2 %beam_last.1 = bf16[8,128,128]{2,1,0:T(8,128)(2,1)S(1)} custom-call(bf16[7,2,2,32,128]{4,3,2,1,0:T(8,128)(2,1)S(1)} %copy-done.1, bf16[7,2,2,32,128]{4,3,2,1,0:T(8,128)(2,1)S(1)} %collective-permute-done.12.refs_1_, bf16[7,2,2,32,128]{4,3,2,1,0:T(8,128)(2,1)S(1)} %collective-permute-done.4.refs_2_, ...), custom_call_target="tpu_custom_call" | custom-call | flops 1024 | bytes 1024 | tf_op jit(solution)/shard_map/beam_last/pallas_call | solution.py:245
  69.5 12.0 %all_to_all.5 = bf16[8,128,128]{2,1,0:T(8,128)(2,1)S(1)} all-to-all(bf16[8,128,128]{2,1,0:T(8,128)(2,1)S(1)} %beam_last.1), channel_id=1, replica_groups=mesh['groups'=2,'chan'=4,'tm'=2,'beam'=2] {'chan','tm'}, dimensions={0} | all-to-all | bytes 524288 | tf_op jit(solution)/shard_map/all_to_all | solution.py:396
  81.6 0.7 copy.27
  (12 shorter events, 0.2 us)
Async XLA Ops:
  0.0 15.8 %copy-start.3 = (s32[128,8]{0,1:T(8,128)S(1)}, s32[128,8]{0,1:T(8,128)}, u32[]{:S(2)}) copy-start(s32[128,8]{0,1:T(8,128)} %param.10) | copy-start | bytes 12292
  0.0 15.9 %copy-start.4 = (s32[512]{0:T(512)S(1)}, s32[512]{0:T(512)}, u32[]{:S(2)}) copy-start(s32[512]{0:T(512)} %param.9) | copy-start | bytes 6148
  0.0 16.6 %copy-start.2 = (bf16[256,2,1024]{2,1,0:T(2,128)(2,1)S(1)}, bf16[256,2,1024]{2,1,0:T(2,128)(2,1)}, u32[]{:S(2)}) copy-start(bf16[256,2,1024]{2,1,0:T(2,128)(2,1)} %param.8) | copy-start | bytes 3145732
  5.5 24.8 %collective-permute-start.3 = (bf16[64,7168]{1,0:T(8,128)(2,1)}, bf16[64,7168]{1,0:T(8,128)(2,1)}, u32[]{:S(2)}, u32[]{:S(2)}) collective-permute-start(bf16[64,7168]{1,0:T(8,128)(2,1)} %get-tuple-element.44), channel_id=1, source_target_pairs={{0,2},{1,3},{4,6},{5,7},{8,10},{9,11},{12,14},{13,15},{16,18},{17,... | collective-permute-start | bytes 2752520 | tf_op jit(solution)/shard_map/ppermute | solution.py:39
  11.4 23.8 %collective-permute-start = (bf16[9,2,2,32,128]{4,3,2,1,0:T(8,128)(2,1)}, bf16[9,2,2,32,128]{4,3,2,1,0:T(8,128)(2,1)S(1)}, u32[]{:S(2)}, u32[]{:S(2)}) collective-permute-start(bf16[9,2,2,32,128]{4,3,2,1,0:T(8,128)(2,1)} %get-tuple-element.41), channel_id=1, source_target_pairs={{0,12},{4,8},{8,4},{12,0},{1,13},{5,9},{9,5},{13,1},{2,14},{6,10},... | collective-permute-start | bytes 884744 | tf_op jit(solution)/shard_map/ppermute | solution.py:30
  15.0 25.0 %collective-permute-start.1 = (bf16[9,2,2,32,128]{4,3,2,1,0:T(8,128)(2,1)}, bf16[9,2,2,32,128]{4,3,2,1,0:T(8,128)(2,1)S(1)}, u32[]{:S(2)}, u32[]{:S(2)}) collective-permute-start(bf16[9,2,2,32,128]{4,3,2,1,0:T(8,128)(2,1)} %get-tuple-element.42), channel_id=1, source_target_pairs={{0,8},{4,12},{8,0},{12,4},{1,9},{5,13},{9,1},{13,5},{2,10},{6,14},... | collective-permute-start | bytes 884744 | tf_op jit(solution)/shard_map/ppermute | solution.py:30
  15.0 25.0 %collective-permute-start.2 = (bf16[9,2,2,32,128]{4,3,2,1,0:T(8,128)(2,1)}, bf16[9,2,2,32,128]{4,3,2,1,0:T(8,128)(2,1)}, u32[]{:S(2)}, u32[]{:S(2)}) collective-permute-start(bf16[9,2,2,32,128]{4,3,2,1,0:T(8,128)(2,1)} %get-tuple-element.43), channel_id=1, source_target_pairs={{0,4},{4,0},{8,12},{12,8},{1,5},{5,1},{9,13},{13,9},{2,6},{6,2},{1... | collective-permute-start | bytes 884744 | tf_op jit(solution)/shard_map/ppermute | solution.py:30
  30.3 9.7 %copy-start = (bf16[9,2,2,32,128]{4,3,2,1,0:T(8,128)(2,1)S(1)}, bf16[9,2,2,32,128]{4,3,2,1,0:T(8,128)(2,1)}, u32[]{:S(2)}) copy-start(bf16[9,2,2,32,128]{4,3,2,1,0:T(8,128)(2,1)} %get-tuple-element.57.refs_0_) | copy-start | bytes 884740
  40.0 3.5 %collective-permute-start.7 = (bf16[9,2,2,32,128]{4,3,2,1,0:T(8,128)(2,1)S(1)}, bf16[9,2,2,32,128]{4,3,2,1,0:T(8,128)(2,1)S(1)}, u32[]{:S(2)}, u32[]{:S(2)}) collective-permute-start(bf16[9,2,2,32,128]{4,3,2,1,0:T(8,128)(2,1)S(1)} %copy-done), channel_id=1, source_target_pairs={{0,1},{1,0},{2,3},{3,2},{4,5},{5,4},{6,7},{7,6},{8,9},{9,8},{10,11... | collective-permute-start | bytes 884744 | tf_op jit(solution)/shard_map/ppermute | solution.py:30
  40.0 3.5 %collective-permute-start.8 = (bf16[9,2,2,32,128]{4,3,2,1,0:T(8,128)(2,1)S(1)}, bf16[9,2,2,32,128]{4,3,2,1,0:T(8,128)(2,1)S(1)}, u32[]{:S(2)}, u32[]{:S(2)}) collective-permute-start(bf16[9,2,2,32,128]{4,3,2,1,0:T(8,128)(2,1)S(1)} %collective-permute-done.refs_2_), channel_id=1, source_target_pairs={{0,1},{1,0},{2,3},{3,2},{4,5},{5,4},{6,7},{7,6},{8,9},{9,8},{10,11... | collective-permute-start | bytes 884744 | tf_op jit(solution)/shard_map/ppermute | solution.py:30
  40.5 5.0 %collective-permute-start.9 = (bf16[9,2,2,32,128]{4,3,2,1,0:T(8,128)(2,1)S(1)}, bf16[9,2,2,32,128]{4,3,2,1,0:T(8,128)(2,1)S(1)}, u32[]{:S(2)}, u32[]{:S(2)}) collective-permute-start(bf16[9,2,2,32,128]{4,3,2,1,0:T(8,128)(2,1)S(1)} %collective-permute-done.1.refs_4_), channel_id=1, source_target_pairs={{0,1},{1,0},{2,3},{3,2},{4,5},{5,4},{6,7},{7,6},{8,9},{9,8},{10,11... | collective-permute-start | bytes 884744 | tf_op jit(solution)/shard_map/ppermute | solution.py:30
  40.6 4.9 %collective-permute-start.10 = (bf16[9,2,2,32,128]{4,3,2,1,0:T(8,128)(2,1)}, bf16[9,2,2,32,128]{4,3,2,1,0:T(8,128)(2,1)S(1)}, u32[]{:S(2)}, u32[]{:S(2)}) collective-permute-start(bf16[9,2,2,32,128]{4,3,2,1,0:T(8,128)(2,1)} %collective-permute-done.2.refs_6_), channel_id=1, source_target_pairs={{0,1},{1,0},{2,3},{3,2},{4,5},{5,4},{6,7},{7,6},{8,9},{9,8},{10,11... | collective-permute-start | bytes 884744 | tf_op jit(solution)/shard_map/ppermute | solution.py:30
  41.1 10.8 %collective-permute-start.4 = (bf16[7,2,2,32,128]{4,3,2,1,0:T(8,128)(2,1)}, bf16[7,2,2,32,128]{4,3,2,1,0:T(8,128)(2,1)S(1)}, u32[]{:S(2)}, u32[]{:S(2)}) collective-permute-start(bf16[7,2,2,32,128]{4,3,2,1,0:T(8,128)(2,1)} %get-tuple-element.54), channel_id=1, source_target_pairs={{0,12},{4,8},{8,4},{12,0},{1,13},{5,9},{9,5},{13,1},{2,14},{6,10},... | collective-permute-start | bytes 688136 | tf_op jit(solution)/shard_map/ppermute | solution.py:30
  43.5 19.3 %collective-permute-start.5 = (bf16[7,2,2,32,128]{4,3,2,1,0:T(8,128)(2,1)}, bf16[7,2,2,32,128]{4,3,2,1,0:T(8,128)(2,1)S(1)}, u32[]{:S(2)}, u32[]{:S(2)}) collective-permute-start(bf16[7,2,2,32,128]{4,3,2,1,0:T(8,128)(2,1)} %get-tuple-element.55), channel_id=1, source_target_pairs={{0,8},{4,12},{8,0},{12,4},{1,9},{5,13},{9,1},{13,5},{2,10},{6,14},... | collective-permute-start | bytes 688136 | tf_op jit(solution)/shard_map/ppermute | solution.py:30
  43.5 19.3 %collective-permute-start.6 = (bf16[7,2,2,32,128]{4,3,2,1,0:T(8,128)(2,1)}, bf16[7,2,2,32,128]{4,3,2,1,0:T(8,128)(2,1)S(1)}, u32[]{:S(2)}, u32[]{:S(2)}) collective-permute-start(bf16[7,2,2,32,128]{4,3,2,1,0:T(8,128)(2,1)} %get-tuple-element.56), channel_id=1, source_target_pairs={{0,4},{4,0},{8,12},{12,8},{1,5},{5,1},{9,13},{13,9},{2,6},{6,2},{1... | collective-permute-start | bytes 688136 | tf_op jit(solution)/shard_map/ppermute | solution.py:30
  45.5 17.3 %copy-start.1 = (bf16[7,2,2,32,128]{4,3,2,1,0:T(8,128)(2,1)S(1)}, bf16[7,2,2,32,128]{4,3,2,1,0:T(8,128)(2,1)}, u32[]{:S(2)}) copy-start(bf16[7,2,2,32,128]{4,3,2,1,0:T(8,128)(2,1)} %get-tuple-element.65.refs_0_) | copy-start | bytes 688132
  51.8 11.0 %collective-permute-start.11 = (bf16[512,128]{1,0:T(8,128)(2,1)S(1)}, bf16[512,128]{1,0:T(8,128)(2,1)S(1)}, u32[]{:S(2)}, u32[]{:S(2)}) collective-permute-start(bf16[512,128]{1,0:T(8,128)(2,1)S(1)} %get-tuple-element.69.refs_8_), channel_id=1, source_target_pairs={{0,2},{2,0},{1,3},{3,1},{4,6},{6,4},{5,7},{7,5},{8,10},{10,8},{9,1... | collective-permute-start | bytes 393224 | tf_op jit(solution)/shard_map/ppermute | solution.py:30
  62.8 1.6 %collective-permute-start.12 = (bf16[7,2,2,32,128]{4,3,2,1,0:T(8,128)(2,1)S(1)}, bf16[7,2,2,32,128]{4,3,2,1,0:T(8,128)(2,1)S(1)}, u32[]{:S(2)}, u32[]{:S(2)}) collective-permute-start(bf16[7,2,2,32,128]{4,3,2,1,0:T(8,128)(2,1)S(1)} %copy-done.1), channel_id=1, source_target_pairs={{0,1},{1,0},{2,3},{3,2},{4,5},{5,4},{6,7},{7,6},{8,9},{9,8},{10,11... | collective-permute-start | bytes 688136 | tf_op jit(solution)/shard_map/ppermute | solution.py:30
  62.9 1.8 %collective-permute-start.13 = (bf16[7,2,2,32,128]{4,3,2,1,0:T(8,128)(2,1)S(1)}, bf16[7,2,2,32,128]{4,3,2,1,0:T(8,128)(2,1)S(1)}, u32[]{:S(2)}, u32[]{:S(2)}) collective-permute-start(bf16[7,2,2,32,128]{4,3,2,1,0:T(8,128)(2,1)S(1)} %collective-permute-done.4.refs_2_), channel_id=1, source_target_pairs={{0,1},{1,0},{2,3},{3,2},{4,5},{5,4},{6,7},{7,6},{8,9},{9,8},{10,11... | collective-permute-start | bytes 688136 | tf_op jit(solution)/shard_map/ppermute | solution.py:30
  63.4 1.6 %collective-permute-start.14 = (bf16[7,2,2,32,128]{4,3,2,1,0:T(8,128)(2,1)S(1)}, bf16[7,2,2,32,128]{4,3,2,1,0:T(8,128)(2,1)S(1)}, u32[]{:S(2)}, u32[]{:S(2)}) collective-permute-start(bf16[7,2,2,32,128]{4,3,2,1,0:T(8,128)(2,1)S(1)} %collective-permute-done.5.refs_4_), channel_id=1, source_target_pairs={{0,1},{1,0},{2,3},{3,2},{4,5},{5,4},{6,7},{7,6},{8,9},{9,8},{10,11... | collective-permute-start | bytes 688136 | tf_op jit(solution)/shard_map/ppermute | solution.py:30
  63.5 1.9 %collective-permute-start.15 = (bf16[7,2,2,32,128]{4,3,2,1,0:T(8,128)(2,1)S(1)}, bf16[7,2,2,32,128]{4,3,2,1,0:T(8,128)(2,1)S(1)}, u32[]{:S(2)}, u32[]{:S(2)}) collective-permute-start(bf16[7,2,2,32,128]{4,3,2,1,0:T(8,128)(2,1)S(1)} %collective-permute-done.6.refs_6_), channel_id=1, source_target_pairs={{0,1},{1,0},{2,3},{3,2},{4,5},{5,4},{6,7},{7,6},{8,9},{9,8},{10,11... | collective-permute-start | bytes 688136 | tf_op jit(solution)/shard_map/ppermute | solution.py:30

commit v3 on v2

--- a/solution.py
+++ b/solution.py
@@ -203,7 +203,8 @@
 
     whole = frames // step
     over_frames = jnp.zeros((beams, channels), jnp.float32)
-    over_frames = lax.fori_loop(0, whole, lambda i, carry: group(i * step, step, carry), over_frames)
+    for i in range(whole):
+        over_frames = group(i * step, step, over_frames)
     if frames > whole * step:
         over_frames = group(whole * step, frames - whole * step, over_frames)
     return over_frames
@@ -231,11 +232,11 @@
     level = (level * level_scale).astype(jnp.bfloat16)
     total = earlier_ref[...] - jnp.dot(level, centre_ref[...], preferred_element_type=jnp.float32)
     total = total + placed(high, low, place_ref)
-    blocks, share, width = out.shape
+    blocks, width, share = out.shape
     groups = total.shape[1] // width
     for block in range(blocks):
         row, column = block // groups * share, block % groups * width
-        out[block] = total[row : row + share, column : column + width].astype(jnp.bfloat16)
+        out[block] = total[row : row + share, column : column + width].T.astype(jnp.bfloat16)
 
 
 def beam_call(kernel, name, out_shape, spectra, mixers, *rest):
@@ -384,7 +385,7 @@
     blocks = beam_call(
         functools.partial(last_kernel, len(spectra), len(levels), level_scale),
         "beam_last",
-        jax.ShapeDtypeStruct((chan_devices * time_devices, share, curves * frames_dev), jnp.bfloat16),
+        jax.ShapeDtypeStruct((chan_devices * time_devices, curves * frames_dev, share), jnp.bfloat16),
         spectra,
         mixers,
         *levels,
@@ -395,7 +396,8 @@
     )
     blocks = lax.all_to_all(blocks, ("chan", "tm"), split_axis=0, concat_axis=0, tiled=True)
     final = jnp.sum(blocks.astype(jnp.float32), axis=0)
-    return (final * (1.0 / math.sqrt(length // 2))).reshape(share, curves, frames_dev)
+    final = final * (1.0 / math.sqrt(length // 2))
+    return jnp.transpose(final.reshape(curves, frames_dev, share), (2, 0, 1))
 
 
 def solution(mesh):

time: 82.5 us -> 81.8 us (level)
  Pallas kernels: 21.9 us -> 20.6 us
    pallas_call x2, Pallas kernels: 10.4 us -> 9.08 us  [beam_call(): pl.pallas_call(kernel, out_shape=out_shape, in_specs=[vmem_spec()] * len(...]
  transfers between devices with their start and end apart: 16 -> 16, of which waited for: 7 -> 8; matrix products, arithmetic and copies ran while one was open for 6% -> 6% of each run, Pallas kernels for 15% -> 14%
where the time goes in v3:
time: 81.8 us; the launch traced here: 81.6 us
  waiting for transfers between devices  26.3 us (32%)
  Pallas kernels  20.6 us (25%)
  starting transfers between devices  16.8 us (21%)
  blocking collectives  12 us (15%)
  local copies, waits for them, and re-layouts  5.01 us (6%)
    ppermute x15, waiting for transfers between devices, exchanged(): lax.ppermute(value, axis, [(source, partner(source, step, count)) for sou...  18 us
    all_to_all x1, blocking collectives, shards(): lax.all_to_all(blocks, ('chan', 'tm'), split_axis=0, concat_axis=0, tiled...  12 us
    ppermute x15, starting transfers between devices, exchanged(): lax.ppermute(value, axis, [(source, partner(source, step, count)) for sou...  10.9 us
    pallas_call x2, Pallas kernels, make_spectra(): pl.pallas_call(functools.partial(spectra_kernel, first, frames, length, h...  10.4 us
    pallas_call x2, Pallas kernels, beam_call(): pl.pallas_call(kernel, out_shape=out_shape, in_specs=[vmem_spec()] * len(...  9.08 us
    ppermute x1, waiting for transfers between devices, from_previous(): lax.ppermute(value, axis, [(source, source + 1) for source in range(count...  8.37 us
    ppermute x1, starting transfers between devices, from_previous(): lax.ppermute(value, axis, [(source, source + 1) for source in range(count...  5.84 us
    dynamic_slice x1, local copies, waits for them, and re-layouts, make_tables(): chosen = lax.dynamic_index_in_dim(arranged, core, 3, keepdims=False)  3.27 us
  transfers between devices with their start and end apart: 16, of which 8 were waited for; matrix products, arithmetic and copies ran while one was open for 6% of the time, Pallas kernels for 14%

profile of v3, /device:TPU:0, one launch (start us, length us, event | category | flops | bytes accessed | tf_op | source)
XLA Modules:
  0.0 81.6 jit_solution(14798001869578658041)
XLA Ops:
  0.0 0.0 copy-start.3
  0.0 0.0 copy-start.4
  0.0 0.0 copy-start.2
  0.0 5.5 %spectra_7.1 = (bf16[9,2,2,32,128]{4,3,2,1,0:T(8,128)(2,1)}, bf16[9,2,2,32,128]{4,3,2,1,0:T(8,128)(2,1)}, bf16[9,2,2,32,128]{4,3,2,1,0:T(8,128)(2,1)}, bf16[9,2,...) custom-call(s32[1]{0:T(128)} %bitcast.refs_0_, bf16[64,16384]{1,0:T(8,128)(2,1)} %refs_2_.3, f32[8,1024]{1,0:T(8,128)} %refs_3_.2, ...), custom_call_target="tpu_custom_call" | custom-call | flops 1024 | bytes 1024 | tf_op jit(solution)/shard_map/spectra_7/pallas_call | solution.py:155
  5.5 5.8 %collective-permute-start.3 = (bf16[64,7168]{1,0:T(8,128)(2,1)}, bf16[64,7168]{1,0:T(8,128)(2,1)}, u32[]{:S(2)}, u32[]{:S(2)}) collective-permute-start(bf16[64,7168]{1,0:T(8,128)(2,1)} %get-tuple-element.44), channel_id=1, source_target_pairs={{0,2},{1,3},{4,6},{5,7},{8,10},{9,11},{12,14},{13,15},{16,18},{17,... | collective-permute-start | bytes 2752520 | tf_op jit(solution)/shard_map/ppermute | solution.py:39
  11.4 3.6 %collective-permute-start = (bf16[9,2,2,32,128]{4,3,2,1,0:T(8,128)(2,1)}, bf16[9,2,2,32,128]{4,3,2,1,0:T(8,128)(2,1)S(1)}, u32[]{:S(2)}, u32[]{:S(2)}) collective-permute-start(bf16[9,2,2,32,128]{4,3,2,1,0:T(8,128)(2,1)} %get-tuple-element.41), channel_id=1, source_target_pairs={{0,12},{4,8},{8,4},{12,0},{1,13},{5,9},{9,5},{13,1},{2,14},{6,10},... | collective-permute-start | bytes 884744 | tf_op jit(solution)/shard_map/ppermute | solution.py:30
  15.0 0.0 collective-permute-start.1
  15.0 0.8 collective-permute-start.2
  15.8 0.0 copy-done.3
  15.8 0.1 copy.18.refs_3_
  15.9 0.0 copy-done.4
  15.9 0.1 reshape.96
  16.1 0.1 copy.12
  16.1 0.1 copy.15
  16.2 0.1 copy.14
  16.3 0.1 copy.13
  16.5 0.1 reshape.97
  16.6 0.0 copy-done.2
  16.6 0.7 reshape.98
  17.3 3.3 %dynamic-slice_reduce_fusion = bf16[2,256,4,128]{3,2,0,1:T(4,128)(2,1)S(1)} fusion(bf16[2,256,4,2,128]{4,3,2,0,1:T(2,128)(2,1)S(1)} %reshape.98, s32[]{:T(128)S(6)} %select_n.50), kind=kLoop, calls=%fused_computation | loop fusion | bytes 1048580 | tf_op jit(solution)/shard_map/jit(dynamic_index_in_dim)/dynamic_slice | solution.py:301
  20.6 0.2 reshape.101
  20.8 0.1 copy.20.refs_2_
  20.9 1.1 %tables.1 = (bf16[2,1024,512]{2,1,0:T(8,128)(2,1)S(1)}, bf16[16,128,256]{2,1,0:T(8,128)(2,1)S(1)}, bf16[128,256]{1,0:T(8,128)(2,1)S(1)}) custom-call(s32[1]{0:T(128)} %bitcast.1.refs_0_, s32[3,512]{1,0:T(4,128)S(1)} %pad_add_fusion.1.refs_1_, bf16[2,256,512]{2,1,0:T(8,128)(2,1)S(1)} %copy.20.refs_2_, s32[128,8]{1,0:T(8,128)S(1)} %copy.18.refs_3_), custom_call_target="tpu_custom_call" | custom-call | flops 1024 | bytes 1024 | tf_op jit(solution)/shard_map/tables/pallas_call | solution.py:315
  21.9 8.4 %collective-permute-done.3.refs_1_ = bf16[64,7168]{1,0:T(8,128)(2,1)} collective-permute-done((bf16[64,7168]{1,0:T(8,128)(2,1)}, bf16[64,7168]{1,0:T(8,128)(2,1)}, u32[]{:S(2)}, u32[]{:S(2)}) %collective-permute-start.3) | collective-permute-done | bytes 917536 | tf_op jit(solution)/shard_map/ppermute | solution.py:39
  30.3 0.0 copy-start
  30.3 4.9 %spectra_0.1 = (bf16[7,2,2,32,128]{4,3,2,1,0:T(8,128)(2,1)}, bf16[7,2,2,32,128]{4,3,2,1,0:T(8,128)(2,1)}, bf16[7,2,2,32,128]{4,3,2,1,0:T(8,128)(2,1)}, bf16[7,2,2,32,128]{4,3,2,1,0:T(8,128)(2,1)}) custom-call(s32[1]{0:T(128)} %bitcast.refs_0_, bf16[64,7168]{1,0:T(8,128)(2,1)} %collective-permute-done.3.refs_1_, bf16[64,16384]{1,0:T(8,128)(2,1)} %refs_2_.3, ...), custom_call_target="tpu_custom_call" | custom-call | flops 1024 | bytes 1024 | tf_op jit(solution)/shard_map/spectra_0/pallas_call | solution.py:155
  35.2 0.0 collective-permute-done.refs_2_
  35.2 4.8 %collective-permute-done.1.refs_4_ = bf16[9,2,2,32,128]{4,3,2,1,0:T(8,128)(2,1)S(1)} collective-permute-done((bf16[9,2,2,32,128]{4,3,2,1,0:T(8,128)(2,1)}, bf16[9,2,2,32,128]{4,3,2,1,0:T(8,128)(2,1)S(1)}, u32[]{:S(2)}, u32[]{:S(2)}) %collective-permute-start.1) | collective-permute-done | bytes 294944 | tf_op jit(solution)/shard_map/ppermute | solution.py:30
  40.0 0.0 collective-permute-done.2.refs_6_
  40.0 0.0 copy-done
  40.0 0.0 collective-permute-start.7
  40.0 0.5 collective-permute-start.8
  40.5 0.1 collective-permute-start.9
  40.6 0.4 collective-permute-start.10
  41.1 2.5 %collective-permute-start.4 = (bf16[7,2,2,32,128]{4,3,2,1,0:T(8,128)(2,1)}, bf16[7,2,2,32,128]{4,3,2,1,0:T(8,128)(2,1)S(1)}, u32[]{:S(2)}, u32[]{:S(2)}) collective-permute-start(bf16[7,2,2,32,128]{4,3,2,1,0:T(8,128)(2,1)} %get-tuple-element.54), channel_id=1, source_target_pairs={{0,12},{4,8},{8,4},{12,0},{1,13},{5,9},{9,5},{13,1},{2,14},{6,10},... | collective-permute-start | bytes 688136 | tf_op jit(solution)/shard_map/ppermute | solution.py:30
  43.5 0.0 collective-permute-done.7.refs_1_
  43.5 0.0 collective-permute-start.5
  43.5 0.0 collective-permute-done.8.refs_3_
  43.5 1.9 %collective-permute-start.6 = (bf16[7,2,2,32,128]{4,3,2,1,0:T(8,128)(2,1)}, bf16[7,2,2,32,128]{4,3,2,1,0:T(8,128)(2,1)S(1)}, u32[]{:S(2)}, u32[]{:S(2)}) collective-permute-start(bf16[7,2,2,32,128]{4,3,2,1,0:T(8,128)(2,1)} %get-tuple-element.56), channel_id=1, source_target_pairs={{0,4},{4,0},{8,12},{12,8},{1,5},{5,1},{9,13},{13,9},{2,6},{6,2},{1... | collective-permute-start | bytes 688136 | tf_op jit(solution)/shard_map/ppermute | solution.py:30
  45.5 0.0 copy-start.1
  45.5 0.0 collective-permute-done.9.refs_5_
  45.5 0.0 collective-permute-done.10.refs_7_
  45.5 5.5 %beam_first.1 = (f32[512,256]{1,0:T(8,128)S(1)}, bf16[512,128]{1,0:T(8,128)(2,1)S(1)}) custom-call(bf16[9,2,2,32,128]{4,3,2,1,0:T(8,128)(2,1)S(1)} %copy-done, bf16[9,2,2,32,128]{4,3,2,1,0:T(8,128)(2,1)S(1)} %collective-permute-done.7.refs_1_, bf16[9,2,2,32,128]{4,3,2,1,0:T(8,128)(2,1)S(1)} %collective-permute-done.refs_2_, ...), custom_call_target="tpu_custom_call" | custom-call | flops 1024 | bytes 1024 | tf_op jit(solution)/shard_map/beam_first/pallas_call | solution.py:246
  51.0 0.1 collective-permute-start.11
  51.1 0.6 collective-permute-done.4.refs_2_
  51.7 11.1 %collective-permute-done.5.refs_4_ = bf16[7,2,2,32,128]{4,3,2,1,0:T(8,128)(2,1)S(1)} collective-permute-done((bf16[7,2,2,32,128]{4,3,2,1,0:T(8,128)(2,1)}, bf16[7,2,2,32,128]{4,3,2,1,0:T(8,128)(2,1)S(1)}, u32[]{:S(2)}, u32[]{:S(2)}) %collective-permute-start.5) | collective-permute-done | bytes 229408 | tf_op jit(solution)/shard_map/ppermute | solution.py:30
  62.8 0.0 collective-permute-done.6.refs_6_
  62.8 0.0 collective-permute-done.11.refs_9_
  62.8 0.0 copy-done.1
  62.8 0.1 collective-permute-start.12
  62.9 0.5 collective-permute-start.13
  63.4 0.1 collective-permute-start.14
  63.5 0.4 collective-permute-start.15
  63.9 0.4 collective-permute-done.12.refs_1_
  64.4 0.3 collective-permute-done.13.refs_3_
  64.7 0.3 collective-permute-done.14.refs_5_
  65.0 0.3 collective-permute-done.15.refs_7_
  65.3 3.6 %beam_last.1 = bf16[8,128,128]{2,1,0:T(8,128)(2,1)S(1)} custom-call(bf16[7,2,2,32,128]{4,3,2,1,0:T(8,128)(2,1)S(1)} %copy-done.1, bf16[7,2,2,32,128]{4,3,2,1,0:T(8,128)(2,1)S(1)} %collective-permute-done.12.refs_1_, bf16[7,2,2,32,128]{4,3,2,1,0:T(8,128)(2,1)S(1)} %collective-permute-done.4.refs_2_, ...), custom_call_target="tpu_custom_call" | custom-call | flops 1024 | bytes 1024 | tf_op jit(solution)/shard_map/beam_last/pallas_call | solution.py:246
  69.0 12.0 %all_to_all.5 = bf16[8,128,128]{2,1,0:T(8,128)(2,1)S(1)} all-to-all(bf16[8,128,128]{2,1,0:T(8,128)(2,1)S(1)} %beam_last.1), channel_id=1, replica_groups=mesh['groups'=2,'chan'=4,'tm'=2,'beam'=2] {'chan','tm'}, dimensions={0} | all-to-all | bytes 524288 | tf_op jit(solution)/shard_map/all_to_all | solution.py:397
  81.0 0.6 broadcast_multiply_fusion
  (11 shorter events, 0.2 us)
Async XLA Ops:
  0.0 15.8 %copy-start.3 = (s32[128,8]{0,1:T(8,128)S(1)}, s32[128,8]{0,1:T(8,128)}, u32[]{:S(2)}) copy-start(s32[128,8]{0,1:T(8,128)} %param.10) | copy-start | bytes 12292
  0.0 15.9 %copy-start.4 = (s32[512]{0:T(512)S(1)}, s32[512]{0:T(512)}, u32[]{:S(2)}) copy-start(s32[512]{0:T(512)} %param.9) | copy-start | bytes 6148
  0.0 16.6 %copy-start.2 = (bf16[256,2,1024]{2,1,0:T(2,128)(2,1)S(1)}, bf16[256,2,1024]{2,1,0:T(2,128)(2,1)}, u32[]{:S(2)}) copy-start(bf16[256,2,1024]{2,1,0:T(2,128)(2,1)} %param.8) | copy-start | bytes 3145732
  5.5 24.8 %collective-permute-start.3 = (bf16[64,7168]{1,0:T(8,128)(2,1)}, bf16[64,7168]{1,0:T(8,128)(2,1)}, u32[]{:S(2)}, u32[]{:S(2)}) collective-permute-start(bf16[64,7168]{1,0:T(8,128)(2,1)} %get-tuple-element.44), channel_id=1, source_target_pairs={{0,2},{1,3},{4,6},{5,7},{8,10},{9,11},{12,14},{13,15},{16,18},{17,... | collective-permute-start | bytes 2752520 | tf_op jit(solution)/shard_map/ppermute | solution.py:39
  11.4 23.8 %collective-permute-start = (bf16[9,2,2,32,128]{4,3,2,1,0:T(8,128)(2,1)}, bf16[9,2,2,32,128]{4,3,2,1,0:T(8,128)(2,1)S(1)}, u32[]{:S(2)}, u32[]{:S(2)}) collective-permute-start(bf16[9,2,2,32,128]{4,3,2,1,0:T(8,128)(2,1)} %get-tuple-element.41), channel_id=1, source_target_pairs={{0,12},{4,8},{8,4},{12,0},{1,13},{5,9},{9,5},{13,1},{2,14},{6,10},... | collective-permute-start | bytes 884744 | tf_op jit(solution)/shard_map/ppermute | solution.py:30
  15.0 25.0 %collective-permute-start.1 = (bf16[9,2,2,32,128]{4,3,2,1,0:T(8,128)(2,1)}, bf16[9,2,2,32,128]{4,3,2,1,0:T(8,128)(2,1)S(1)}, u32[]{:S(2)}, u32[]{:S(2)}) collective-permute-start(bf16[9,2,2,32,128]{4,3,2,1,0:T(8,128)(2,1)} %get-tuple-element.42), channel_id=1, source_target_pairs={{0,8},{4,12},{8,0},{12,4},{1,9},{5,13},{9,1},{13,5},{2,10},{6,14},... | collective-permute-start | bytes 884744 | tf_op jit(solution)/shard_map/ppermute | solution.py:30
  15.0 25.0 %collective-permute-start.2 = (bf16[9,2,2,32,128]{4,3,2,1,0:T(8,128)(2,1)}, bf16[9,2,2,32,128]{4,3,2,1,0:T(8,128)(2,1)}, u32[]{:S(2)}, u32[]{:S(2)}) collective-permute-start(bf16[9,2,2,32,128]{4,3,2,1,0:T(8,128)(2,1)} %get-tuple-element.43), channel_id=1, source_target_pairs={{0,4},{4,0},{8,12},{12,8},{1,5},{5,1},{9,13},{13,9},{2,6},{6,2},{1... | collective-permute-start | bytes 884744 | tf_op jit(solution)/shard_map/ppermute | solution.py:30
  30.3 9.7 %copy-start = (bf16[9,2,2,32,128]{4,3,2,1,0:T(8,128)(2,1)S(1)}, bf16[9,2,2,32,128]{4,3,2,1,0:T(8,128)(2,1)}, u32[]{:S(2)}) copy-start(bf16[9,2,2,32,128]{4,3,2,1,0:T(8,128)(2,1)} %get-tuple-element.57.refs_0_) | copy-start | bytes 884740
  40.0 3.5 %collective-permute-start.7 = (bf16[9,2,2,32,128]{4,3,2,1,0:T(8,128)(2,1)S(1)}, bf16[9,2,2,32,128]{4,3,2,1,0:T(8,128)(2,1)S(1)}, u32[]{:S(2)}, u32[]{:S(2)}) collective-permute-start(bf16[9,2,2,32,128]{4,3,2,1,0:T(8,128)(2,1)S(1)} %copy-done), channel_id=1, source_target_pairs={{0,1},{1,0},{2,3},{3,2},{4,5},{5,4},{6,7},{7,6},{8,9},{9,8},{10,11... | collective-permute-start | bytes 884744 | tf_op jit(solution)/shard_map/ppermute | solution.py:30
  40.0 3.5 %collective-permute-start.8 = (bf16[9,2,2,32,128]{4,3,2,1,0:T(8,128)(2,1)S(1)}, bf16[9,2,2,32,128]{4,3,2,1,0:T(8,128)(2,1)S(1)}, u32[]{:S(2)}, u32[]{:S(2)}) collective-permute-start(bf16[9,2,2,32,128]{4,3,2,1,0:T(8,128)(2,1)S(1)} %collective-permute-done.refs_2_), channel_id=1, source_target_pairs={{0,1},{1,0},{2,3},{3,2},{4,5},{5,4},{6,7},{7,6},{8,9},{9,8},{10,11... | collective-permute-start | bytes 884744 | tf_op jit(solution)/shard_map/ppermute | solution.py:30
  40.5 5.0 %collective-permute-start.9 = (bf16[9,2,2,32,128]{4,3,2,1,0:T(8,128)(2,1)S(1)}, bf16[9,2,2,32,128]{4,3,2,1,0:T(8,128)(2,1)S(1)}, u32[]{:S(2)}, u32[]{:S(2)}) collective-permute-start(bf16[9,2,2,32,128]{4,3,2,1,0:T(8,128)(2,1)S(1)} %collective-permute-done.1.refs_4_), channel_id=1, source_target_pairs={{0,1},{1,0},{2,3},{3,2},{4,5},{5,4},{6,7},{7,6},{8,9},{9,8},{10,11... | collective-permute-start | bytes 884744 | tf_op jit(solution)/shard_map/ppermute | solution.py:30
  40.6 4.9 %collective-permute-start.10 = (bf16[9,2,2,32,128]{4,3,2,1,0:T(8,128)(2,1)}, bf16[9,2,2,32,128]{4,3,2,1,0:T(8,128)(2,1)S(1)}, u32[]{:S(2)}, u32[]{:S(2)}) collective-permute-start(bf16[9,2,2,32,128]{4,3,2,1,0:T(8,128)(2,1)} %collective-permute-done.2.refs_6_), channel_id=1, source_target_pairs={{0,1},{1,0},{2,3},{3,2},{4,5},{5,4},{6,7},{7,6},{8,9},{9,8},{10,11... | collective-permute-start | bytes 884744 | tf_op jit(solution)/shard_map/ppermute | solution.py:30
  41.1 10.6 %collective-permute-start.4 = (bf16[7,2,2,32,128]{4,3,2,1,0:T(8,128)(2,1)}, bf16[7,2,2,32,128]{4,3,2,1,0:T(8,128)(2,1)S(1)}, u32[]{:S(2)}, u32[]{:S(2)}) collective-permute-start(bf16[7,2,2,32,128]{4,3,2,1,0:T(8,128)(2,1)} %get-tuple-element.54), channel_id=1, source_target_pairs={{0,12},{4,8},{8,4},{12,0},{1,13},{5,9},{9,5},{13,1},{2,14},{6,10},... | collective-permute-start | bytes 688136 | tf_op jit(solution)/shard_map/ppermute | solution.py:30
  43.5 19.3 %collective-permute-start.5 = (bf16[7,2,2,32,128]{4,3,2,1,0:T(8,128)(2,1)}, bf16[7,2,2,32,128]{4,3,2,1,0:T(8,128)(2,1)S(1)}, u32[]{:S(2)}, u32[]{:S(2)}) collective-permute-start(bf16[7,2,2,32,128]{4,3,2,1,0:T(8,128)(2,1)} %get-tuple-element.55), channel_id=1, source_target_pairs={{0,8},{4,12},{8,0},{12,4},{1,9},{5,13},{9,1},{13,5},{2,10},{6,14},... | collective-permute-start | bytes 688136 | tf_op jit(solution)/shard_map/ppermute | solution.py:30
  43.5 19.3 %collective-permute-start.6 = (bf16[7,2,2,32,128]{4,3,2,1,0:T(8,128)(2,1)}, bf16[7,2,2,32,128]{4,3,2,1,0:T(8,128)(2,1)S(1)}, u32[]{:S(2)}, u32[]{:S(2)}) collective-permute-start(bf16[7,2,2,32,128]{4,3,2,1,0:T(8,128)(2,1)} %get-tuple-element.56), channel_id=1, source_target_pairs={{0,4},{4,0},{8,12},{12,8},{1,5},{5,1},{9,13},{13,9},{2,6},{6,2},{1... | collective-permute-start | bytes 688136 | tf_op jit(solution)/shard_map/ppermute | solution.py:30
  45.5 17.3 %copy-start.1 = (bf16[7,2,2,32,128]{4,3,2,1,0:T(8,128)(2,1)S(1)}, bf16[7,2,2,32,128]{4,3,2,1,0:T(8,128)(2,1)}, u32[]{:S(2)}) copy-start(bf16[7,2,2,32,128]{4,3,2,1,0:T(8,128)(2,1)} %get-tuple-element.65.refs_0_) | copy-start | bytes 688132
  51.0 11.8 %collective-permute-start.11 = (bf16[512,128]{1,0:T(8,128)(2,1)S(1)}, bf16[512,128]{1,0:T(8,128)(2,1)S(1)}, u32[]{:S(2)}, u32[]{:S(2)}) collective-permute-start(bf16[512,128]{1,0:T(8,128)(2,1)S(1)} %get-tuple-element.69.refs_8_), channel_id=1, source_target_pairs={{0,2},{2,0},{1,3},{3,1},{4,6},{6,4},{5,7},{7,5},{8,10},{10,8},{9,1... | collective-permute-start | bytes 393224 | tf_op jit(solution)/shard_map/ppermute | solution.py:30
  62.8 1.6 %collective-permute-start.12 = (bf16[7,2,2,32,128]{4,3,2,1,0:T(8,128)(2,1)S(1)}, bf16[7,2,2,32,128]{4,3,2,1,0:T(8,128)(2,1)S(1)}, u32[]{:S(2)}, u32[]{:S(2)}) collective-permute-start(bf16[7,2,2,32,128]{4,3,2,1,0:T(8,128)(2,1)S(1)} %copy-done.1), channel_id=1, source_target_pairs={{0,1},{1,0},{2,3},{3,2},{4,5},{5,4},{6,7},{7,6},{8,9},{9,8},{10,11... | collective-permute-start | bytes 688136 | tf_op jit(solution)/shard_map/ppermute | solution.py:30
  62.9 1.8 %collective-permute-start.13 = (bf16[7,2,2,32,128]{4,3,2,1,0:T(8,128)(2,1)S(1)}, bf16[7,2,2,32,128]{4,3,2,1,0:T(8,128)(2,1)S(1)}, u32[]{:S(2)}, u32[]{:S(2)}) collective-permute-start(bf16[7,2,2,32,128]{4,3,2,1,0:T(8,128)(2,1)S(1)} %collective-permute-done.4.refs_2_), channel_id=1, source_target_pairs={{0,1},{1,0},{2,3},{3,2},{4,5},{5,4},{6,7},{7,6},{8,9},{9,8},{10,11... | collective-permute-start | bytes 688136 | tf_op jit(solution)/shard_map/ppermute | solution.py:30
  63.4 1.6 %collective-permute-start.14 = (bf16[7,2,2,32,128]{4,3,2,1,0:T(8,128)(2,1)S(1)}, bf16[7,2,2,32,128]{4,3,2,1,0:T(8,128)(2,1)S(1)}, u32[]{:S(2)}, u32[]{:S(2)}) collective-permute-start(bf16[7,2,2,32,128]{4,3,2,1,0:T(8,128)(2,1)S(1)} %collective-permute-done.5.refs_4_), channel_id=1, source_target_pairs={{0,1},{1,0},{2,3},{3,2},{4,5},{5,4},{6,7},{7,6},{8,9},{9,8},{10,11... | collective-permute-start | bytes 688136 | tf_op jit(solution)/shard_map/ppermute | solution.py:30
  63.5 1.9 %collective-permute-start.15 = (bf16[7,2,2,32,128]{4,3,2,1,0:T(8,128)(2,1)S(1)}, bf16[7,2,2,32,128]{4,3,2,1,0:T(8,128)(2,1)S(1)}, u32[]{:S(2)}, u32[]{:S(2)}) collective-permute-start(bf16[7,2,2,32,128]{4,3,2,1,0:T(8,128)(2,1)S(1)} %collective-permute-done.6.refs_6_), channel_id=1, source_target_pairs={{0,1},{1,0},{2,3},{3,2},{4,5},{5,4},{6,7},{7,6},{8,9},{9,8},{10,11... | collective-permute-start | bytes 688136 | tf_op jit(solution)/shard_map/ppermute | solution.py:30

commit v4 on v3

--- a/solution.py
+++ b/solution.py
@@ -354,7 +354,7 @@
             mixers, place, centre = make_tables(*late, in_dev, frames_dev)
             place = place.reshape(frames_dev * channels, -1)
         ready.append([own[0]] + [exchanged(own[d], "chan", d) for d in range(1, chan_devices)])
-    ready[0], ready[1][0] = lax.optimization_barrier((ready[0], ready[1][0]))
+    ready[0][1:], ready[1][0] = lax.optimization_barrier((ready[0][1:], ready[1][0]))
 
     def with_hops(arrived):
         pieces = []
@@ -378,7 +378,7 @@
         place[half * channels :],
     )
     levels = [level] + [exchanged(level, "tm", e) for e in range(1, time_devices)]
-    ready[1], sums, levels = lax.optimization_barrier((ready[1], sums, levels))
+    ready[1][1:], sums, levels = lax.optimization_barrier((ready[1][1:], sums, levels))
     spectra = with_hops(ready[1])
     level_scale = 1.0 / (time_devices * (frames_dev - half))
     share = beams // chan_devices

time: 81.8 us -> 81.3 us (level)
  starting transfers between devices: 16.8 us -> 15.8 us
    ppermute x15, starting transfers between devices: 10.9 us -> 10 us  [exchanged(): lax.ppermute(value, axis, [(source, partner(source, step, count)) for sou...]
  transfers between devices with their start and end apart: 16 -> 16, of which waited for: 8 -> 7; matrix products, arithmetic and copies ran while one was open for 6% -> 6% of each run, Pallas kernels for 14% -> 14%
where the time goes in v4:
time: 81.3 us; the launch traced here: 81.1 us
  waiting for transfers between devices  26.5 us (33%)
  Pallas kernels  20.8 us (26%)
  starting transfers between devices  15.8 us (19%)
  blocking collectives  12 us (15%)
  local copies, waits for them, and re-layouts  5.01 us (6%)
    ppermute x15, waiting for transfers between devices, exchanged(): lax.ppermute(value, axis, [(source, partner(source, step, count)) for sou...  18.1 us
    all_to_all x1, blocking collectives, shards(): lax.all_to_all(blocks, ('chan', 'tm'), split_axis=0, concat_axis=0, tiled...  12 us
    pallas_call x2, Pallas kernels, make_spectra(): pl.pallas_call(functools.partial(spectra_kernel, first, frames, length, h...  10.4 us
    ppermute x15, starting transfers between devices, exchanged(): lax.ppermute(value, axis, [(source, partner(source, step, count)) for sou...  10 us
    pallas_call x2, Pallas kernels, beam_call(): pl.pallas_call(kernel, out_shape=out_shape, in_specs=[vmem_spec()] * len(...  9.37 us
    ppermute x1, waiting for transfers between devices, from_previous(): lax.ppermute(value, axis, [(source, source + 1) for source in range(count...  8.36 us
    ppermute x1, starting transfers between devices, from_previous(): lax.ppermute(value, axis, [(source, source + 1) for source in range(count...  5.82 us
    dynamic_slice x1, local copies, waits for them, and re-layouts, make_tables(): chosen = lax.dynamic_index_in_dim(arranged, core, 3, keepdims=False)  3.27 us
  transfers between devices with their start and end apart: 16, of which 7 were waited for; matrix products, arithmetic and copies ran while one was open for 6% of the time, Pallas kernels for 14%

profile of v4, /device:TPU:0, one launch (start us, length us, event | category | flops | bytes accessed | tf_op | source)
XLA Modules:
  0.0 81.1 jit_solution(10885326899526890505)
XLA Ops:
  0.0 0.0 copy-start.4
  0.0 0.0 copy-start.2
  0.0 5.5 %spectra_7.1 = (bf16[9,2,2,32,128]{4,3,2,1,0:T(8,128)(2,1)}, bf16[9,2,2,32,128]{4,3,2,1,0:T(8,128)(2,1)}, bf16[9,2,2,32,128]{4,3,2,1,0:T(8,128)(2,1)}, bf16[9,2,...) custom-call(s32[1]{0:T(128)} %bitcast.refs_0_, bf16[64,16384]{1,0:T(8,128)(2,1)} %refs_2_.3, f32[8,1024]{1,0:T(8,128)} %refs_3_.2, ...), custom_call_target="tpu_custom_call" | custom-call | flops 1024 | bytes 1024 | tf_op jit(solution)/shard_map/spectra_7/pallas_call | solution.py:155
  5.5 5.8 %collective-permute-start.3 = (bf16[64,7168]{1,0:T(8,128)(2,1)}, bf16[64,7168]{1,0:T(8,128)(2,1)}, u32[]{:S(2)}, u32[]{:S(2)}) collective-permute-start(bf16[64,7168]{1,0:T(8,128)(2,1)} %get-tuple-element.40), channel_id=1, source_target_pairs={{0,2},{1,3},{4,6},{5,7},{8,10},{9,11},{12,14},{13,15},{16,18},{17,... | collective-permute-start | bytes 2752520 | tf_op jit(solution)/shard_map/ppermute | solution.py:39
  11.4 3.6 %collective-permute-start = (bf16[9,2,2,32,128]{4,3,2,1,0:T(8,128)(2,1)}, bf16[9,2,2,32,128]{4,3,2,1,0:T(8,128)(2,1)}, u32[]{:S(2)}, u32[]{:S(2)}) collective-permute-start(bf16[9,2,2,32,128]{4,3,2,1,0:T(8,128)(2,1)} %get-tuple-element.37), channel_id=1, source_target_pairs={{0,12},{4,8},{8,4},{12,0},{1,13},{5,9},{9,5},{13,1},{2,14},{6,10},... | collective-permute-start | bytes 884744 | tf_op jit(solution)/shard_map/ppermute | solution.py:30
  15.0 0.0 collective-permute-start.1
  15.0 0.8 collective-permute-start.2
  15.8 0.0 collective-permute-start.8
  15.8 0.0 copy-done.4
  15.8 0.1 reshape.96
  15.9 0.1 copy.12
  16.0 0.1 copy.13
  16.1 0.1 copy.14
  16.2 0.1 copy.15
  16.4 0.1 reshape.97
  16.5 0.0 copy-done.2
  16.5 0.7 reshape.98
  17.2 0.0 copy-start.3
  17.2 3.3 %dynamic-slice_reduce_fusion = bf16[2,256,4,128]{3,2,0,1:T(4,128)(2,1)S(1)} fusion(bf16[2,256,4,2,128]{4,3,2,0,1:T(2,128)(2,1)S(1)} %reshape.98, s32[]{:T(128)S(6)} %select_n.50), kind=kLoop, calls=%fused_computation | loop fusion | bytes 1048580 | tf_op jit(solution)/shard_map/jit(dynamic_index_in_dim)/dynamic_slice | solution.py:301
  20.5 0.2 reshape.101
  20.7 0.1 copy.20.refs_2_
  20.7 0.0 copy-done.3
  20.7 0.1 copy.18.refs_3_
  20.9 1.1 %tables.1 = (bf16[2,1024,512]{2,1,0:T(8,128)(2,1)S(1)}, bf16[16,128,256]{2,1,0:T(8,128)(2,1)S(1)}, bf16[128,256]{1,0:T(8,128)(2,1)S(1)}) custom-call(s32[1]{0:T(128)} %bitcast.1.refs_0_, s32[3,512]{1,0:T(4,128)S(1)} %pad_add_fusion.1.refs_1_, bf16[2,256,512]{2,1,0:T(8,128)(2,1)S(1)} %copy.20.refs_2_, s32[128,8]{1,0:T(8,128)S(1)} %copy.18.refs_3_), custom_call_target="tpu_custom_call" | custom-call | flops 1024 | bytes 1024 | tf_op jit(solution)/shard_map/tables/pallas_call | solution.py:315
  21.9 8.4 %collective-permute-done.3.refs_1_ = bf16[64,7168]{1,0:T(8,128)(2,1)} collective-permute-done((bf16[64,7168]{1,0:T(8,128)(2,1)}, bf16[64,7168]{1,0:T(8,128)(2,1)}, u32[]{:S(2)}, u32[]{:S(2)}) %collective-permute-start.3) | collective-permute-done | bytes 917536 | tf_op jit(solution)/shard_map/ppermute | solution.py:39
  30.3 0.0 copy-start
  30.3 4.9 %spectra_0.1 = (bf16[7,2,2,32,128]{4,3,2,1,0:T(8,128)(2,1)}, bf16[7,2,2,32,128]{4,3,2,1,0:T(8,128)(2,1)}, bf16[7,2,2,32,128]{4,3,2,1,0:T(8,128)(2,1)}, bf16[7,2,2,32,128]{4,3,2,1,0:T(8,128)(2,1)}) custom-call(s32[1]{0:T(128)} %bitcast.refs_0_, bf16[64,7168]{1,0:T(8,128)(2,1)} %collective-permute-done.3.refs_1_, bf16[64,16384]{1,0:T(8,128)(2,1)} %refs_2_.3, ...), custom_call_target="tpu_custom_call" | custom-call | flops 1024 | bytes 1024 | tf_op jit(solution)/shard_map/spectra_0/pallas_call | solution.py:155
  35.2 0.0 collective-permute-done.refs_2_
  35.2 4.9 %collective-permute-done.1.refs_4_ = bf16[9,2,2,32,128]{4,3,2,1,0:T(8,128)(2,1)} collective-permute-done((bf16[9,2,2,32,128]{4,3,2,1,0:T(8,128)(2,1)}, bf16[9,2,2,32,128]{4,3,2,1,0:T(8,128)(2,1)}, u32[]{:S(2)}, u32[]{:S(2)}) %collective-permute-start.1) | collective-permute-done | bytes 294944 | tf_op jit(solution)/shard_map/ppermute | solution.py:30
  40.1 0.0 collective-permute-done.2.refs_6_
  40.1 0.0 collective-permute-start.10
  40.1 0.5 collective-permute-start.11
  40.6 0.0 collective-permute-start.9
  40.6 2.5 %collective-permute-start.5 = (bf16[7,2,2,32,128]{4,3,2,1,0:T(8,128)(2,1)}, bf16[7,2,2,32,128]{4,3,2,1,0:T(8,128)(2,1)S(1)}, u32[]{:S(2)}, u32[]{:S(2)}) collective-permute-start(bf16[7,2,2,32,128]{4,3,2,1,0:T(8,128)(2,1)} %get-tuple-element.51), channel_id=1, source_target_pairs={{0,12},{4,8},{8,4},{12,0},{1,13},{5,9},{9,5},{13,1},{2,14},{6,10},... | collective-permute-start | bytes 688136 | tf_op jit(solution)/shard_map/ppermute | solution.py:30
  43.1 0.0 collective-permute-done.8.refs_1_
  43.1 0.0 collective-permute-start.6
  43.1 0.0 collective-permute-done.10.refs_5_
  43.1 1.9 %collective-permute-start.7 = (bf16[7,2,2,32,128]{4,3,2,1,0:T(8,128)(2,1)}, bf16[7,2,2,32,128]{4,3,2,1,0:T(8,128)(2,1)S(1)}, u32[]{:S(2)}, u32[]{:S(2)}) collective-permute-start(bf16[7,2,2,32,128]{4,3,2,1,0:T(8,128)(2,1)} %get-tuple-element.53), channel_id=1, source_target_pairs={{0,4},{4,0},{8,12},{12,8},{1,5},{5,1},{9,13},{13,9},{2,6},{6,2},{1... | collective-permute-start | bytes 688136 | tf_op jit(solution)/shard_map/ppermute | solution.py:30
  45.1 0.0 copy-start.1
  45.1 0.0 collective-permute-done.11.refs_7_
  45.1 0.0 collective-permute-done.9.refs_3_
  45.1 0.0 copy-done
  45.1 5.8 %beam_first.1 = (f32[512,256]{1,0:T(8,128)S(1)}, bf16[512,128]{1,0:T(8,128)(2,1)S(1)}) custom-call(bf16[9,2,2,32,128]{4,3,2,1,0:T(8,128)(2,1)S(1)} %copy-done, bf16[9,2,2,32,128]{4,3,2,1,0:T(8,128)(2,1)} %collective-permute-done.8.refs_1_, bf16[9,2,2,32,128]{4,3,2,1,0:T(8,128)(2,1)} %collective-permute-done.refs_2_, ...), custom_call_target="tpu_custom_call" | custom-call | flops 1024 | bytes 1024 | tf_op jit(solution)/shard_map/beam_first/pallas_call | solution.py:246
  50.9 0.1 collective-permute-start.12
  51.0 0.0 copy-done.1
  51.0 0.1 collective-permute-start.4
  51.1 0.1 collective-permute-done.5.refs_2_
  51.2 11.5 %collective-permute-done.6.refs_4_ = bf16[7,2,2,32,128]{4,3,2,1,0:T(8,128)(2,1)S(1)} collective-permute-done((bf16[7,2,2,32,128]{4,3,2,1,0:T(8,128)(2,1)}, bf16[7,2,2,32,128]{4,3,2,1,0:T(8,128)(2,1)S(1)}, u32[]{:S(2)}, u32[]{:S(2)}) %collective-permute-start.6) | collective-permute-done | bytes 229408 | tf_op jit(solution)/shard_map/ppermute | solution.py:30
  62.7 0.0 collective-permute-done.7.refs_6_
  62.7 0.0 collective-permute-done.12.refs_9_
  62.7 0.0 collective-permute-start.13
  62.7 0.5 collective-permute-start.14
  63.2 0.1 collective-permute-start.15
  63.3 0.0 collective-permute-done.4.refs_1_
  63.3 0.9 %collective-permute-done.13.refs_3_ = bf16[7,2,2,32,128]{4,3,2,1,0:T(8,128)(2,1)S(1)} collective-permute-done((bf16[7,2,2,32,128]{4,3,2,1,0:T(8,128)(2,1)S(1)}, bf16[7,2,2,32,128]{4,3,2,1,0:T(8,128)(2,1)S(1)}, u32[]{:S(2)}, u32[]{:S(2)}) %collective-permute-start.13) | collective-permute-done | bytes 229408 | tf_op jit(solution)/shard_map/ppermute | solution.py:30
  64.2 0.3 collective-permute-done.14.refs_5_
  64.5 0.3 collective-permute-done.15.refs_7_
  64.9 3.6 %beam_last.1 = bf16[8,128,128]{2,1,0:T(8,128)(2,1)S(1)} custom-call(bf16[7,2,2,32,128]{4,3,2,1,0:T(8,128)(2,1)S(1)} %copy-done.1, bf16[7,2,2,32,128]{4,3,2,1,0:T(8,128)(2,1)S(1)} %collective-permute-done.4.refs_1_, bf16[7,2,2,32,128]{4,3,2,1,0:T(8,128)(2,1)S(1)} %collective-permute-done.5.refs_2_, ...), custom_call_target="tpu_custom_call" | custom-call | flops 1024 | bytes 1024 | tf_op jit(solution)/shard_map/beam_last/pallas_call | solution.py:246
  68.5 12.0 %all_to_all.5 = bf16[8,128,128]{2,1,0:T(8,128)(2,1)S(1)} all-to-all(bf16[8,128,128]{2,1,0:T(8,128)(2,1)S(1)} %beam_last.1), channel_id=1, replica_groups=mesh['groups'=2,'chan'=4,'tm'=2,'beam'=2] {'chan','tm'}, dimensions={0} | all-to-all | bytes 524288 | tf_op jit(solution)/shard_map/all_to_all | solution.py:397
  80.5 0.6 broadcast_multiply_fusion
  (11 shorter events, 0.2 us)
Async XLA Ops:
  0.0 15.8 %copy-start.4 = (s32[512]{0:T(512)S(1)}, s32[512]{0:T(512)}, u32[]{:S(2)}) copy-start(s32[512]{0:T(512)} %param.9) | copy-start | bytes 6148
  0.0 16.5 %copy-start.2 = (bf16[256,2,1024]{2,1,0:T(2,128)(2,1)S(1)}, bf16[256,2,1024]{2,1,0:T(2,128)(2,1)}, u32[]{:S(2)}) copy-start(bf16[256,2,1024]{2,1,0:T(2,128)(2,1)} %param.8) | copy-start | bytes 3145732
  5.5 24.8 %collective-permute-start.3 = (bf16[64,7168]{1,0:T(8,128)(2,1)}, bf16[64,7168]{1,0:T(8,128)(2,1)}, u32[]{:S(2)}, u32[]{:S(2)}) collective-permute-start(bf16[64,7168]{1,0:T(8,128)(2,1)} %get-tuple-element.40), channel_id=1, source_target_pairs={{0,2},{1,3},{4,6},{5,7},{8,10},{9,11},{12,14},{13,15},{16,18},{17,... | collective-permute-start | bytes 2752520 | tf_op jit(solution)/shard_map/ppermute | solution.py:39
  11.4 23.8 %collective-permute-start = (bf16[9,2,2,32,128]{4,3,2,1,0:T(8,128)(2,1)}, bf16[9,2,2,32,128]{4,3,2,1,0:T(8,128)(2,1)}, u32[]{:S(2)}, u32[]{:S(2)}) collective-permute-start(bf16[9,2,2,32,128]{4,3,2,1,0:T(8,128)(2,1)} %get-tuple-element.37), channel_id=1, source_target_pairs={{0,12},{4,8},{8,4},{12,0},{1,13},{5,9},{9,5},{13,1},{2,14},{6,10},... | collective-permute-start | bytes 884744 | tf_op jit(solution)/shard_map/ppermute | solution.py:30
  15.0 25.2 %collective-permute-start.1 = (bf16[9,2,2,32,128]{4,3,2,1,0:T(8,128)(2,1)}, bf16[9,2,2,32,128]{4,3,2,1,0:T(8,128)(2,1)}, u32[]{:S(2)}, u32[]{:S(2)}) collective-permute-start(bf16[9,2,2,32,128]{4,3,2,1,0:T(8,128)(2,1)} %get-tuple-element.38), channel_id=1, source_target_pairs={{0,8},{4,12},{8,0},{12,4},{1,9},{5,13},{9,1},{13,5},{2,10},{6,14},... | collective-permute-start | bytes 884744 | tf_op jit(solution)/shard_map/ppermute | solution.py:30
  15.0 25.2 %collective-permute-start.2 = (bf16[9,2,2,32,128]{4,3,2,1,0:T(8,128)(2,1)}, bf16[9,2,2,32,128]{4,3,2,1,0:T(8,128)(2,1)}, u32[]{:S(2)}, u32[]{:S(2)}) collective-permute-start(bf16[9,2,2,32,128]{4,3,2,1,0:T(8,128)(2,1)} %get-tuple-element.39), channel_id=1, source_target_pairs={{0,4},{4,0},{8,12},{12,8},{1,5},{5,1},{9,13},{13,9},{2,6},{6,2},{1... | collective-permute-start | bytes 884744 | tf_op jit(solution)/shard_map/ppermute | solution.py:30
  15.8 27.4 %collective-permute-start.8 = (bf16[9,2,2,32,128]{4,3,2,1,0:T(8,128)(2,1)}, bf16[9,2,2,32,128]{4,3,2,1,0:T(8,128)(2,1)}, u32[]{:S(2)}, u32[]{:S(2)}) collective-permute-start(bf16[9,2,2,32,128]{4,3,2,1,0:T(8,128)(2,1)} %get-tuple-element.54.refs_0_), channel_id=1, source_target_pairs={{0,1},{1,0},{2,3},{3,2},{4,5},{5,4},{6,7},{7,6},{8,9},{9,8},{10,11... | collective-permute-start | bytes 884744 | tf_op jit(solution)/shard_map/ppermute | solution.py:30
  17.2 3.6 %copy-start.3 = (s32[128,8]{0,1:T(8,128)S(1)}, s32[128,8]{0,1:T(8,128)}, u32[]{:S(2)}) copy-start(s32[128,8]{0,1:T(8,128)} %param.10) | copy-start | bytes 12292
  30.3 14.8 %copy-start = (bf16[9,2,2,32,128]{4,3,2,1,0:T(8,128)(2,1)S(1)}, bf16[9,2,2,32,128]{4,3,2,1,0:T(8,128)(2,1)}, u32[]{:S(2)}) copy-start(bf16[9,2,2,32,128]{4,3,2,1,0:T(8,128)(2,1)} %get-tuple-element.54.refs_0_) | copy-start | bytes 884740
  40.1 3.0 %collective-permute-start.10 = (bf16[9,2,2,32,128]{4,3,2,1,0:T(8,128)(2,1)}, bf16[9,2,2,32,128]{4,3,2,1,0:T(8,128)(2,1)S(1)}, u32[]{:S(2)}, u32[]{:S(2)}) collective-permute-start(bf16[9,2,2,32,128]{4,3,2,1,0:T(8,128)(2,1)} %collective-permute-done.1.refs_4_), channel_id=1, source_target_pairs={{0,1},{1,0},{2,3},{3,2},{4,5},{5,4},{6,7},{7,6},{8,9},{9,8},{10,11... | collective-permute-start | bytes 884744 | tf_op jit(solution)/shard_map/ppermute | solution.py:30
  40.1 5.0 %collective-permute-start.11 = (bf16[9,2,2,32,128]{4,3,2,1,0:T(8,128)(2,1)}, bf16[9,2,2,32,128]{4,3,2,1,0:T(8,128)(2,1)S(1)}, u32[]{:S(2)}, u32[]{:S(2)}) collective-permute-start(bf16[9,2,2,32,128]{4,3,2,1,0:T(8,128)(2,1)} %collective-permute-done.2.refs_6_), channel_id=1, source_target_pairs={{0,1},{1,0},{2,3},{3,2},{4,5},{5,4},{6,7},{7,6},{8,9},{9,8},{10,11... | collective-permute-start | bytes 884744 | tf_op jit(solution)/shard_map/ppermute | solution.py:30
  40.6 4.5 %collective-permute-start.9 = (bf16[9,2,2,32,128]{4,3,2,1,0:T(8,128)(2,1)}, bf16[9,2,2,32,128]{4,3,2,1,0:T(8,128)(2,1)S(1)}, u32[]{:S(2)}, u32[]{:S(2)}) collective-permute-start(bf16[9,2,2,32,128]{4,3,2,1,0:T(8,128)(2,1)} %collective-permute-done.refs_2_), channel_id=1, source_target_pairs={{0,1},{1,0},{2,3},{3,2},{4,5},{5,4},{6,7},{7,6},{8,9},{9,8},{10,11... | collective-permute-start | bytes 884744 | tf_op jit(solution)/shard_map/ppermute | solution.py:30
  40.6 10.6 %collective-permute-start.5 = (bf16[7,2,2,32,128]{4,3,2,1,0:T(8,128)(2,1)}, bf16[7,2,2,32,128]{4,3,2,1,0:T(8,128)(2,1)S(1)}, u32[]{:S(2)}, u32[]{:S(2)}) collective-permute-start(bf16[7,2,2,32,128]{4,3,2,1,0:T(8,128)(2,1)} %get-tuple-element.51), channel_id=1, source_target_pairs={{0,12},{4,8},{8,4},{12,0},{1,13},{5,9},{9,5},{13,1},{2,14},{6,10},... | collective-permute-start | bytes 688136 | tf_op jit(solution)/shard_map/ppermute | solution.py:30
  43.1 19.6 %collective-permute-start.6 = (bf16[7,2,2,32,128]{4,3,2,1,0:T(8,128)(2,1)}, bf16[7,2,2,32,128]{4,3,2,1,0:T(8,128)(2,1)S(1)}, u32[]{:S(2)}, u32[]{:S(2)}) collective-permute-start(bf16[7,2,2,32,128]{4,3,2,1,0:T(8,128)(2,1)} %get-tuple-element.52), channel_id=1, source_target_pairs={{0,8},{4,12},{8,0},{12,4},{1,9},{5,13},{9,1},{13,5},{2,10},{6,14},... | collective-permute-start | bytes 688136 | tf_op jit(solution)/shard_map/ppermute | solution.py:30
  43.1 19.6 %collective-permute-start.7 = (bf16[7,2,2,32,128]{4,3,2,1,0:T(8,128)(2,1)}, bf16[7,2,2,32,128]{4,3,2,1,0:T(8,128)(2,1)S(1)}, u32[]{:S(2)}, u32[]{:S(2)}) collective-permute-start(bf16[7,2,2,32,128]{4,3,2,1,0:T(8,128)(2,1)} %get-tuple-element.53), channel_id=1, source_target_pairs={{0,4},{4,0},{8,12},{12,8},{1,5},{5,1},{9,13},{13,9},{2,6},{6,2},{1... | collective-permute-start | bytes 688136 | tf_op jit(solution)/shard_map/ppermute | solution.py:30
  45.1 5.9 %copy-start.1 = (bf16[7,2,2,32,128]{4,3,2,1,0:T(8,128)(2,1)S(1)}, bf16[7,2,2,32,128]{4,3,2,1,0:T(8,128)(2,1)}, u32[]{:S(2)}) copy-start(bf16[7,2,2,32,128]{4,3,2,1,0:T(8,128)(2,1)} %get-tuple-element.50.refs_0_) | copy-start | bytes 688132
  50.9 11.8 %collective-permute-start.12 = (bf16[512,128]{1,0:T(8,128)(2,1)S(1)}, bf16[512,128]{1,0:T(8,128)(2,1)S(1)}, u32[]{:S(2)}, u32[]{:S(2)}) collective-permute-start(bf16[512,128]{1,0:T(8,128)(2,1)S(1)} %get-tuple-element.65.refs_8_), channel_id=1, source_target_pairs={{0,2},{2,0},{1,3},{3,1},{4,6},{6,4},{5,7},{7,5},{8,10},{10,8},{9,1... | collective-permute-start | bytes 393224 | tf_op jit(solution)/shard_map/ppermute | solution.py:30
  51.0 12.4 %collective-permute-start.4 = (bf16[7,2,2,32,128]{4,3,2,1,0:T(8,128)(2,1)S(1)}, bf16[7,2,2,32,128]{4,3,2,1,0:T(8,128)(2,1)S(1)}, u32[]{:S(2)}, u32[]{:S(2)}) collective-permute-start(bf16[7,2,2,32,128]{4,3,2,1,0:T(8,128)(2,1)S(1)} %copy-done.1), channel_id=1, source_target_pairs={{0,1},{1,0},{2,3},{3,2},{4,5},{5,4},{6,7},{7,6},{8,9},{9,8},{10,11... | collective-permute-start | bytes 688136 | tf_op jit(solution)/shard_map/ppermute | solution.py:30
  62.7 1.5 %collective-permute-start.13 = (bf16[7,2,2,32,128]{4,3,2,1,0:T(8,128)(2,1)S(1)}, bf16[7,2,2,32,128]{4,3,2,1,0:T(8,128)(2,1)S(1)}, u32[]{:S(2)}, u32[]{:S(2)}) collective-permute-start(bf16[7,2,2,32,128]{4,3,2,1,0:T(8,128)(2,1)S(1)} %collective-permute-done.5.refs_2_), channel_id=1, source_target_pairs={{0,1},{1,0},{2,3},{3,2},{4,5},{5,4},{6,7},{7,6},{8,9},{9,8},{10,11... | collective-permute-start | bytes 688136 | tf_op jit(solution)/shard_map/ppermute | solution.py:30
  62.7 1.8 %collective-permute-start.14 = (bf16[7,2,2,32,128]{4,3,2,1,0:T(8,128)(2,1)S(1)}, bf16[7,2,2,32,128]{4,3,2,1,0:T(8,128)(2,1)S(1)}, u32[]{:S(2)}, u32[]{:S(2)}) collective-permute-start(bf16[7,2,2,32,128]{4,3,2,1,0:T(8,128)(2,1)S(1)} %collective-permute-done.6.refs_4_), channel_id=1, source_target_pairs={{0,1},{1,0},{2,3},{3,2},{4,5},{5,4},{6,7},{7,6},{8,9},{9,8},{10,11... | collective-permute-start | bytes 688136 | tf_op jit(solution)/shard_map/ppermute | solution.py:30
  63.2 1.6 %collective-permute-start.15 = (bf16[7,2,2,32,128]{4,3,2,1,0:T(8,128)(2,1)S(1)}, bf16[7,2,2,32,128]{4,3,2,1,0:T(8,128)(2,1)S(1)}, u32[]{:S(2)}, u32[]{:S(2)}) collective-permute-start(bf16[7,2,2,32,128]{4,3,2,1,0:T(8,128)(2,1)S(1)} %collective-permute-done.7.refs_6_), channel_id=1, source_target_pairs={{0,1},{1,0},{2,3},{3,2},{4,5},{5,4},{6,7},{7,6},{8,9},{9,8},{10,11... | collective-permute-start | bytes 688136 | tf_op jit(solution)/shard_map/ppermute | solution.py:30

commit v5 on v4

--- a/solution.py
+++ b/solution.py
@@ -79,7 +79,14 @@
                 )
             )
             copies[-1].start()
-    table_copy = pltpu.make_async_copy(dft_hbm, dft_ref, sems.at[1])
+    count = dft_ref.shape[0]
+    steps = (*range(1, count), 0)
+    table_copies = []
+    for d in steps:
+        block = partner(me_ref[0], d, count)
+        table_copies.append(
+            pltpu.make_async_copy(dft_hbm.at[block], dft_ref.at[block], sems.at[sems.shape[0] - 1 - d])
+        )
     writes = []
     if emit:
         *outs, rim_out = outs
@@ -118,18 +125,19 @@
             copy.wait()
         if block == 0:
             taps_copy.wait()
-            table_copy.start()
+            for table_copy in table_copies:
+                table_copy.start()
         filtered_block(block)
     if emit:
         writes.append(
             pltpu.make_async_copy(volt.at[:, pl.ds(frames * length, history * length)], rim_out, sems.at[2])
         )
         writes[-1].start()
-    table_copy.wait()
-    count = dft_ref.shape[0]
+    for table_copy in table_copies:
+        table_copy.wait()
     stations = rows // 2
     channels = outs[0].shape[-1]
-    for d in (*range(1, count), 0):
+    for d in steps:
         block = partner(me_ref[0], d, count)
         result = jnp.dot(filt[...], dft_ref[block], preferred_element_type=jnp.float32).astype(jnp.bfloat16)
         for f in range(frames):

time: 81.3 us -> 81.3 us (level)
  no operation moved by 1% of the time
where the time goes in v5:
time: 81.3 us; the launch traced here: 81.1 us
  waiting for transfers between devices  26.5 us (33%)
  Pallas kernels  20.9 us (26%)
  starting transfers between devices  15.8 us (19%)
  blocking collectives  12 us (15%)
  local copies, waits for them, and re-layouts  5.01 us (6%)
    ppermute x15, waiting for transfers between devices, exchanged(): lax.ppermute(value, axis, [(source, partner(source, step, count)) for sou...  18.1 us
    all_to_all x1, blocking collectives, shards(): lax.all_to_all(blocks, ('chan', 'tm'), split_axis=0, concat_axis=0, tiled...  12 us
    pallas_call x2, Pallas kernels, make_spectra(): pl.pallas_call(functools.partial(spectra_kernel, first, frames, length, h...  10.4 us
    ppermute x15, starting transfers between devices, exchanged(): lax.ppermute(value, axis, [(source, partner(source, step, count)) for sou...  10 us
    pallas_call x2, Pallas kernels, beam_call(): pl.pallas_call(kernel, out_shape=out_shape, in_specs=[vmem_spec()] * len(...  9.36 us
    ppermute x1, waiting for transfers between devices, from_previous(): lax.ppermute(value, axis, [(source, source + 1) for source in range(count...  8.35 us
    ppermute x1, starting transfers between devices, from_previous(): lax.ppermute(value, axis, [(source, source + 1) for source in range(count...  5.82 us
    dynamic_slice x1, local copies, waits for them, and re-layouts, make_tables(): chosen = lax.dynamic_index_in_dim(arranged, core, 3, keepdims=False)  3.27 us
  transfers between devices with their start and end apart: 16, of which 7 were waited for; matrix products, arithmetic and copies ran while one was open for 6% of the time, Pallas kernels for 14%

profile of v5, /device:TPU:0, one launch (start us, length us, event | category | flops | bytes accessed | tf_op | source)
XLA Modules:
  0.0 81.1 jit_solution(1571398631598882079)
XLA Ops:
  0.0 0.0 copy-start.4
  0.0 0.0 copy-start.2
  0.0 5.5 %spectra_7.1 = (bf16[9,2,2,32,128]{4,3,2,1,0:T(8,128)(2,1)}, bf16[9,2,2,32,128]{4,3,2,1,0:T(8,128)(2,1)}, bf16[9,2,2,32,128]{4,3,2,1,0:T(8,128)(2,1)}, bf16[9,2,...) custom-call(s32[1]{0:T(128)} %bitcast.refs_0_, bf16[64,16384]{1,0:T(8,128)(2,1)} %refs_2_.3, f32[8,1024]{1,0:T(8,128)} %refs_3_.2, ...), custom_call_target="tpu_custom_call" | custom-call | flops 1024 | bytes 1024 | tf_op jit(solution)/shard_map/spectra_7/pallas_call | solution.py:163
  5.5 5.8 %collective-permute-start.3 = (bf16[64,7168]{1,0:T(8,128)(2,1)}, bf16[64,7168]{1,0:T(8,128)(2,1)}, u32[]{:S(2)}, u32[]{:S(2)}) collective-permute-start(bf16[64,7168]{1,0:T(8,128)(2,1)} %get-tuple-element.40), channel_id=1, source_target_pairs={{0,2},{1,3},{4,6},{5,7},{8,10},{9,11},{12,14},{13,15},{16,18},{17,... | collective-permute-start | bytes 2752520 | tf_op jit(solution)/shard_map/ppermute | solution.py:39
  11.4 3.6 %collective-permute-start = (bf16[9,2,2,32,128]{4,3,2,1,0:T(8,128)(2,1)}, bf16[9,2,2,32,128]{4,3,2,1,0:T(8,128)(2,1)}, u32[]{:S(2)}, u32[]{:S(2)}) collective-permute-start(bf16[9,2,2,32,128]{4,3,2,1,0:T(8,128)(2,1)} %get-tuple-element.37), channel_id=1, source_target_pairs={{0,12},{4,8},{8,4},{12,0},{1,13},{5,9},{9,5},{13,1},{2,14},{6,10},... | collective-permute-start | bytes 884744 | tf_op jit(solution)/shard_map/ppermute | solution.py:30
  15.0 0.0 collective-permute-start.1
  15.0 0.8 collective-permute-start.2
  15.8 0.0 collective-permute-start.8
  15.8 0.0 copy-done.4
  15.8 0.1 reshape.96
  16.0 0.1 copy.12
  16.0 0.1 copy.13
  16.1 0.1 copy.14
  16.2 0.1 copy.15
  16.4 0.1 reshape.97
  16.5 0.0 copy-done.2
  16.5 0.7 reshape.98
  17.2 0.0 copy-start.3
  17.2 3.3 %dynamic-slice_reduce_fusion = bf16[2,256,4,128]{3,2,0,1:T(4,128)(2,1)S(1)} fusion(bf16[2,256,4,2,128]{4,3,2,0,1:T(2,128)(2,1)S(1)} %reshape.98, s32[]{:T(128)S(6)} %select_n.50), kind=kLoop, calls=%fused_computation | loop fusion | bytes 1048580 | tf_op jit(solution)/shard_map/jit(dynamic_index_in_dim)/dynamic_slice | solution.py:309
  20.5 0.2 reshape.101
  20.7 0.1 copy.20.refs_2_
  20.7 0.0 copy-done.3
  20.7 0.1 copy.18.refs_3_
  20.9 1.1 %tables.1 = (bf16[2,1024,512]{2,1,0:T(8,128)(2,1)S(1)}, bf16[16,128,256]{2,1,0:T(8,128)(2,1)S(1)}, bf16[128,256]{1,0:T(8,128)(2,1)S(1)}) custom-call(s32[1]{0:T(128)} %bitcast.1.refs_0_, s32[3,512]{1,0:T(4,128)S(1)} %pad_add_fusion.1.refs_1_, bf16[2,256,512]{2,1,0:T(8,128)(2,1)S(1)} %copy.20.refs_2_, s32[128,8]{1,0:T(8,128)S(1)} %copy.18.refs_3_), custom_call_target="tpu_custom_call" | custom-call | flops 1024 | bytes 1024 | tf_op jit(solution)/shard_map/tables/pallas_call | solution.py:323
  21.9 8.3 %collective-permute-done.3.refs_1_ = bf16[64,7168]{1,0:T(8,128)(2,1)} collective-permute-done((bf16[64,7168]{1,0:T(8,128)(2,1)}, bf16[64,7168]{1,0:T(8,128)(2,1)}, u32[]{:S(2)}, u32[]{:S(2)}) %collective-permute-start.3) | collective-permute-done | bytes 917536 | tf_op jit(solution)/shard_map/ppermute | solution.py:39
  30.3 0.0 copy-start
  30.3 4.9 %spectra_0.1 = (bf16[7,2,2,32,128]{4,3,2,1,0:T(8,128)(2,1)}, bf16[7,2,2,32,128]{4,3,2,1,0:T(8,128)(2,1)}, bf16[7,2,2,32,128]{4,3,2,1,0:T(8,128)(2,1)}, bf16[7,2,2,32,128]{4,3,2,1,0:T(8,128)(2,1)}) custom-call(s32[1]{0:T(128)} %bitcast.refs_0_, bf16[64,7168]{1,0:T(8,128)(2,1)} %collective-permute-done.3.refs_1_, bf16[64,16384]{1,0:T(8,128)(2,1)} %refs_2_.3, ...), custom_call_target="tpu_custom_call" | custom-call | flops 1024 | bytes 1024 | tf_op jit(solution)/shard_map/spectra_0/pallas_call | solution.py:163
  35.2 0.0 collective-permute-done.refs_2_
  35.2 4.9 %collective-permute-done.1.refs_4_ = bf16[9,2,2,32,128]{4,3,2,1,0:T(8,128)(2,1)} collective-permute-done((bf16[9,2,2,32,128]{4,3,2,1,0:T(8,128)(2,1)}, bf16[9,2,2,32,128]{4,3,2,1,0:T(8,128)(2,1)}, u32[]{:S(2)}, u32[]{:S(2)}) %collective-permute-start.1) | collective-permute-done | bytes 294944 | tf_op jit(solution)/shard_map/ppermute | solution.py:30
  40.1 0.0 collective-permute-done.2.refs_6_
  40.1 0.0 collective-permute-start.10
  40.1 0.5 collective-permute-start.11
  40.6 0.0 collective-permute-start.9
  40.6 2.5 %collective-permute-start.5 = (bf16[7,2,2,32,128]{4,3,2,1,0:T(8,128)(2,1)}, bf16[7,2,2,32,128]{4,3,2,1,0:T(8,128)(2,1)S(1)}, u32[]{:S(2)}, u32[]{:S(2)}) collective-permute-start(bf16[7,2,2,32,128]{4,3,2,1,0:T(8,128)(2,1)} %get-tuple-element.51), channel_id=1, source_target_pairs={{0,12},{4,8},{8,4},{12,0},{1,13},{5,9},{9,5},{13,1},{2,14},{6,10},... | collective-permute-start | bytes 688136 | tf_op jit(solution)/shard_map/ppermute | solution.py:30
  43.1 0.0 collective-permute-done.8.refs_1_
  43.1 0.0 collective-permute-start.6
  43.1 0.0 collective-permute-done.10.refs_5_
  43.1 1.9 %collective-permute-start.7 = (bf16[7,2,2,32,128]{4,3,2,1,0:T(8,128)(2,1)}, bf16[7,2,2,32,128]{4,3,2,1,0:T(8,128)(2,1)S(1)}, u32[]{:S(2)}, u32[]{:S(2)}) collective-permute-start(bf16[7,2,2,32,128]{4,3,2,1,0:T(8,128)(2,1)} %get-tuple-element.53), channel_id=1, source_target_pairs={{0,4},{4,0},{8,12},{12,8},{1,5},{5,1},{9,13},{13,9},{2,6},{6,2},{1... | collective-permute-start | bytes 688136 | tf_op jit(solution)/shard_map/ppermute | solution.py:30
  45.1 0.0 copy-start.1
  45.1 0.0 collective-permute-done.11.refs_7_
  45.1 0.0 collective-permute-done.9.refs_3_
  45.1 0.0 copy-done
  45.1 5.8 %beam_first.1 = (f32[512,256]{1,0:T(8,128)S(1)}, bf16[512,128]{1,0:T(8,128)(2,1)S(1)}) custom-call(bf16[9,2,2,32,128]{4,3,2,1,0:T(8,128)(2,1)S(1)} %copy-done, bf16[9,2,2,32,128]{4,3,2,1,0:T(8,128)(2,1)} %collective-permute-done.8.refs_1_, bf16[9,2,2,32,128]{4,3,2,1,0:T(8,128)(2,1)} %collective-permute-done.refs_2_, ...), custom_call_target="tpu_custom_call" | custom-call | flops 1024 | bytes 1024 | tf_op jit(solution)/shard_map/beam_first/pallas_call | solution.py:254
  50.9 0.1 collective-permute-start.12
  51.0 0.0 copy-done.1
  51.0 0.1 collective-permute-start.4
  51.1 0.1 collective-permute-done.5.refs_2_
  51.2 11.5 %collective-permute-done.6.refs_4_ = bf16[7,2,2,32,128]{4,3,2,1,0:T(8,128)(2,1)S(1)} collective-permute-done((bf16[7,2,2,32,128]{4,3,2,1,0:T(8,128)(2,1)}, bf16[7,2,2,32,128]{4,3,2,1,0:T(8,128)(2,1)S(1)}, u32[]{:S(2)}, u32[]{:S(2)}) %collective-permute-start.6) | collective-permute-done | bytes 229408 | tf_op jit(solution)/shard_map/ppermute | solution.py:30
  62.7 0.0 collective-permute-done.7.refs_6_
  62.7 0.0 collective-permute-done.12.refs_9_
  62.7 0.0 collective-permute-start.13
  62.7 0.5 collective-permute-start.14
  63.2 0.1 collective-permute-start.15
  63.3 0.0 collective-permute-done.4.refs_1_
  63.3 0.9 %collective-permute-done.13.refs_3_ = bf16[7,2,2,32,128]{4,3,2,1,0:T(8,128)(2,1)S(1)} collective-permute-done((bf16[7,2,2,32,128]{4,3,2,1,0:T(8,128)(2,1)S(1)}, bf16[7,2,2,32,128]{4,3,2,1,0:T(8,128)(2,1)S(1)}, u32[]{:S(2)}, u32[]{:S(2)}) %collective-permute-start.13) | collective-permute-done | bytes 229408 | tf_op jit(solution)/shard_map/ppermute | solution.py:30
  64.2 0.3 collective-permute-done.14.refs_5_
  64.5 0.3 collective-permute-done.15.refs_7_
  64.9 3.6 %beam_last.1 = bf16[8,128,128]{2,1,0:T(8,128)(2,1)S(1)} custom-call(bf16[7,2,2,32,128]{4,3,2,1,0:T(8,128)(2,1)S(1)} %copy-done.1, bf16[7,2,2,32,128]{4,3,2,1,0:T(8,128)(2,1)S(1)} %collective-permute-done.4.refs_1_, bf16[7,2,2,32,128]{4,3,2,1,0:T(8,128)(2,1)S(1)} %collective-permute-done.5.refs_2_, ...), custom_call_target="tpu_custom_call" | custom-call | flops 1024 | bytes 1024 | tf_op jit(solution)/shard_map/beam_last/pallas_call | solution.py:254
  68.5 12.0 %all_to_all.5 = bf16[8,128,128]{2,1,0:T(8,128)(2,1)S(1)} all-to-all(bf16[8,128,128]{2,1,0:T(8,128)(2,1)S(1)} %beam_last.1), channel_id=1, replica_groups=mesh['groups'=2,'chan'=4,'tm'=2,'beam'=2] {'chan','tm'}, dimensions={0} | all-to-all | bytes 524288 | tf_op jit(solution)/shard_map/all_to_all | solution.py:405
  80.5 0.6 broadcast_multiply_fusion
  (11 shorter events, 0.2 us)
Async XLA Ops:
  0.0 15.8 %copy-start.4 = (s32[512]{0:T(512)S(1)}, s32[512]{0:T(512)}, u32[]{:S(2)}) copy-start(s32[512]{0:T(512)} %param.9) | copy-start | bytes 6148
  0.0 16.5 %copy-start.2 = (bf16[256,2,1024]{2,1,0:T(2,128)(2,1)S(1)}, bf16[256,2,1024]{2,1,0:T(2,128)(2,1)}, u32[]{:S(2)}) copy-start(bf16[256,2,1024]{2,1,0:T(2,128)(2,1)} %param.8) | copy-start | bytes 3145732
  5.5 24.8 %collective-permute-start.3 = (bf16[64,7168]{1,0:T(8,128)(2,1)}, bf16[64,7168]{1,0:T(8,128)(2,1)}, u32[]{:S(2)}, u32[]{:S(2)}) collective-permute-start(bf16[64,7168]{1,0:T(8,128)(2,1)} %get-tuple-element.40), channel_id=1, source_target_pairs={{0,2},{1,3},{4,6},{5,7},{8,10},{9,11},{12,14},{13,15},{16,18},{17,... | collective-permute-start | bytes 2752520 | tf_op jit(solution)/shard_map/ppermute | solution.py:39
  11.4 23.8 %collective-permute-start = (bf16[9,2,2,32,128]{4,3,2,1,0:T(8,128)(2,1)}, bf16[9,2,2,32,128]{4,3,2,1,0:T(8,128)(2,1)}, u32[]{:S(2)}, u32[]{:S(2)}) collective-permute-start(bf16[9,2,2,32,128]{4,3,2,1,0:T(8,128)(2,1)} %get-tuple-element.37), channel_id=1, source_target_pairs={{0,12},{4,8},{8,4},{12,0},{1,13},{5,9},{9,5},{13,1},{2,14},{6,10},... | collective-permute-start | bytes 884744 | tf_op jit(solution)/shard_map/ppermute | solution.py:30
  15.0 25.2 %collective-permute-start.1 = (bf16[9,2,2,32,128]{4,3,2,1,0:T(8,128)(2,1)}, bf16[9,2,2,32,128]{4,3,2,1,0:T(8,128)(2,1)}, u32[]{:S(2)}, u32[]{:S(2)}) collective-permute-start(bf16[9,2,2,32,128]{4,3,2,1,0:T(8,128)(2,1)} %get-tuple-element.38), channel_id=1, source_target_pairs={{0,8},{4,12},{8,0},{12,4},{1,9},{5,13},{9,1},{13,5},{2,10},{6,14},... | collective-permute-start | bytes 884744 | tf_op jit(solution)/shard_map/ppermute | solution.py:30
  15.0 25.2 %collective-permute-start.2 = (bf16[9,2,2,32,128]{4,3,2,1,0:T(8,128)(2,1)}, bf16[9,2,2,32,128]{4,3,2,1,0:T(8,128)(2,1)}, u32[]{:S(2)}, u32[]{:S(2)}) collective-permute-start(bf16[9,2,2,32,128]{4,3,2,1,0:T(8,128)(2,1)} %get-tuple-element.39), channel_id=1, source_target_pairs={{0,4},{4,0},{8,12},{12,8},{1,5},{5,1},{9,13},{13,9},{2,6},{6,2},{1... | collective-permute-start | bytes 884744 | tf_op jit(solution)/shard_map/ppermute | solution.py:30
  15.8 27.4 %collective-permute-start.8 = (bf16[9,2,2,32,128]{4,3,2,1,0:T(8,128)(2,1)}, bf16[9,2,2,32,128]{4,3,2,1,0:T(8,128)(2,1)}, u32[]{:S(2)}, u32[]{:S(2)}) collective-permute-start(bf16[9,2,2,32,128]{4,3,2,1,0:T(8,128)(2,1)} %get-tuple-element.54.refs_0_), channel_id=1, source_target_pairs={{0,1},{1,0},{2,3},{3,2},{4,5},{5,4},{6,7},{7,6},{8,9},{9,8},{10,11... | collective-permute-start | bytes 884744 | tf_op jit(solution)/shard_map/ppermute | solution.py:30
  17.2 3.6 %copy-start.3 = (s32[128,8]{0,1:T(8,128)S(1)}, s32[128,8]{0,1:T(8,128)}, u32[]{:S(2)}) copy-start(s32[128,8]{0,1:T(8,128)} %param.10) | copy-start | bytes 12292
  30.3 14.8 %copy-start = (bf16[9,2,2,32,128]{4,3,2,1,0:T(8,128)(2,1)S(1)}, bf16[9,2,2,32,128]{4,3,2,1,0:T(8,128)(2,1)}, u32[]{:S(2)}) copy-start(bf16[9,2,2,32,128]{4,3,2,1,0:T(8,128)(2,1)} %get-tuple-element.54.refs_0_) | copy-start | bytes 884740
  40.1 3.0 %collective-permute-start.10 = (bf16[9,2,2,32,128]{4,3,2,1,0:T(8,128)(2,1)}, bf16[9,2,2,32,128]{4,3,2,1,0:T(8,128)(2,1)S(1)}, u32[]{:S(2)}, u32[]{:S(2)}) collective-permute-start(bf16[9,2,2,32,128]{4,3,2,1,0:T(8,128)(2,1)} %collective-permute-done.1.refs_4_), channel_id=1, source_target_pairs={{0,1},{1,0},{2,3},{3,2},{4,5},{5,4},{6,7},{7,6},{8,9},{9,8},{10,11... | collective-permute-start | bytes 884744 | tf_op jit(solution)/shard_map/ppermute | solution.py:30
  40.1 5.0 %collective-permute-start.11 = (bf16[9,2,2,32,128]{4,3,2,1,0:T(8,128)(2,1)}, bf16[9,2,2,32,128]{4,3,2,1,0:T(8,128)(2,1)S(1)}, u32[]{:S(2)}, u32[]{:S(2)}) collective-permute-start(bf16[9,2,2,32,128]{4,3,2,1,0:T(8,128)(2,1)} %collective-permute-done.2.refs_6_), channel_id=1, source_target_pairs={{0,1},{1,0},{2,3},{3,2},{4,5},{5,4},{6,7},{7,6},{8,9},{9,8},{10,11... | collective-permute-start | bytes 884744 | tf_op jit(solution)/shard_map/ppermute | solution.py:30
  40.6 4.5 %collective-permute-start.9 = (bf16[9,2,2,32,128]{4,3,2,1,0:T(8,128)(2,1)}, bf16[9,2,2,32,128]{4,3,2,1,0:T(8,128)(2,1)S(1)}, u32[]{:S(2)}, u32[]{:S(2)}) collective-permute-start(bf16[9,2,2,32,128]{4,3,2,1,0:T(8,128)(2,1)} %collective-permute-done.refs_2_), channel_id=1, source_target_pairs={{0,1},{1,0},{2,3},{3,2},{4,5},{5,4},{6,7},{7,6},{8,9},{9,8},{10,11... | collective-permute-start | bytes 884744 | tf_op jit(solution)/shard_map/ppermute | solution.py:30
  40.6 10.6 %collective-permute-start.5 = (bf16[7,2,2,32,128]{4,3,2,1,0:T(8,128)(2,1)}, bf16[7,2,2,32,128]{4,3,2,1,0:T(8,128)(2,1)S(1)}, u32[]{:S(2)}, u32[]{:S(2)}) collective-permute-start(bf16[7,2,2,32,128]{4,3,2,1,0:T(8,128)(2,1)} %get-tuple-element.51), channel_id=1, source_target_pairs={{0,12},{4,8},{8,4},{12,0},{1,13},{5,9},{9,5},{13,1},{2,14},{6,10},... | collective-permute-start | bytes 688136 | tf_op jit(solution)/shard_map/ppermute | solution.py:30
  43.1 19.6 %collective-permute-start.6 = (bf16[7,2,2,32,128]{4,3,2,1,0:T(8,128)(2,1)}, bf16[7,2,2,32,128]{4,3,2,1,0:T(8,128)(2,1)S(1)}, u32[]{:S(2)}, u32[]{:S(2)}) collective-permute-start(bf16[7,2,2,32,128]{4,3,2,1,0:T(8,128)(2,1)} %get-tuple-element.52), channel_id=1, source_target_pairs={{0,8},{4,12},{8,0},{12,4},{1,9},{5,13},{9,1},{13,5},{2,10},{6,14},... | collective-permute-start | bytes 688136 | tf_op jit(solution)/shard_map/ppermute | solution.py:30
  43.1 19.6 %collective-permute-start.7 = (bf16[7,2,2,32,128]{4,3,2,1,0:T(8,128)(2,1)}, bf16[7,2,2,32,128]{4,3,2,1,0:T(8,128)(2,1)S(1)}, u32[]{:S(2)}, u32[]{:S(2)}) collective-permute-start(bf16[7,2,2,32,128]{4,3,2,1,0:T(8,128)(2,1)} %get-tuple-element.53), channel_id=1, source_target_pairs={{0,4},{4,0},{8,12},{12,8},{1,5},{5,1},{9,13},{13,9},{2,6},{6,2},{1... | collective-permute-start | bytes 688136 | tf_op jit(solution)/shard_map/ppermute | solution.py:30
  45.1 5.9 %copy-start.1 = (bf16[7,2,2,32,128]{4,3,2,1,0:T(8,128)(2,1)S(1)}, bf16[7,2,2,32,128]{4,3,2,1,0:T(8,128)(2,1)}, u32[]{:S(2)}) copy-start(bf16[7,2,2,32,128]{4,3,2,1,0:T(8,128)(2,1)} %get-tuple-element.50.refs_0_) | copy-start | bytes 688132
  50.9 11.8 %collective-permute-start.12 = (bf16[512,128]{1,0:T(8,128)(2,1)S(1)}, bf16[512,128]{1,0:T(8,128)(2,1)S(1)}, u32[]{:S(2)}, u32[]{:S(2)}) collective-permute-start(bf16[512,128]{1,0:T(8,128)(2,1)S(1)} %get-tuple-element.65.refs_8_), channel_id=1, source_target_pairs={{0,2},{2,0},{1,3},{3,1},{4,6},{6,4},{5,7},{7,5},{8,10},{10,8},{9,1... | collective-permute-start | bytes 393224 | tf_op jit(solution)/shard_map/ppermute | solution.py:30
  51.0 12.4 %collective-permute-start.4 = (bf16[7,2,2,32,128]{4,3,2,1,0:T(8,128)(2,1)S(1)}, bf16[7,2,2,32,128]{4,3,2,1,0:T(8,128)(2,1)S(1)}, u32[]{:S(2)}, u32[]{:S(2)}) collective-permute-start(bf16[7,2,2,32,128]{4,3,2,1,0:T(8,128)(2,1)S(1)} %copy-done.1), channel_id=1, source_target_pairs={{0,1},{1,0},{2,3},{3,2},{4,5},{5,4},{6,7},{7,6},{8,9},{9,8},{10,11... | collective-permute-start | bytes 688136 | tf_op jit(solution)/shard_map/ppermute | solution.py:30
  62.7 1.5 %collective-permute-start.13 = (bf16[7,2,2,32,128]{4,3,2,1,0:T(8,128)(2,1)S(1)}, bf16[7,2,2,32,128]{4,3,2,1,0:T(8,128)(2,1)S(1)}, u32[]{:S(2)}, u32[]{:S(2)}) collective-permute-start(bf16[7,2,2,32,128]{4,3,2,1,0:T(8,128)(2,1)S(1)} %collective-permute-done.5.refs_2_), channel_id=1, source_target_pairs={{0,1},{1,0},{2,3},{3,2},{4,5},{5,4},{6,7},{7,6},{8,9},{9,8},{10,11... | collective-permute-start | bytes 688136 | tf_op jit(solution)/shard_map/ppermute | solution.py:30
  62.7 1.8 %collective-permute-start.14 = (bf16[7,2,2,32,128]{4,3,2,1,0:T(8,128)(2,1)S(1)}, bf16[7,2,2,32,128]{4,3,2,1,0:T(8,128)(2,1)S(1)}, u32[]{:S(2)}, u32[]{:S(2)}) collective-permute-start(bf16[7,2,2,32,128]{4,3,2,1,0:T(8,128)(2,1)S(1)} %collective-permute-done.6.refs_4_), channel_id=1, source_target_pairs={{0,1},{1,0},{2,3},{3,2},{4,5},{5,4},{6,7},{7,6},{8,9},{9,8},{10,11... | collective-permute-start | bytes 688136 | tf_op jit(solution)/shard_map/ppermute | solution.py:30
  63.2 1.6 %collective-permute-start.15 = (bf16[7,2,2,32,128]{4,3,2,1,0:T(8,128)(2,1)S(1)}, bf16[7,2,2,32,128]{4,3,2,1,0:T(8,128)(2,1)S(1)}, u32[]{:S(2)}, u32[]{:S(2)}) collective-permute-start(bf16[7,2,2,32,128]{4,3,2,1,0:T(8,128)(2,1)S(1)} %collective-permute-done.7.refs_6_), channel_id=1, source_target_pairs={{0,1},{1,0},{2,3},{3,2},{4,5},{5,4},{6,7},{7,6},{8,9},{9,8},{10,11... | collective-permute-start | bytes 688136 | tf_op jit(solution)/shard_map/ppermute | solution.py:30
